TPU v7x, 32 devices: a whole 2x2x4 slice. The times are simulated.
32 devices in a mesh: dp: 4 (over y, core), fsdp: 8 (over z, x).
Axes of the slice: x: 2, y: 2, z: 4, core: 2. Of those that a mesh axis runs over, the one named last changes fastest.
Arguments:
- tokens: bfloat16 [2, 32, 1024, 768], P(None, ('dp', 'fsdp')), may hold values from -6 to 6
- task_ids: int32 [2, 32, 4], P(None, ('dp', 'fsdp')), may hold values from 0 to 7
- logit_grads: bfloat16 [2, 32, 4, 100], P(None, ('dp', 'fsdp')), may hold values from -6 to 6
- prompts: bfloat16 [8, 50, 768], replicated, may hold values from -6 to 6
- head_weights: bfloat16 [8, 768, 100], replicated, may hold values from -0.21875 to 0.21875
- qkv_weight: bfloat16 [768, 2304], P('fsdp'), may hold values from -0.3125 to 0.3125
- out_weight: bfloat16 [768, 768], P('fsdp'), may hold values from -0.875 to 0.875
- up_weight: bfloat16 [768, 3072], P('fsdp'), may hold values from -0.21875 to 0.21875
- down_weight: bfloat16 [3072, 768], P('fsdp'), may hold values from -0.109375 to 0.109375
- attn_gain: float32 [768], replicated, may hold values from 0.5 to 1.5
- mlp_gain: float32 [768], replicated, may hold values from 0.5 to 1.5
- final_gain: float32 [768], replicated, may hold values from 0.5 to 1.5
Outputs:
- activations: bfloat16 [2, 32, 1024, 768], P(None, ('dp', 'fsdp'))
- input_grads: float32 [2, 32, 1024, 768], P(None, ('dp', 'fsdp'))
- prompt_grads: float32 [8, 50, 768], replicated
- head_grads: float32 [8, 768, 100], replicated
All inputs are finite; a program needn't handle non-finite values.
Results may differ from a plain program's by a relative error of at most 0.011.
The roundings to bfloat16 on the way count: a program that leaves them out, or rounds other values in their place, can miss the bound.
Values may be sent and summed in bfloat16 or wider, within the bound.
No kernel may reach another device: no remote copies, remote signals or barrier semaphores. Data moves between devices by JAX's collectives and lax.ppermute only.
A program may use at most 192 MiB of HBM per device.

v0:
```python
import jax
import jax.numpy as jnp
from jax import lax
from jax.sharding import PartitionSpec as P

D = 768
HEADS = 12
HDIM = 64
FF = 3072
CLASSES = 100
TASKS = 8
PROMPTS = 50
IMG = 247
IMGS_ROW = 4
ROW = 1024
MB = 2


EPSILON = 1e-06
PRECISE = lax.Precision.HIGHEST
MASKED_SCORE = -1e30


def layer_norm(rows, gain):
    row_mean = jnp.mean(rows, axis=-1, keepdims=True)
    centred = rows - row_mean
    inv_std = lax.rsqrt(jnp.mean(centred * centred, axis=-1, keepdims=True) + EPSILON)
    unit_rows = centred * inv_std
    return (unit_rows * gain, unit_rows, inv_std)


def norm_back(grad_out, unit_rows, inv_std, gain):
    scaled = grad_out * gain
    inner_mean = jnp.mean(scaled * unit_rows, axis=-1, keepdims=True)
    return inv_std * (scaled - jnp.mean(scaled, axis=-1, keepdims=True) - unit_rows * inner_mean)


def gelu_exact(inputs):
    return jax.nn.gelu(inputs, approximate=False)


def segments():
    places = jnp.arange(ROW, dtype=jnp.int32)
    return jnp.minimum(places // IMG, IMGS_ROW)


def class_rows(rows_val):
    rows_n = rows_val.shape[0]
    return rows_val[:, : IMGS_ROW * IMG].reshape(rows_n, IMGS_ROW, IMG, rows_val.shape[-1])[:, :, 0]


def at_class(rows_val, class_val):
    rows_n = rows_val.shape[0]
    images = rows_val[:, : IMGS_ROW * IMG].reshape(rows_n, IMGS_ROW, IMG, D)
    images = jnp.concatenate([images[:, :, :1] + class_val[:, :, None], images[:, :, 1:]], axis=2)
    return jnp.concatenate(
        [images.reshape(rows_n, IMGS_ROW * IMG, D), rows_val[:, IMGS_ROW * IMG :]], axis=1
    )


def assemble(tok_rows, one_hot, prompts):
    rows_n = tok_rows.shape[0]
    chosen = jnp.dot(
        one_hot.reshape(rows_n * IMGS_ROW, TASKS).astype(jnp.bfloat16),
        prompts.reshape(TASKS, PROMPTS * D),
        preferred_element_type=jnp.float32,
    ).reshape(rows_n, IMGS_ROW, PROMPTS, D)
    as_float = tok_rows.astype(jnp.float32)
    images = as_float[:, : IMGS_ROW * IMG].reshape(rows_n, IMGS_ROW, IMG, D)
    images = jnp.concatenate([images[:, :, :1], chosen, images[:, :, 1 + PROMPTS :]], axis=2)
    return jnp.concatenate(
        [images.reshape(rows_n, IMGS_ROW * IMG, D), as_float[:, IMGS_ROW * IMG :]], axis=1
    )


def attend_group(group_vals):
    scale = HDIM ** (-0.5)
    groups_n = group_vals.shape[0]
    span = group_vals.shape[1]
    split = group_vals.reshape(groups_n, span, 3, HEADS, HDIM)
    queries = split[:, :, 0]
    key_vecs = split[:, :, 1]
    value_vecs = split[:, :, 2]
    scores = (
        jnp.einsum("iqhd,ikhd->ihqk", queries, key_vecs, preferred_element_type=jnp.float32) * scale
    )
    attn_probs = jax.nn.softmax(scores, axis=-1).astype(jnp.bfloat16)
    context = jnp.einsum(
        "ihqk,ikhd->iqhd", attn_probs, value_vecs, preferred_element_type=jnp.float32
    )
    return context.astype(jnp.bfloat16).reshape(groups_n * span, D)


def attend_row(packed_row):
    image_span = IMGS_ROW * IMG
    pieces = [attend_group(packed_row[:image_span].reshape(IMGS_ROW, IMG, 3 * D))]
    pieces.append(attend_group(packed_row[image_span:].reshape(1, ROW - image_span, 3 * D)))
    return jnp.concatenate(pieces, axis=0)


def attend_back(packed_item):
    packed_row, d_context = packed_item
    segment_of = segments()
    scale = HDIM ** (-0.5)
    queries = packed_row[:, :D].reshape(ROW, HEADS, HDIM)
    key_vecs = packed_row[:, D : 2 * D].reshape(ROW, HEADS, HDIM)
    value_vecs = packed_row[:, 2 * D :].reshape(ROW, HEADS, HDIM)
    class_query = queries[: IMGS_ROW * IMG].reshape(IMGS_ROW, IMG, HEADS, HDIM)[:, 0]
    scores = (
        jnp.einsum("ihd,khd->ihk", class_query, key_vecs, preferred_element_type=jnp.float32)
        * scale
    )
    same_image = jnp.arange(IMGS_ROW, dtype=jnp.int32)[:, None] == segment_of[None, :]
    attn_probs = jax.nn.softmax(jnp.where(same_image[:, None, :], scores, MASKED_SCORE), axis=-1)
    probs_low = attn_probs.astype(jnp.bfloat16)
    d_probs = jnp.einsum("ihd,khd->ihk", d_context, value_vecs, preferred_element_type=jnp.float32)
    d_scores = (
        attn_probs * (d_probs - jnp.sum(attn_probs * d_probs, axis=-1, keepdims=True))
    ).astype(jnp.bfloat16)
    d_query = (
        jnp.einsum("ihk,khd->ihd", d_scores, key_vecs, preferred_element_type=jnp.float32) * scale
    )
    d_key = (
        jnp.einsum("ihk,ihd->khd", d_scores, class_query, preferred_element_type=jnp.float32)
        * scale
    )
    d_value = jnp.einsum("ihk,ihd->khd", probs_low, d_context, preferred_element_type=jnp.float32)
    d_keyval = jnp.concatenate([d_key.reshape(ROW, D), d_value.reshape(ROW, D)], axis=1).astype(
        jnp.bfloat16
    )
    return (d_query.astype(jnp.bfloat16).reshape(IMGS_ROW, D), d_keyval)


def forward(tok_rows, one_hot, prompts, forward_set, attn_gain, mlp_gain):
    qkv_all, out_all, up_all, down_all = forward_set
    resid = assemble(tok_rows, one_hot, prompts)
    normed_one, unit_one, inv_one = layer_norm(resid, attn_gain)
    packed = jnp.einsum(
        "rpd,de->rpe", normed_one.astype(jnp.bfloat16), qkv_all, preferred_element_type=jnp.float32
    ).astype(jnp.bfloat16)
    context = lax.map(attend_row, packed)
    middle = resid + jnp.einsum("rpd,de->rpe", context, out_all, preferred_element_type=jnp.float32)
    normed_two, unit_two, inv_two = layer_norm(middle, mlp_gain)
    pre_act = jnp.einsum(
        "rpd,df->rpf", normed_two.astype(jnp.bfloat16), up_all, preferred_element_type=jnp.float32
    )
    activated = gelu_exact(pre_act).astype(jnp.bfloat16)
    output = middle + jnp.einsum(
        "rpf,fd->rpd", activated, down_all, preferred_element_type=jnp.float32
    )
    saved = (
        unit_one,
        inv_one,
        packed,
        class_rows(unit_two),
        class_rows(inv_two),
        class_rows(pre_act),
        class_rows(output),
    )
    return (output, saved)


def backward(saved, one_hot, grads_in, head_weights, backward_set, attn_gain, mlp_gain, final_gain):
    unit_one, inv_one, packed, unit_cls, inv_cls, pre_cls, output_cls = saved
    qkv_all, out_all, up_all, down_all = backward_set
    rows_n = packed.shape[0]
    final_rows, unit_fin, inv_fin = layer_norm(output_cls, final_gain)
    final_low = final_rows.astype(jnp.bfloat16).reshape(rows_n * IMGS_ROW, D)
    selected = (one_hot.astype(jnp.bfloat16)[..., None] * grads_in[..., None, :]).reshape(
        rows_n * IMGS_ROW, TASKS, CLASSES
    )
    head_part = jnp.einsum("nd,ntc->tdc", final_low, selected, preferred_element_type=jnp.float32)
    d_final = jnp.einsum("ntc,tdc->nd", selected, head_weights, preferred_element_type=jnp.float32)
    d_output = norm_back(d_final.reshape(rows_n, IMGS_ROW, D), unit_fin, inv_fin, final_gain)
    d_act = jnp.einsum(
        "nd,fd->nf",
        d_output.astype(jnp.bfloat16).reshape(-1, D),
        down_all,
        preferred_element_type=jnp.float32,
    )
    unused_value, gelu_pull = jax.vjp(gelu_exact, pre_cls.reshape(-1, FF))
    d_pre = gelu_pull(d_act)[0].astype(jnp.bfloat16)
    d_norm_two = jnp.einsum("nf,df->nd", d_pre, up_all, preferred_element_type=jnp.float32).reshape(
        rows_n, IMGS_ROW, D
    )
    d_middle = d_output + norm_back(d_norm_two, unit_cls, inv_cls, mlp_gain)
    d_context = jnp.einsum(
        "nd,ed->ne",
        d_middle.astype(jnp.bfloat16).reshape(-1, D),
        out_all,
        preferred_element_type=jnp.float32,
    ).astype(jnp.bfloat16)
    d_context = d_context.reshape(rows_n, IMGS_ROW, HEADS, HDIM)
    d_query, d_keyval = lax.map(attend_back, (packed, d_context))
    d_norm_one = jnp.einsum(
        "rpc,dc->rpd", d_keyval, qkv_all[:, D:], preferred_element_type=jnp.float32
    )
    d_class_norm = jnp.einsum(
        "ric,dc->rid", d_query, qkv_all[:, :D], preferred_element_type=jnp.float32
    )
    d_norm_one = at_class(d_norm_one, d_class_norm)
    d_resid = at_class(norm_back(d_norm_one, unit_one, inv_one, attn_gain), d_middle)
    images = d_resid[:, : IMGS_ROW * IMG].reshape(rows_n, IMGS_ROW, IMG, D)
    prompt_part = jnp.dot(
        one_hot.reshape(-1, TASKS).T,
        images[:, :, 1 : 1 + PROMPTS].reshape(-1, PROMPTS * D),
        precision=PRECISE,
        preferred_element_type=jnp.float32,
    ).reshape(TASKS, PROMPTS, D)
    images = jnp.concatenate(
        [
            images[:, :, :1],
            jnp.zeros_like(images[:, :, 1 : 1 + PROMPTS]),
            images[:, :, 1 + PROMPTS :],
        ],
        axis=2,
    )
    input_part = jnp.concatenate(
        [images.reshape(rows_n, IMGS_ROW * IMG, D), d_resid[:, IMGS_ROW * IMG :]], axis=1
    )
    return (input_part, prompt_part, head_part)


def body(
    tokens,
    task_ids,
    logit_grads,
    prompts,
    head_weights,
    qkv_weight,
    out_weight,
    up_weight,
    down_weight,
    attn_gain,
    mlp_gain,
    final_gain,
):
    hot_all = (task_ids[..., None] == jnp.arange(TASKS, dtype=jnp.int32)).astype(jnp.float32)
    shares = None
    results = []
    input_list = []
    for micro_step in range(MB):
        forward_set = (
            lax.all_gather(qkv_weight, "fsdp", axis=0, tiled=True),
            lax.all_gather(out_weight, "fsdp", axis=0, tiled=True),
            lax.all_gather(up_weight, "fsdp", axis=0, tiled=True),
            lax.all_gather(down_weight, "fsdp", axis=0, tiled=True),
        )
        output, saved = forward(
            tokens[micro_step], hot_all[micro_step], prompts, forward_set, attn_gain, mlp_gain
        )
        results.append(output.astype(jnp.bfloat16))
        backward_set = (
            lax.all_gather(qkv_weight, "fsdp", axis=0, tiled=True),
            lax.all_gather(out_weight, "fsdp", axis=0, tiled=True),
            lax.all_gather(up_weight, "fsdp", axis=0, tiled=True),
            lax.all_gather(down_weight, "fsdp", axis=0, tiled=True),
        )
        input_part, prompt_part, head_part = backward(
            saved,
            hot_all[micro_step],
            logit_grads[micro_step],
            head_weights,
            backward_set,
            attn_gain,
            mlp_gain,
            final_gain,
        )
        input_list.append(input_part)
        reduced = (
            lax.psum_scatter(
                prompt_part.reshape(-1), ("dp", "fsdp"), scatter_dimension=0, tiled=True
            ),
            lax.psum_scatter(
                head_part.reshape(-1), ("dp", "fsdp"), scatter_dimension=0, tiled=True
            ),
        )
        shares = reduced if shares is None else (shares[0] + reduced[0], shares[1] + reduced[1])
    gathered = (
        lax.all_gather(shares[0], ("dp", "fsdp"), axis=0, tiled=True),
        lax.all_gather(shares[1], ("dp", "fsdp"), axis=0, tiled=True),
    )
    return (
        jnp.stack(results),
        jnp.stack(input_list),
        gathered[0].reshape(prompts.shape),
        gathered[1].reshape(head_weights.shape),
    )


def solution(mesh):
    in_specs = (
        P(None, ("dp", "fsdp"), None, None),
        P(None, ("dp", "fsdp"), None),
        P(None, ("dp", "fsdp"), None, None),
        P(),
        P(),
        P("fsdp", None),
        P("fsdp", None),
        P("fsdp", None),
        P("fsdp", None),
        P(),
        P(),
        P(),
    )
    out_specs = (P(None, ("dp", "fsdp"), None, None), P(None, ("dp", "fsdp"), None, None), P(), P())
    return jax.shard_map(body, mesh=mesh, in_specs=in_specs, out_specs=out_specs, check_vma=False)
```

profile of v0, /device:TPU:0, one launch (start us, length us, event | category | flops | bytes accessed | tf_op | source)
XLA Modules:
  0.0 830.4 jit_solution(17857909599731042366)
XLA Ops:
  13.1 4.0 bitcast_convert_fusion.1
  19.0 4.0 reshape.1853
  29.3 3.8 reshape.1864
  37.9 3.8 reshape.1866
  41.7 3.9 concatenate.149
  49.4 3.9 reshape.1856
  53.3 3.9 concatenate.143
  63.6 14.5 %all-gather.9.cloned.1.call-done = bf16[768,2304]{1,0:T(8,128)(2,1)} async-done(((bf16[96,2304]{1,0:T(8,128)(2,1)}), bf16[768,2304]{1,0:T(8,128)(2,1)}) %all-gather.9.cloned.1.call-update) | async-done | bytes 3538960 | tf_op jit(solution)/shard_map/all_gather | solution.py:244
  78.2 6.9 convolution_convert_fusion.1
  92.8 5.3 convolution_convert_fusion
  116.7 7.2 copy.183
  123.8 9.4 %reshape.1857 = bf16[4,247,3,12,64]{1,0,4,3,2:T(4,128)(2,1)} reshape(bf16[1,988,2304]{1,2,0:T(8,128)(2,1)} %copy.183) | data formatting | bytes 9105408 | tf_op jit(solution)/shard_map/while/body/eval_jaxpr/reshape;while/body/eval_jaxpr/reshape | solution.py:80
  138.5 4.1 reshape.1887
  146.6 6.6 copy.196
  153.2 9.4 %reshape.1867 = bf16[4,247,3,12,64]{1,0,4,3,2:T(4,128)(2,1)} reshape(bf16[1,988,2304]{1,2,0:T(8,128)(2,1)} %copy.196) | data formatting | bytes 9105408 | tf_op jit(solution)/shard_map/while/body/eval_jaxpr/reshape;while/body/eval_jaxpr/reshape | solution.py:80
  162.6 5.0 fusion.458
  167.6 11.7 %fusion.464 = (f32[4,12,247]{2,1,0:T(8,128)}, f32[4,12,247,247]{2,3,1,0:T(8,128)}) fusion(bf16[4,247,1,12,64]{1,0,4,3,2:T(4,128)(2,1)} %get-tuple-element.88, bf16[4,247,1,12,64]{1,0,4,3,2:T(4,128)(2,1)} %get-tuple-element.89), kind=kOutput, calls=%fused_computation.602 | convolution fusion | flops 383624864 | bytes 14796288 | tf_op jit(solution)/shard_map/while/body/eval_jaxpr/sub | solution.py:87
  179.3 7.3 fusion.97
  193.7 3.8 copy.201
  197.5 4.0 reshape.1868
  201.5 4.3 fusion.465
  209.3 4.0 reshape.1893
  214.8 4.8 fusion.457
  219.6 11.0 %fusion.467 = (f32[4,12,247]{2,1,0:T(8,128)S(1)}, f32[4,12,247,247]{2,3,1,0:T(8,128)}) fusion(bf16[4,247,1,12,64]{1,0,4,3,2:T(4,128)(2,1)} %get-tuple-element.85, bf16[4,247,1,12,64]{1,0,4,3,2:T(4,128)(2,1)} %get-tuple-element.86), kind=kOutput, calls=%fused_computation.605 | convolution fusion | flops 383624864 | bytes 14796288 | tf_op jit(solution)/shard_map/while/body/eval_jaxpr/sub | solution.py:87
  230.6 6.1 fusion.96
  239.1 4.0 reshape.1858
  243.1 4.3 fusion.468
  253.9 3.8 reshape.1880
  266.9 11.4 %fusion.76 = f32[1024,3072]{1,0:T(8,128)} fusion(bf16[768,3072]{1,0:T(8,128)(2,1)} %all-gather.13.cloned.1.call-done, f32[1024,768]{1,0:T(8,128)} %copy-done.13, f32[768]{0:T(1024)S(1)} %copy-done.58, f32[1024]{0:T(1024)S(1)} %add_rsqrt_fusion.2, f32[1024]{0:T(1024)S(1)} %broadcast_multiply_fusion.6), kind=kOutput, calls=%fused_computation.118 | convolution fusion | flops 4834983936 | bytes 20458496 | tf_op jit(solution)/shard_map/rpd,df->rpf/dot_general | solution.py:144
  278.3 10.4 %slice.382 = f32[1,988,3072]{2,1,0:T(8,128)} slice(f32[1,1024,3072]{2,1,0:T(8,128)} %bitcast.493), slice={[0:1], [0:988], [0:3072]} | slice | bytes 24281088 | tf_op jit(solution)/shard_map/slice | solution.py:49
  288.8 10.2 %reshape.1879 = f32[1,4,247,3072]{3,2,1,0:T(8,128)} reshape(f32[1,988,3072]{2,1,0:T(8,128)} %slice.382) | data formatting | bytes 24281088 | tf_op jit(solution)/shard_map/reshape | solution.py:49
  300.6 35.0 %fusion.66 = f32[1024,768]{1,0:T(8,128)S(1)} fusion(f32[1024,768]{1,0:T(8,128)} %copy-done.13, bf16[3072,768]{1,0:T(8,128)(2,1)} %all-gather.15.cloned.1.call-done, f32[1024,3072]{1,0:T(8,128)} %fusion.76), kind=kOutput, calls=%fused_computation.110 | convolution fusion | flops 5037096960 | bytes 23592960 | tf_op jit(solution)/shard_map/rpf,fd->rpd/dot_general | solution.py:148
  339.1 3.9 reshape.1877
  343.0 8.5 %fusion.77 = f32[1024,3072]{1,0:T(8,128)S(1)} fusion(bf16[768,3072]{1,0:T(8,128)(2,1)} %all-gather.13.cloned.1.call-done, f32[1024,768]{1,0:T(8,128)} %copy-done.11, f32[1024]{0:T(1024)S(1)} %add_rsqrt_fusion, f32[1024]{0:T(1024)S(1)} %copy-done.53, f32[768]{0:T(1024)S(1)} %copy-done.58), kind=kOutput, calls=%fused_computation.119 | convolution fusion | flops 4834983936 | bytes 20458496 | tf_op jit(solution)/shard_map/rpd,df->rpf/dot_general | solution.py:144
  351.6 31.8 %fusion.69 = f32[1024,768]{1,0:T(8,128)S(1)} fusion(f32[1024,768]{1,0:T(8,128)S(1)} %copy-done.12, bf16[3072,768]{1,0:T(8,128)(2,1)S(1)} %bitcast.483, f32[1024,3072]{1,0:T(8,128)S(1)} %fusion.77), kind=kOutput, calls=%fused_computation.111 | convolution fusion | flops 5037096960 | bytes 23592960 | tf_op jit(solution)/shard_map/rpf,fd->rpd/dot_general | solution.py:148
  386.9 3.9 reshape.1890
  392.7 6.6 fusion.451
  405.7 10.4 %slice.404 = f32[1,988,3072]{2,1,0:T(8,128)} slice(f32[1,1024,3072]{2,1,0:T(8,128)} %bitcast.492), slice={[0:1], [0:988], [0:3072]} | slice | bytes 24281088 | tf_op jit(solution)/shard_map/slice | solution.py:49
  416.0 10.3 %reshape.1892 = f32[1,4,247,3072]{3,2,1,0:T(8,128)} reshape(f32[1,988,3072]{2,1,0:T(8,128)} %slice.404) | data formatting | bytes 24281088 | tf_op jit(solution)/shard_map/reshape | solution.py:49
  428.2 6.6 fusion.453
  441.7 5.0 fusion.56
  448.6 3.9 reshape.1896
  453.4 3.8 slice.410
  459.0 5.1 fusion.61
  466.0 3.9 reshape.1883
  470.7 3.8 slice.390
  478.6 3.8 pad_maximum_fusion.10
  482.4 3.8 concatenate.162
  488.0 3.8 pad_maximum_fusion.8
  491.9 4.0 concatenate.156
  496.0 9.2 %fusion.75 = (f32[1024]{0:T(1024)S(1)}, f32[1024]{0:T(1024)S(1)}, f32[1024]{0:T(1024)S(1)}, f32[1024]{0:T(1024)S(1)}) fusion(f32[1,36,768]{2,1,0:T(8,128)S(1)} %slice.391, f32[1,988,768]{2,1,0:T(8,128)} %concatenate.156, f32[768]{0:T(1024)S(1)} %copy-done.61, f32[1024]{0:T(1024)S(1)} %copy-done.57, f32[1024]{0:T(1024)S(1)} %copy-done.47, ...), kind=kLoop, calls=%fused_computation.117 | loop fusion | flops 12578816 | bytes 12618752 | tf_op jit(solution)/shard_map/reduce_sum | solution.py:35
  505.3 5.6 subtract_multiply_fusion.1
  514.5 3.8 reshape.1885
  522.0 3.8 reshape.1898
  531.5 3.8 add_bitcast_fusion
  538.9 6.3 reshape.1909
  545.3 139.1 %all-reduce.5.cloned.1.call-done = (f32[307200]{0:T(1024)}, f32[614400]{0:T(1024)}) async-done(((f32[307200]{0:T(1024)}, f32[614400]{0:T(1024)}), (f32[307200]{0:T(1024)}, f32[614400]{0:T(1024)})) %all-reduce.5.cloned.1.call-update) | async-done | bytes 3686416
  697.2 3.9 reshape.1886
  701.1 3.9 reshape.1899
  716.4 25.3 %all-gather.17.cloned.1.call-done = f32[32,1,9600]{2,1,0:T(1,128)} async-done(((f32[1,1,9600]{2,1,0:T(1,128)}), f32[32,1,9600]{2,1,0:T(1,128)}) %all-gather.17.cloned.1.call-update) | async-done | bytes 1228816 | tf_op jit(solution)/shard_map/all_gather | solution.py:280
  741.6 5.2 reduce.50
  749.9 52.2 %all-gather.19.cloned.1.call-done = f32[32,1,19200]{2,1,0:T(1,128)} async-done(((f32[1,1,19200]{2,1,0:T(1,128)}), f32[32,1,19200]{2,1,0:T(1,128)}) %all-gather.19.cloned.1.call-update) | async-done | bytes 2457616 | tf_op jit(solution)/shard_map/all_gather | solution.py:281
  802.1 9.3 %reduce.51 = f32[32,19200]{1,0:T(8,128)} reduce(f32[32,1,19200]{2,1,0:T(1,128)} %all-gather.19.cloned.1.call-done, f32[]{:T(128)} %constant.235), dimensions={1}, to_apply=%all-gather.1.reduce_sub_computation | reduce | bytes 4915204 | tf_op jit(solution)/shard_map/all_gather | solution.py:281
  811.3 8.2 reshape.1905
  (340 shorter events, 180.2 us)
Async XLA Ops:
  7.2 384.9 %copy-start = (bf16[8,768,100]{1,0,2:T(8,128)(2,1)S(1)}, bf16[8,768,100]{1,0,2:T(8,128)(2,1)}, u32[]{:S(2)}) copy-start(bf16[8,768,100]{1,0,2:T(8,128)(2,1)} %param.16) | copy-start | bytes 3686404
  7.2 5.6 copy-start.28
  7.2 71.0 %all-gather.9.cloned.1.call-start = ((), (), s32[]{:S(2)}) async-start(), calls=%async_computation | async-start | bytes 3981312 | tf_op jit(solution)/shard_map/all_gather | solution.py:244
  7.9 193.6 %all-gather.11.cloned.1.call-start = ((), (), s32[]{:S(2)}) async-start(), calls=%async_computation.1 | async-start | bytes 1327104 | tf_op jit(solution)/shard_map/all_gather | solution.py:245
  8.7 258.2 %all-gather.13.cloned.1.call-start = ((), (), s32[]{:S(2)}) async-start(), calls=%async_computation.2 | async-start | bytes 5308416 | tf_op jit(solution)/shard_map/all_gather | solution.py:246
  9.4 291.2 %all-gather.15.cloned.1.call-start = ((), (), s32[]{:S(2)}) async-start(), calls=%async_computation.3 | async-start | bytes 5308416 | tf_op jit(solution)/shard_map/all_gather | solution.py:247
  10.0 674.4 %all-reduce.5.cloned.1.call-start = ((), (), s32[]{:S(2)}) async-start(), calls=%async_computation.6 | async-start | bytes 7372800
  17.1 45.9 %copy-start.23 = (f32[1,36,768]{2,1,0:T(8,128)}, f32[1,36,768]{2,1,0:T(8,128)S(1)}, u32[]{:S(2)}) copy-start(f32[1,36,768]{2,1,0:T(8,128)S(1)} %get-tuple-element.90) | copy-start | bytes 331780
  17.2 61.0 %copy-start.38 = (f32[36,768]{1,0:T(8,128)}, f32[36,768]{1,0:T(8,128)S(1)}, u32[]{:S(2)}) copy-start(f32[36,768]{1,0:T(8,128)S(1)} %get-tuple-element.91) | copy-start | bytes 331780
  23.0 4.4 copy-start.8
  27.4 33.9 %copy-start.25 = (f32[1,36,768]{2,1,0:T(8,128)}, f32[1,36,768]{2,1,0:T(8,128)S(1)}, u32[]{:S(2)}) copy-start(f32[1,36,768]{2,1,0:T(8,128)S(1)} %get-tuple-element.94) | copy-start | bytes 331780
  27.4 63.5 %copy-start.40 = (f32[36,768]{1,0:T(8,128)}, f32[36,768]{1,0:T(8,128)S(1)}, u32[]{:S(2)}) copy-start(f32[36,768]{1,0:T(8,128)S(1)} %get-tuple-element.95) | copy-start | bytes 331780
  61.9 29.0 %copy-start.44 = (f32[1024]{0:T(1024)}, f32[1024]{0:T(1024)S(1)}, u32[]{:S(2)}) copy-start(f32[1024]{0:T(1024)S(1)} %broadcast_multiply_fusion.5) | copy-start | bytes 12292
  62.4 28.5 %copy-start.54 = (f32[1024]{0:T(1024)}, f32[1024]{0:T(1024)S(1)}, u32[]{:S(2)}) copy-start(f32[1024]{0:T(1024)S(1)} %add_rsqrt_fusion.1) | copy-start | bytes 12292
  62.8 15.3 %copy-start.60 = (f32[768]{0:T(1024)S(1)}, f32[768]{0:T(1024)}, u32[]{:S(2)}) copy-start(f32[768]{0:T(1024)} %param.21) | copy-start | bytes 9220
  63.1 22.0 %copy-start.46 = (f32[1024]{0:T(1024)}, f32[1024]{0:T(1024)S(1)}, u32[]{:S(2)}) copy-start(f32[1024]{0:T(1024)S(1)} %broadcast_multiply_fusion.7) | copy-start | bytes 12292
  63.6 21.5 %copy-start.56 = (f32[1024]{0:T(1024)}, f32[1024]{0:T(1024)S(1)}, u32[]{:S(2)}) copy-start(f32[1024]{0:T(1024)S(1)} %add_rsqrt_fusion.3) | copy-start | bytes 12292
  88.3 4.6 copy-start.29
  109.2 4.1 copy-start.22
  113.3 147.4 %copy-start.50 = (bf16[4,1,12,64]{3,0,2,1:T(4,128)(2,1)}, bf16[4,1,12,64]{3,0,2,1:T(4,128)(2,1)S(1)}, u32[]{:S(2)}) copy-start(bf16[4,1,12,64]{3,0,2,1:T(4,128)(2,1)S(1)} %copy.263) | copy-start | bytes 18436
  116.7 144.0 %copy-start.19 = (bf16[1024,768]{0,1:T(8,128)(2,1)}, bf16[1024,768]{0,1:T(8,128)(2,1)S(1)}, u32[]{:S(2)}) copy-start(bf16[1024,768]{0,1:T(8,128)(2,1)S(1)} %copy.210) | copy-start | bytes 4718596
  146.6 116.5 %copy-start.48 = (bf16[4,1,12,64]{3,0,2,1:T(4,128)(2,1)}, bf16[4,1,12,64]{3,0,2,1:T(4,128)(2,1)S(1)}, u32[]{:S(2)}) copy-start(bf16[4,1,12,64]{3,0,2,1:T(4,128)(2,1)S(1)} %copy.269) | copy-start | bytes 18436
  167.6 19.0 %slice-start.2 = ((s8[4718592]{0:T(1024)(128)(4,1)}), s8[524288]{0:T(1024)(128)(4,1)S(1)}, s32[]{:S(2)}) async-start(s8[4718592]{0:T(1024)(128)(4,1)} %bitcast.486), calls=%async_computation.9 | async-start | bytes 1048576
  179.3 7.3 slice-start.3
  193.7 7.8 copy-start.41
  236.7 6.4 copy-start.36
  236.7 6.4 copy-start.39
  257.7 9.2 %copy-start.58 = (f32[768]{0:T(1024)S(1)}, f32[768]{0:T(1024)}, u32[]{:S(2)}) copy-start(f32[768]{0:T(1024)} %param.22) | copy-start | bytes 9220
  339.1 3.9 copy-start.53
  339.1 12.4 %slice-start = ((s8[4718592]{0:T(1024)(128)(4,1)}), s8[524288]{0:T(1024)(128)(4,1)S(1)}, s32[]{:S(2)}) async-start(s8[4718592]{0:T(1024)(128)(4,1)} %bitcast.482), calls=%async_computation.7 | async-start | bytes 1048576
  343.0 8.6 %slice-start.1 = ((s8[4718592]{0:T(1024)(128)(4,1)}), s8[4194304]{0:T(1024)(128)(4,1)S(1)}, s32[]{:S(2)}) async-start(s8[4718592]{0:T(1024)(128)(4,1)} %bitcast.482), calls=%async_computation.8 | async-start | bytes 8388608
  343.0 8.6 %copy-start.12 = (f32[1024,768]{1,0:T(8,128)S(1)}, f32[1024,768]{1,0:T(8,128)}, u32[]{:S(2)}) copy-start(f32[1024,768]{1,0:T(8,128)} %copy-done.11) | copy-start | bytes 9437188
  351.6 31.8 %copy-start.18 = (f32[1024,3072]{1,0:T(8,128)}, f32[1024,3072]{1,0:T(8,128)S(1)}, u32[]{:S(2)}) copy-start(f32[1024,3072]{1,0:T(8,128)S(1)} %fusion.77) | copy-start | bytes 37748740
  386.9 5.2 copy-start.59
  386.9 5.2 copy-start.63
  386.9 5.2 copy-start.66
  386.9 5.7 copy-start.34
  386.9 5.7 copy-start.43
  392.7 6.7 copy-start.70
  392.7 8.7 %copy-start.37 = (f32[4,12,1024]{2,0,1:T(4,128)S(1)}, f32[4,12,1024]{2,0,1:T(4,128)}, u32[]{:S(2)}) copy-start(f32[4,12,1024]{2,0,1:T(4,128)} %get-tuple-element.131) | copy-start | bytes 589828
  392.7 8.7 %copy-start.64 = (f32[4,12]{0,1:T(8,128)S(1)}, f32[4,12]{0,1:T(8,128)}, u32[]{:S(2)}) copy-start(f32[4,12]{0,1:T(8,128)} %get-tuple-element.130) | copy-start | bytes 580
  399.3 3.9 copy-start.20
  416.0 11.6 %copy-start.62 = (bf16[4,8]{0,1:T(8,128)(2,1)S(1)}, bf16[4,8]{0,1:T(8,128)(2,1)}, u32[]{:S(2)}) copy-start(bf16[4,8]{0,1:T(8,128)(2,1)} %copy.229) | copy-start | bytes 196
  416.0 11.6 %copy-start.67 = (bf16[4,100]{1,0:T(4,128)(2,1)S(1)}, bf16[4,100]{1,0:T(4,128)(2,1)}, u32[]{:S(2)}) copy-start(bf16[4,100]{1,0:T(4,128)(2,1)} %get-tuple-element.111) | copy-start | bytes 2404
  416.0 12.1 %copy-start.42 = (f32[1,4,1,768]{3,2,1,0:T(1,128)S(1)}, f32[1,4,1,768]{3,2,1,0:T(1,128)}, u32[]{:S(2)}) copy-start(f32[1,4,1,768]{3,2,1,0:T(1,128)} %slice.407) | copy-start | bytes 36868
  428.2 6.7 copy-start.69
  428.2 8.7 %copy-start.35 = (f32[4,12,1024]{2,0,1:T(4,128)S(1)}, f32[4,12,1024]{2,0,1:T(4,128)}, u32[]{:S(2)}) copy-start(f32[4,12,1024]{2,0,1:T(4,128)} %get-tuple-element.137) | copy-start | bytes 589828
  428.2 8.7 %copy-start.65 = (f32[4,12]{0,1:T(8,128)S(1)}, f32[4,12]{0,1:T(8,128)}, u32[]{:S(2)}) copy-start(f32[4,12]{0,1:T(8,128)} %get-tuple-element.136) | copy-start | bytes 580
  434.8 3.9 copy-start.21
  452.5 4.7 copy-start.31
  491.9 4.0 copy-start.24
  491.9 4.0 copy-start.26
  491.9 4.0 copy-start.45
  491.9 4.0 copy-start.47
  491.9 4.0 copy-start.55
  491.9 4.0 copy-start.57
  491.9 4.0 copy-start.61
  495.9 9.3 %copy-start.2 = (f32[1,988,768]{2,1,0:T(8,128)S(1)}, f32[1,988,768]{2,1,0:T(8,128)}, u32[]{:S(2)}) copy-start(f32[1,988,768]{2,1,0:T(8,128)} %reshape.1866) | copy-start | bytes 9105412
  495.9 9.3 %copy-start.4 = (f32[1,988,768]{2,1,0:T(8,128)S(1)}, f32[1,988,768]{2,1,0:T(8,128)}, u32[]{:S(2)}) copy-start(f32[1,988,768]{2,1,0:T(8,128)} %reshape.1856) | copy-start | bytes 9105412
  495.9 9.3 %copy-start.5 = (f32[1,988,768]{2,1,0:T(8,128)S(1)}, f32[1,988,768]{2,1,0:T(8,128)}, u32[]{:S(2)}) copy-start(f32[1,988,768]{2,1,0:T(8,128)} %concatenate.162) | copy-start | bytes 9105412
  496.0 9.3 %copy-start.6 = (f32[1,988,768]{2,1,0:T(8,128)S(1)}, f32[1,988,768]{2,1,0:T(8,128)}, u32[]{:S(2)}) copy-start(f32[1,988,768]{2,1,0:T(8,128)} %concatenate.156) | copy-start | bytes 9105412
  545.2 196.4 %all-gather.17.cloned.1.call-start = ((), (), s32[]{:S(2)}) async-start(), calls=%async_computation.4 | async-start | bytes 1267200 | tf_op jit(solution)/shard_map/all_gather | solution.py:280
  685.9 116.2 %all-gather.19.cloned.1.call-start = ((), (), s32[]{:S(2)}) async-start(), calls=%async_computation.5 | async-start | bytes 2534400 | tf_op jit(solution)/shard_map/all_gather | solution.py:281
  687.9 5.8 copy-start.10
  (19 other events, 41.8 us)
Sparse Core Ops, SparseCore 0:
  10.2 67.8 all-gather.8
  80.3 39.5 all-gather.10
  122.1 78.6 all-gather.12
  202.8 78.0 all-gather.14
  545.3 138.9 all-reduce.4
  688.0 53.5 all-gather.16
  745.5 56.5 all-gather.18
where the time goes:
time: 841 us; the launch traced here: 830 us
  local copies, waits for them, and re-layouts  310 us (37%)
  waiting for transfers between devices  234 us (28%)
  matrix products  199 us (24%)
  other arithmetic  71.5 us (9%)
  between operations  15.9 us (2%)
    unnamed x8, waiting for transfers between devices  142 us
    dot_general x2, matrix products, forward(): jnp.einsum('rpf,fd->rpd', activated, down_all, preferred_element_type=jnp...  66.8 us
    all_gather x1, waiting for transfers between devices, body(): lax.all_gather(shares[1], ('dp', 'fsdp'), axis=0, tiled=True)  52.2 us
    reshape x8, local copies, waits for them, and re-layouts, class_rows(): rows_val[:, :IMGS_ROW * IMG]  36.3 us
    slice x13, local copies, waits for them, and re-layouts, class_rows(): rows_val[:, :IMGS_ROW * IMG]  35.2 us
    unnamed x164, local copies, waits for them, and re-layouts  30.1 us
    all_gather x1, waiting for transfers between devices, body(): lax.all_gather(shares[0], ('dp', 'fsdp'), axis=0, tiled=True)  25.3 us
    sub x4, matrix products, attend_group(): attn_probs = jax.nn.softmax(scores, axis=-1).astype(jnp.bfloat16)  24.1 us
  transfers between devices with their start and end apart: 7, of which 4 were waited for; matrix products, arithmetic and copies ran while one was open for 37% of the time, Pallas kernels for 0%

commit v1 on v0

v1 whole, which is shorter than its diff:
```python
import functools

import jax
import jax.numpy as jnp
import numpy as np
from jax import lax
from jax.experimental import pallas as pl
from jax.experimental.pallas import tpu as pltpu
from jax.sharding import PartitionSpec as P

D = 768
HEADS = 12
HDIM = 64
FF = 3072
CLASSES = 100
TASKS = 8
PROMPTS = 50
IMG = 247
IMGS_ROW = 4
ROW = 1024
MB = 2

BLOCK = 256
TAIL = BLOCK - IMG
TAIL_AT = IMGS_ROW * IMG
HEADS_PAD = 16
SLOTS = 64
EPSILON = 1e-06
MASKED_SCORE = -1e30
BF16 = jnp.bfloat16
F32 = jnp.float32


def dot(lhs, rhs):
    return lax.dot_general(lhs, rhs, (((1,), (0,)), ((), ())), preferred_element_type=F32)


def dot_t(lhs, rhs):
    return lax.dot_general(lhs, rhs, (((1,), (1,)), ((), ())), preferred_element_type=F32)


def unit_norm(rows):
    centred = rows - jnp.mean(rows, axis=-1, keepdims=True)
    inv_std = lax.rsqrt(jnp.mean(centred * centred, axis=-1, keepdims=True) + EPSILON)
    return centred * inv_std, inv_std


def norm_back(grad_out, unit_rows, inv_std, gain):
    scaled = grad_out * gain
    inner_mean = jnp.mean(scaled * unit_rows, axis=-1, keepdims=True)
    return inv_std * (scaled - jnp.mean(scaled, axis=-1, keepdims=True) - unit_rows * inner_mean)


def gelu(rows):
    return 0.5 * rows * (1.0 + lax.erf(rows * np.float32(np.sqrt(0.5))))


def gelu_slope(rows):
    upper = 0.5 * (1.0 + lax.erf(rows * np.float32(np.sqrt(0.5))))
    return upper + rows * jnp.exp(-0.5 * rows * rows) * np.float32(1.0 / np.sqrt(2.0 * np.pi))


def params(mib):
    return pltpu.CompilerParams(vmem_limit_bytes=mib << 20)


def cost(gflops, mbytes):
    return pl.CostEstimate(flops=int(gflops * 1e9), bytes_accessed=int(mbytes * 1e6), transcendentals=0)


def far(array):
    return pltpu.with_memory_space_constraint(array, pltpu.HBM)


def whole(array):
    return pl.BlockSpec(array.shape, lambda *grid: (0,) * array.ndim, pipeline_mode=pl.Buffered(1))


def make_copies(pairs, sems, first=0):
    return [pltpu.make_async_copy(src, dst, sems.at[first + k]) for k, (src, dst) in enumerate(pairs)]


def start_copies(pairs, sems):
    copies = make_copies(pairs, sems)
    for copy in copies:
        copy.start()
    return copies


def run_copies(pairs, sems):
    for copy in start_copies(pairs, sems):
        copy.wait()


LANES = 128
LANE_BLOCKS = [slice(at, at + LANES) for at in range(0, D, LANES)]


def by_lanes(buf, rows):
    for block, lanes in enumerate(LANE_BLOCKS):
        buf[block] = rows[:, lanes]


def read_strided(buf, start, count):
    at = pl.ds(start, count, stride=TASKS)
    return jnp.concatenate([buf[block, at] for block in range(len(LANE_BLOCKS))], axis=1)


def write_strided(buf, start, rows):
    at = pl.ds(start, rows.shape[0], stride=TASKS)
    for block, lanes in enumerate(LANE_BLOCKS):
        buf[block, at] = rows[:, lanes]


def assemble_kernel(
    ids_ref, tokens_ref, prompts_ref, gain_ref, resid_ref, normed_ref, row_buf, img_buf, prompt_buf
):
    row_at = pl.program_id(0)
    by_lanes(prompt_buf, prompts_ref[...].astype(F32))
    row_buf[...] = tokens_ref[0].astype(F32)
    for img in range(IMGS_ROW):
        img_buf[0 : IMG + 1] = row_buf[img * IMG : img * IMG + IMG + 1]
        img_buf[IMG:BLOCK] = row_buf[TAIL_AT + img * TAIL : TAIL_AT + (img + 1) * TAIL]
        img_buf[1 : 1 + PROMPTS] = read_strided(prompt_buf, ids_ref[row_at, img], PROMPTS)
        rows = img_buf[...]
        at = slice(img * BLOCK, (img + 1) * BLOCK)
        resid_ref[0, at] = rows.astype(BF16)
        unit_rows, _ = unit_norm(rows)
        normed_ref[0, at] = (unit_rows * gain_ref[...]).astype(BF16)


def assemble(ids, tokens, prompts, gain):
    rows_n = tokens.shape[0]
    row_spec = pl.BlockSpec((1, ROW, D), lambda r: (r, 0, 0))
    return pl.pallas_call(
        assemble_kernel,
        grid=(rows_n,),
        in_specs=[pl.BlockSpec(memory_space=pltpu.SMEM), row_spec, whole(prompts), whole(gain)],
        out_specs=[row_spec, row_spec],
        out_shape=[jax.ShapeDtypeStruct(tokens.shape, BF16)] * 2,
        scratch_shapes=[
            pltpu.VMEM((ROW, D), F32),
            pltpu.VMEM((BLOCK, D), F32),
            pltpu.VMEM((len(LANE_BLOCKS), PROMPTS * TASKS, LANES), F32),
        ],
        compiler_params=params(32),
        cost_estimate=cost(0.1, 10),
        name="assemble",
    )(ids, tokens, prompts, gain)


def softmax_pair(queries, keys, values_ext, bias, first_half):
    halves = []
    for scale_row in first_half:
        scores = dot_t(queries * scale_row, keys) + bias
        weights = jnp.exp(scores - jnp.max(scores, axis=-1, keepdims=True)).astype(BF16)
        summed = dot(weights, values_ext)
        halves.append(summed[:, :128] / summed[:, 128:])
    lanes = lax.broadcasted_iota(jnp.int32, halves[0].shape, 1)
    return jnp.where(lanes < HDIM, halves[0], halves[1])


def attend_kernel(plan, normed_ref, resid_ref, gain_ref, *refs):
    pieces, refs = refs[:-11], refs[-11:]
    kv_ref, query_ref, probs_ref, middle_ref, class_ref, normed_two_ref, front_ref = refs[:7]
    packed_buf, tail_buf, tail_context, sems = refs[7:]
    img = pl.program_id(1)
    lane = lax.broadcasted_iota(jnp.int32, (1, 128), 1)
    scale = HDIM ** (-0.5)
    halves = [
        jnp.where(lane < HDIM, scale, 0.0).astype(BF16),
        jnp.where(lane < HDIM, 0.0, scale).astype(BF16),
    ]

    @pl.when((pl.program_id(0) == 0) & (img == 0))
    def _():
        run_copies(plan(pieces, front_ref), sems)

    @pl.when(img == 0)
    def _():
        ends = [normed_ref[0, (at + 1) * BLOCK - 16 : (at + 1) * BLOCK, :] for at in range(IMGS_ROW)]
        tail_buf[...] = dot(jnp.concatenate(ends, axis=0), front_ref[:, : 3 * D]).astype(BF16)
        tail_at = lax.broadcasted_iota(jnp.int32, (1, 16 * IMGS_ROW), 1)
        tail_bias = jnp.where(tail_at % 16 >= 16 - TAIL, 0.0, MASKED_SCORE)
        tail_ones = jnp.ones((16 * IMGS_ROW, 128), BF16)
        for pair in range(HEADS // 2):
            q, k, v = (tail_buf[:, part * D + pair * 128 : part * D + (pair + 1) * 128] for part in range(3))
            tail_context[:, pair * 128 : (pair + 1) * 128] = softmax_pair(
                q, k, jnp.concatenate([v, tail_ones], axis=1), tail_bias, halves
            )

    tokens = normed_ref[0, pl.ds(pl.multiple_of(img * BLOCK, BLOCK), BLOCK), :]
    for part in range(3):
        cols = slice(part * D, (part + 1) * D)
        packed_buf[:, cols] = dot(tokens, front_ref[:, cols]).astype(BF16)
    kv_ref[0] = packed_buf[:, D:]
    query_ref[0] = packed_buf[:16, :D]
    key_at = lax.broadcasted_iota(jnp.int32, (1, BLOCK), 1)
    bias = jnp.where(key_at < IMG, 0.0, MASKED_SCORE)
    queries = packed_buf[0:1, :D] * head_rows_mask().astype(BF16) * np.float32(scale).astype(BF16)
    scores = dot_t(queries, packed_buf[:, D : 2 * D]) + bias
    probs = jnp.exp(scores - jnp.max(scores, axis=-1, keepdims=True))
    probs_ref[0] = probs / jnp.sum(probs, axis=-1, keepdims=True)
    ones = jnp.ones((BLOCK, 128), BF16)
    is_tail = lax.broadcasted_iota(jnp.int32, (16, D), 0) >= 16 - TAIL
    context = []
    for pair in range(HEADS // 2):
        q, k, v = (packed_buf[:, part * D + pair * 128 : part * D + (pair + 1) * 128] for part in range(3))
        context.append(softmax_pair(q, k, jnp.concatenate([v, ones], axis=1), bias, halves))
    context = jnp.concatenate(context, axis=1)
    tail = tail_context[pl.ds(pl.multiple_of(img * 16, 16), 16), :]
    last = jnp.where(is_tail, tail, context[BLOCK - 16 :])
    context = jnp.concatenate([context[: BLOCK - 16], last], axis=0).astype(BF16)
    middle = resid_ref[0].astype(F32) + dot(context, front_ref[:, 3 * D :])
    middle_ref[...] = middle
    class_ref[0] = middle[:8]
    normed_two_ref[...] = (unit_norm(middle)[0] * gain_ref[...]).astype(BF16)


def head_rows_mask():
    return (
        lax.broadcasted_iota(jnp.int32, (HEADS_PAD, D), 1) // HDIM
        == lax.broadcasted_iota(jnp.int32, (HEADS_PAD, D), 0)
    ).astype(F32)


def attend(normed, resid, gain, pieces, plan, copies_n):
    rows_n = normed.shape[0]
    images = rows_n * IMGS_ROW
    flat = lambda r, i: (r * IMGS_ROW + i, 0)
    cube = lambda r, i: (r * IMGS_ROW + i, 0, 0)
    front = jax.ShapeDtypeStruct((D, 4 * D), BF16)
    outs = [
        (images, BLOCK, 2 * D, BF16),
        (images, 16, D, BF16),
        (images, HEADS_PAD, BLOCK, F32),
        (images * BLOCK, D, F32),
        (images, 8, D, F32),
        (images * BLOCK, D, BF16),
    ]
    specs = [
        pl.BlockSpec((1, *o[1:-1]), cube) if len(o) == 4 else pl.BlockSpec((BLOCK, D), flat) for o in outs
    ]
    return pl.pallas_call(
        functools.partial(attend_kernel, plan),
        grid=(rows_n, IMGS_ROW),
        in_specs=[
            pl.BlockSpec((1, ROW, D), lambda r, i: (r, 0, 0)),
            pl.BlockSpec((1, BLOCK, D), lambda r, i: (r, i, 0)),
            whole(gain),
        ]
        + [pl.BlockSpec(memory_space=pltpu.HBM)] * len(pieces),
        out_specs=[*specs, whole(front)],
        out_shape=[*(jax.ShapeDtypeStruct(o[:-1], o[-1]) for o in outs), front],
        scratch_shapes=[
            pltpu.VMEM((BLOCK, 3 * D), BF16),
            pltpu.VMEM((16 * IMGS_ROW, 3 * D), BF16),
            pltpu.VMEM((16 * IMGS_ROW, D), F32),
            pltpu.SemaphoreType.DMA((copies_n,)),
        ],
        compiler_params=params(40),
        cost_estimate=cost(16, 30),
        name="attend",
    )(far(normed), far(resid), gain, *pieces)


def class_kernel(
    plans, ids_ref, middle_ref, queries_ref, probs_ref, grads_ref, heads_ref,
    attn_gain_ref, mlp_gain_ref, final_gain_ref, kv_hbm, front_hbm, *refs,
):
    feed_refs = refs[:-16]
    (
        sent_ref, weights_ref, routes_ref, d_class_ref, d_middle_ref, up_ref, down_ref,
        q_buf, c_buf, dq_buf, score_slots, prob_slots, front_ref, kv_ref, sems, feed_sems,
    ) = refs[-16:]
    images = middle_ref.shape[0]
    up_plan, down_plan = plans
    up_pairs, down_pairs = sum(up_plan(feed_refs, up_ref), []), sum(down_plan(feed_refs, down_ref), [])
    feed_copies = start_copies(up_pairs + down_pairs, feed_sems)
    front_copy = pltpu.make_async_copy(front_hbm, front_ref, sems.at[0])
    front_copy.start()
    kv_copy = pltpu.make_async_copy(kv_hbm, kv_ref, sems.at[1])
    kv_copy.start()
    spread = (
        lax.broadcasted_iota(jnp.int32, (128, CLASSES * TASKS), 1) // TASKS
        == lax.broadcasted_iota(jnp.int32, (128, CLASSES * TASKS), 0)
    ).astype(F32).astype(BF16)
    task_at = lax.broadcasted_iota(jnp.int32, (images, CLASSES * TASKS), 1) % TASKS
    chosen = jnp.where(ids_ref[...] == task_at, dot(grads_ref[...], spread), 0.0).astype(BF16)
    d_final = dot(chosen, heads_ref[...])
    mlp_gain, final_gain = mlp_gain_ref[...], final_gain_ref[...]
    middle = middle_ref[:, 0, :]
    unit_mlp, inv_mlp = unit_norm(middle)
    for copy in feed_copies[: len(up_pairs)]:
        copy.wait()
    pre = dot((unit_mlp * mlp_gain).astype(BF16), up_ref[...])
    activated = gelu(pre).astype(BF16)
    for copy in feed_copies[len(up_pairs) :]:
        copy.wait()
    output = middle + dot(activated, down_ref[...])
    unit_fin, inv_fin = unit_norm(output)
    sent_ref[:, 2 * D : 3 * D] = (unit_fin * final_gain).astype(BF16)
    d_output = norm_back(d_final, unit_fin, inv_fin, final_gain)
    d_act = dot_t(d_output.astype(BF16), down_ref[...])
    d_pre = (d_act * gelu_slope(pre)).astype(BF16)
    d_middle = d_output + norm_back(dot_t(d_pre, up_ref[...]), unit_mlp, inv_mlp, mlp_gain)
    d_middle_ref[...] = d_middle
    front_copy.wait()
    d_context = dot_t(d_middle.astype(BF16), front_ref[:, 3 * D :]).astype(BF16)
    sent_ref[:, 3 * D : 4 * D] = d_context
    of_head = head_rows_mask()
    own = of_head.astype(BF16)
    scale = HDIM ** (-0.5)
    kv_copy.wait()
    for img in range(images):
        at = slice(img * HEADS_PAD, (img + 1) * HEADS_PAD)
        query = queries_ref[img, 0:1, :]
        sent_ref[img : img + 1, :D] = query
        q_buf[at] = query * own * np.float32(scale).astype(BF16)
        d_rows = d_context[img : img + 1] * own
        c_buf[at] = d_rows
        keys, values = kv_ref[img, :, :D], kv_ref[img, :, D:]
        probs = probs_ref[img]
        d_probs = dot_t(d_rows, values)
        d_scores = probs * (d_probs - jnp.sum(probs * d_probs, axis=-1, keepdims=True))
        score_slots[at] = d_scores[:, :128]
        prob_slots[at] = probs[:, :128]
        d_scores = d_scores.astype(BF16)
        weights_ref[img, :HEADS_PAD] = d_scores
        weights_ref[img, HEADS_PAD:] = probs.astype(BF16)
        dq_buf[img : img + 1] = jnp.sum(dot(d_scores, keys) * of_head, axis=0, keepdims=True) * scale
    lane = lax.broadcasted_iota(jnp.int32, (images, 128), 1)
    for slots, start in ((prob_slots, D), (score_slots, 4 * D)):
        for pair in range(HEADS // 2):
            first, second = (slots[pl.ds(2 * pair + h, images, stride=HEADS_PAD)] for h in range(2))
            both = jnp.where(lane < SLOTS, first, pltpu.roll(second, SLOTS, 1))
            sent_ref[:, start + pair * 128 : start + (pair + 1) * 128] = both.astype(BF16)
    sent_ref[:, 5 * D :] = grads_ref[...]
    by_key = dot_t(q_buf[...], front_ref[:, D : 2 * D]).astype(BF16)
    by_value = dot_t(c_buf[...], front_ref[:, 2 * D : 3 * D]).astype(BF16)
    for img in range(images):
        at = slice(img * HEADS_PAD, (img + 1) * HEADS_PAD)
        routes_ref[img, :HEADS_PAD] = by_key[at]
        routes_ref[img, HEADS_PAD:] = by_value[at]
    d_class_ref[...] = dot_t(dq_buf[...].astype(BF16), front_ref[:, :D])


SENT = 5 * D + 128


def class_path(ids, middle, queries, probs, grads, heads, gains, kv, front, feed_weights):
    images = middle.shape[0]
    operands = (ids, middle, queries, probs, grads, heads, *gains)
    feed_arrays, plans, copies_n = feed_weights
    remote = (kv, front, *feed_arrays)
    outs = [
        jax.ShapeDtypeStruct((images, SENT), BF16),
        jax.ShapeDtypeStruct((images, 2 * HEADS_PAD, BLOCK), BF16),
        jax.ShapeDtypeStruct((images, 2 * HEADS_PAD, D), BF16),
        jax.ShapeDtypeStruct((images, D), F32),
        jax.ShapeDtypeStruct((images, D), F32),
    ]
    near = [pltpu.VMEM((D, FF), BF16), pltpu.VMEM((FF, D), BF16)]
    return pl.pallas_call(
        functools.partial(class_kernel, plans),
        in_specs=[pl.BlockSpec(memory_space=pltpu.VMEM)] * len(operands)
        + [pl.BlockSpec(memory_space=pltpu.HBM)] * len(remote),
        out_specs=[pl.BlockSpec(memory_space=pltpu.VMEM)] * (len(outs) + 2),
        out_shape=outs + near,
        scratch_shapes=[
            pltpu.VMEM((images * HEADS_PAD, D), BF16),
            pltpu.VMEM((images * HEADS_PAD, D), BF16),
            pltpu.VMEM((images, D), F32),
            pltpu.VMEM((images * HEADS_PAD, 128), F32),
            pltpu.VMEM((images * HEADS_PAD, 128), F32),
            pltpu.VMEM((D, 4 * D), BF16),
            pltpu.VMEM((images, BLOCK, 2 * D), BF16),
            pltpu.SemaphoreType.DMA((2,)),
            pltpu.SemaphoreType.DMA((copies_n,)),
        ],
        compiler_params=params(40),
        cost_estimate=cost(8, 30),
        name="class_path",
    )(*operands, *remote)


FF_STEP = 768


def feed_kernel(normed_ref, middle_ref, up_ref, down_ref, *refs):
    out_ref, row_buf = refs[-2:]
    img = pl.program_id(1)
    rows = normed_ref[...]
    total = middle_ref[...]
    for step in range(FF // FF_STEP):
        at = slice(step * FF_STEP, (step + 1) * FF_STEP)
        total = total + dot(gelu(dot(rows, up_ref[:, at])).astype(BF16), down_ref[at, :])
    for at in range(IMGS_ROW):

        @pl.when(img == at)
        def _():
            row_buf[at * IMG : (at + 1) * IMG] = total[:IMG]
            row_buf[TAIL_AT + at * TAIL : TAIL_AT + (at + 1) * TAIL] = total[IMG:]

    @pl.when(img == IMGS_ROW - 1)
    def _():
        out_ref[0] = row_buf[...].astype(BF16)


def feed(normed, middle, up_all, down_all, first, count, chain):
    rows_n = normed.shape[0] // ROW
    spec = pl.BlockSpec((BLOCK, D), lambda r, i: ((r + first) * IMGS_ROW + i, 0))
    chained = [] if chain is None else [chain]
    return pl.pallas_call(
        feed_kernel,
        grid=(count, IMGS_ROW),
        in_specs=[spec, spec]
        + [pl.BlockSpec(memory_space=pltpu.VMEM)] * 2
        + [pl.BlockSpec(memory_space=pltpu.HBM)] * len(chained),
        out_specs=pl.BlockSpec((1, ROW, D), lambda r, i: (r + first, 0, 0)),
        out_shape=jax.ShapeDtypeStruct((rows_n, ROW, D), BF16),
        input_output_aliases={} if chain is None else {4: 0},
        scratch_shapes=[pltpu.VMEM((ROW, D), F32)],
        compiler_params=params(24),
        cost_estimate=cost(10 * count, 20),
        name="feed",
    )(far(normed), far(middle), up_all, down_all, *chained)


def token_grads_kernel(resid_ref, weights_ref, routes_ref, d_class_ref, d_middle_ref, gain_ref, out_ref):
    row_at = pl.program_id(0)
    gain = gain_ref[...]
    place = lax.broadcasted_iota(jnp.int32, (BLOCK, 1), 0)
    is_class = (place == 0).astype(F32)
    keep = jnp.where((place == 0) | (place > PROMPTS), 1.0, 0.0)
    for img in range(IMGS_ROW):
        one = pl.ds(row_at * IMGS_ROW + img, 1)
        unit_rows, inv_std = unit_norm(resid_ref[0, img * BLOCK : (img + 1) * BLOCK].astype(F32))
        d_normed = lax.dot_general(
            weights_ref[img], routes_ref[img], (((0,), (0,)), ((), ())), preferred_element_type=F32
        )
        d_normed = d_normed + is_class * d_class_ref[one]
        d_resid = norm_back(d_normed, unit_rows, inv_std, gain) + is_class * d_middle_ref[one]
        out_ref[0, img * IMG : (img + 1) * IMG] = (d_resid * keep)[:IMG]
    out_ref[0, TAIL_AT:] = jnp.zeros((ROW - TAIL_AT, D), F32)


def token_grads(resid, weights, routes, d_class, d_middle, gain):
    rows_n = resid.shape[0]
    row_spec = pl.BlockSpec((1, ROW, D), lambda r: (r, 0, 0))
    img_spec = lambda width: pl.BlockSpec((IMGS_ROW, 2 * HEADS_PAD, width), lambda r: (r, 0, 0))
    return pl.pallas_call(
        token_grads_kernel,
        grid=(rows_n,),
        in_specs=[row_spec, img_spec(BLOCK), img_spec(D), whole(d_class), whole(d_middle), whole(gain)],
        out_specs=row_spec,
        out_shape=jax.ShapeDtypeStruct(resid.shape, F32),
        compiler_params=params(32),
        cost_estimate=cost(0.5, 20),
        name="token_grads",
    )(far(resid), weights, routes, d_class, d_middle, gain)


def sums_kernel(front_ref, prompts_ref, gain_ref, *refs):
    parts, (prompt_out, head_out, all_buf, sum_buf, head_buf, prompt_buf, sems) = refs[:-7], refs[-7:]
    rows = parts[0].shape[0]
    run_copies([(part, all_buf.at[pl.ds(at * rows, rows), :]) for at, part in enumerate(parts)], sems)
    scale = np.float32(HDIM ** (-0.5)).astype(BF16)
    column = lambda at: all_buf[:, at * D : (at + 1) * D]
    by_class = all_buf[:, 5 * D :].T
    ids = by_class[CLASSES : CLASSES + 1].astype(F32)
    masks = [(ids == task).astype(F32).astype(BF16) for task in range(TASKS)]
    finals = column(2)
    for task in range(TASKS):
        write_strided(head_buf, task, dot(by_class * masks[task], finals)[:CLASSES])
    for block, lanes in enumerate(LANE_BLOCKS):
        head_out[:, lanes] = head_buf[block]
    lane = lax.broadcasted_iota(jnp.int32, (SLOTS, 128), 1)
    for side, (slots, lane_rows) in enumerate(((column(4), column(0) * scale), (column(1), column(3)))):
        slots = slots.T
        for pair in range(HEADS // 2):
            at = slice(pair * 128, (pair + 1) * 128)
            summed = dot(jnp.concatenate([slots[at] * mask for mask in masks], axis=0), lane_rows[:, at])
            for task in range(TASKS):
                first, second = (summed[task * 128 + h * SLOTS : task * 128 + (h + 1) * SLOTS] for h in range(2))
                sum_buf[task * SLOTS : (task + 1) * SLOTS, side * D + pair * 128 : side * D + (pair + 1) * 128] = (
                    jnp.where(lane < HDIM, first, second).astype(BF16)
                )
    d_normed = dot_t(sum_buf[...], front_ref[:, D : 3 * D])
    by_lanes(prompt_buf, prompts_ref[...].astype(F32))
    for task in range(TASKS):
        unit_rows, inv_std = unit_norm(read_strided(prompt_buf, task, PROMPTS))
        d_task = d_normed[task * SLOTS + 1 : task * SLOTS + 1 + PROMPTS]
        write_strided(prompt_buf, task, norm_back(d_task, unit_rows, inv_std, gain_ref[...]))
    for block, lanes in enumerate(LANE_BLOCKS):
        prompt_out[:, lanes] = prompt_buf[block]


def sums(front, prompts, gain, parts):
    operands = (front, prompts, gain)
    outs = [
        jax.ShapeDtypeStruct((PROMPTS * TASKS, D), F32),
        jax.ShapeDtypeStruct((CLASSES * TASKS, D), F32),
    ]
    images = sum(part.shape[0] for part in parts)
    return pl.pallas_call(
        sums_kernel,
        grid=(1,),
        in_specs=[whole(o) for o in operands] + [pl.BlockSpec(memory_space=pltpu.HBM)] * len(parts),
        out_specs=[whole(o) for o in outs],
        out_shape=outs,
        scratch_shapes=[
            pltpu.VMEM((images, SENT), BF16),
            pltpu.VMEM((TASKS * SLOTS, 2 * D), BF16),
            pltpu.VMEM((len(LANE_BLOCKS), CLASSES * TASKS, LANES), F32),
            pltpu.VMEM((len(LANE_BLOCKS), PROMPTS * TASKS, LANES), F32),
            pltpu.SemaphoreType.DMA((len(parts),)),
        ],
        compiler_params=params(56),
        cost_estimate=cost(5, 15),
        name="sums",
    )(*operands, *parts)


def gather_rows(shard, dp):
    part = shard.shape[0] // dp
    mine = lax.dynamic_slice_in_dim(shard, lax.axis_index("dp") * part, part, 0)
    return lax.all_gather(mine, ("fsdp", "dp"), axis=0, tiled=True)


def copy_whole(at):
    return lambda refs, dst: [(refs[at], dst)]


def places():
    d, f = lax.axis_index("dp"), lax.axis_index("fsdp")
    return d // 2, d % 2, f // 2, f % 2


def exchange(value, dy=0, dc=0, dz=0, dx=0):
    pairs = []
    for at in range(32):
        y, c, z, x = at // 16, at // 8 % 2, at // 2 % 4, at % 2
        pairs.append((at, (((y ^ dy) * 2 + (c ^ dc)) * 4 + (z ^ dz)) * 2 + (x ^ dx)))
    return lax.ppermute(value, ("dp", "fsdp"), pairs)


HALF_COLS = 2 * D


def fetch_front(shard, beside):
    y, c, _, _ = places()
    mine = lax.dynamic_slice(shard, (y * 48, c * HALF_COLS), (48, HALF_COLS))
    along_z = [exchange(mine, dz=r) for r in (1, 2, 3)]
    half = lax.dynamic_slice(shard, (0, c * HALF_COLS), (96, HALF_COLS))
    own_x = exchange(half, dx=1)
    column, *beside = lax.optimization_barrier((jnp.concatenate(along_z, axis=0), *beside))
    over_x, over_y = exchange(column, dx=1), exchange(column, dy=1)
    diag_y, diag_x = exchange(over_x[:80], dy=1), exchange(over_y[80:], dx=1)
    near = [own_x, column, over_x, over_y, diag_y, diag_x]
    pieces = [shard] + near + [exchange(piece, dc=1) for piece in near]

    def plan(refs, dst):
        y, c, z, x = places()
        pairs = [(refs[0], dst.at[pl.ds(pl.multiple_of((z * 2 + x) * 96, 96), 96), :])]
        for side in range(2):
            cols = pl.ds(pl.multiple_of((c ^ side) * HALF_COLS, 128), HALF_COLS)
            own_x, column, over_x, over_y, diag_y, diag_x = refs[1 + 6 * side : 7 + 6 * side]

            def add(ref, start, count, r, x_at, y_at, within=0):
                row = ((z ^ r) * 2 + x_at) * 96 + y_at * 48 + within
                pairs.append((ref.at[pl.ds(start, count), :], dst.at[pl.ds(pl.multiple_of(row, 16), count), cols]))

            add(own_x, 0, 96, 0, x ^ 1, 0)
            for r in (1, 2, 3):
                start = (r - 1) * 48
                add(column, start, 48, r, x, y)
                add(over_x, start, 48, r, x ^ 1, y)
                add(over_y, start, 48, r, x, y ^ 1)
            add(diag_y, 0, 48, 1, x ^ 1, y ^ 1)
            add(diag_y, 48, 32, 2, x ^ 1, y ^ 1)
            add(diag_x, 0, 16, 2, x ^ 1, y ^ 1, 32)
            add(diag_x, 16, 48, 3, x ^ 1, y ^ 1)
        return pairs

    return (pieces, plan, 29), beside


def fetch_rest(up_shard, down_shard):
    d = lax.axis_index("dp")
    up_part = lax.dynamic_slice(up_shard, (0, d * D), (96, D))
    down_part = lax.dynamic_slice_in_dim(down_shard, d * 96, 96, 0)
    gathered = lax.all_gather(jnp.concatenate([up_part, down_part], axis=0), ("fsdp", "dp"), axis=0)

    def up_plan(refs, dst):
        return [
            [(refs[0].at[4 * f + d, 0:96, :], dst.at[96 * f : 96 * f + 96, D * d : D * d + D]) for f in range(8)]
            for d in range(4)
        ]

    def down_plan(refs, dst):
        return [
            [(refs[0].at[at, 96:192, :], dst.at[96 * at : 96 * at + 96]) for at in range(8 * d, 8 * d + 8)]
            for d in range(4)
        ]

    return [gathered], (up_plan, down_plan), 64


def share_rows(rows, works):
    done, parts = None, [rows]
    for work, shifts in zip(works, ([dict(dz=r) for r in (1, 2, 3)], [dict(dx=1)], [dict(dy=1)])):
        rows = jnp.concatenate(parts, axis=0) if len(parts) > 1 else rows
        if done is not None:
            rows, done = lax.optimization_barrier((rows, done))
        parts = [rows] + [exchange(rows, **shift) for shift in shifts]
        done = work(done)
    *parts, done = lax.optimization_barrier((*parts, done))
    return parts + [exchange(part, dc=1) for part in parts], done


def body(
    tuned, dp, tokens, task_ids, logit_grads, prompts, head_weights, qkv_weight, out_weight, up_weight, down_weight,
    attn_gain, mlp_gain, final_gain,
):
    rows_n = tokens.shape[0] * tokens.shape[1]
    images = rows_n * IMGS_ROW
    front_shard = jnp.concatenate([qkv_weight, out_weight], axis=1)
    gains = [gain.reshape(1, D) for gain in (attn_gain, mlp_gain, final_gain)]
    ids = task_ids.reshape(rows_n, IMGS_ROW)
    prompt_rows = prompts.transpose(1, 0, 2).reshape(PROMPTS * TASKS, D)
    resid, normed = assemble(ids, tokens.reshape(rows_n, ROW, D), prompt_rows, gains[0])
    if tuned:
        front_pieces, (resid, normed) = fetch_front(front_shard, (resid, normed))
        feed_weights = fetch_rest(up_weight, down_weight)
    else:
        front_pieces = [gather_rows(front_shard, dp)], copy_whole(0), 1
        plans = tuple(lambda refs, dst, at=at: [copy_whole(at)(refs, dst)] for at in range(2))
        feed_weights = [gather_rows(w, dp) for w in (up_weight, down_weight)], plans, 2
    ids_col = ids.reshape(images, 1)
    head_rows = head_weights.transpose(2, 0, 1).reshape(CLASSES * TASKS, D)
    grads = jnp.concatenate(
        [logit_grads.reshape(images, CLASSES), jnp.broadcast_to(ids_col, (images, 128 - CLASSES)).astype(BF16)], axis=1
    )
    kv, queries, probs, middle, class_middle, normed_two, front = attend(normed, resid, gains[1], *front_pieces)
    sent, weights, routes, d_class, d_middle, up_all, down_all = class_path(
        ids_col, class_middle, queries, probs, grads, head_rows, gains, kv, front, feed_weights
    )
    first_n = rows_n // 2

    def grads_work(done):
        return token_grads(resid, weights, routes, d_class, d_middle, gains[0]), None

    def feed_work(start, count):
        return lambda done: (done[0], feed(normed_two, middle, up_all, down_all, start, count, done[1]))

    works = grads_work, feed_work(0, first_n), feed_work(first_n, rows_n - first_n)
    if tuned:
        parts, (input_grads, activations) = share_rows(sent, works)
    else:
        parts = [lax.all_gather(sent, ("dp", "fsdp"), axis=0, tiled=True)]
        input_grads, activations = works[2](works[1](works[0](None)))
    prompt_out, head_out = sums(front, prompt_rows, gains[0], parts)
    return (
        activations.reshape(tokens.shape),
        input_grads.reshape(tokens.shape),
        prompt_out.reshape(PROMPTS, TASKS, D).transpose(1, 0, 2),
        head_out.reshape(CLASSES, TASKS, D).transpose(1, 2, 0),
    )


def solution(mesh):
    rows = P(None, ("dp", "fsdp"), None, None)
    in_specs = (rows, P(None, ("dp", "fsdp"), None), rows, P(), P(), *(P("fsdp", None),) * 4, P(), P(), P())
    return jax.shard_map(
        functools.partial(body, dict(mesh.shape) == {"dp": 4, "fsdp": 8}, mesh.shape["dp"]),
        mesh=mesh,
        in_specs=in_specs,
        out_specs=(rows, rows, P(), P()),
        check_vma=False,
    )
```

time: 841 us -> 186 us (0.22); the launches traced: 830 us -> 185 us
  local copies, waits for them, and re-layouts: 310 us -> 25.1 us
  waiting for transfers between devices: 234 us -> 27.4 us
  matrix products: 199 us -> 0 us
  Pallas kernels: 0 us -> 95.6 us
  other arithmetic: 71.5 us -> 1.58 us
  starting transfers between devices: 0.53 us -> 21.5 us
    dot_general x38 -> x0, matrix products: 175 us -> none  [the longest x2 66.8 us: forward(): jnp.einsum('rpf,fd->rpd', activated, down_all, preferred_element_type=jnp...]
    unnamed x8 -> x1, waiting for transfers between devices: 142 us -> 0.02 us
    slice x59 -> x2, local copies, waits for them, and re-layouts: 124 us -> 0.71 us  [fetch_front(): diag_y, diag_x = (exchange(over_x[:80], dy=1), exchange(over_y[80:], dx=1))]
    reshape x30 -> x3, local copies, waits for them, and re-layouts: 120 us -> 0.01 us  [body(): gains = [gain.reshape(1, D) for gain in (attn_gain, mlp_gain, final_gain)]]
    pallas_call x0 -> x7, Pallas kernels: none -> 95.6 us  [the longest x1 30.9 us: attend(): pl.pallas_call(functools.partial(attend_kernel, plan), grid=(rows_n, IMGS...]
    all_gather x6 -> x1, waiting for transfers between devices: 92 us -> 0.01 us  [fetch_rest(): lax.all_gather(jnp.concatenate([up_part, down_part], axis=0), ('fsdp', 'd...]
    ppermute x0 -> x21, waiting for transfers between devices: none -> 27.4 us  [exchange(): return lax.ppermute(value, ('dp', 'fsdp'), pairs)]
    sub x4 -> x0, matrix products: 24.1 us -> none  [attend_group(): attn_probs = jax.nn.softmax(scores, axis=-1).astype(jnp.bfloat16)]
  transfers between devices with their start and end apart: 7 -> 22, of which waited for: 4 -> 8; matrix products, arithmetic and copies ran while one was open for 37% -> 2% of each run, Pallas kernels for 0% -> 38%
where the time goes in v1:
time: 186 us; the launch traced here: 185 us
  Pallas kernels  95.6 us (51%)
  waiting for transfers between devices  27.4 us (15%)
  local copies, waits for them, and re-layouts  25.1 us (13%)
  starting transfers between devices  21.5 us (12%)
  between operations  14.3 us (8%)
    pallas_call x1, Pallas kernels, attend(): pl.pallas_call(functools.partial(attend_kernel, plan), grid=(rows_n, IMGS...  30.9 us
    pallas_call x2, Pallas kernels, feed(): pl.pallas_call(feed_kernel, grid=(count, IMGS_ROW), in_specs=[spec, spec]...  28.1 us
    ppermute x21, waiting for transfers between devices, exchange(): return lax.ppermute(value, ('dp', 'fsdp'), pairs)  27.4 us
    unnamed x64, local copies, waits for them, and re-layouts  22 us
    ppermute x21, starting transfers between devices, exchange(): return lax.ppermute(value, ('dp', 'fsdp'), pairs)  21.4 us
    pallas_call x1, Pallas kernels, class_path(): pl.pallas_call(functools.partial(class_kernel, plans), in_specs=[pl.Block...  15.3 us
    pallas_call x1, Pallas kernels, sums(): pl.pallas_call(sums_kernel, grid=(1,), in_specs=[whole(o) for o in operan...  10 us
    pallas_call x1, Pallas kernels, token_grads(): pl.pallas_call(token_grads_kernel, grid=(rows_n,), in_specs=[row_spec, im...  7.83 us
  transfers between devices with their start and end apart: 22, of which 8 were waited for; matrix products, arithmetic and copies ran while one was open for 2% of the time, Pallas kernels for 38%

profile of v1, /device:TPU:0, one launch (start us, length us, event | category | flops | bytes accessed | tf_op | source)
XLA Modules:
  0.0 185.4 jit_solution(14720618695600865936)
XLA Ops:
  7.2 0.0 all-gather.3.cloned.1.call-start
  7.2 1.2 constant_dynamic-slice_fusion
  8.4 0.7 pad_maximum_fusion.2
  9.1 0.0 all-gather.3.cloned.1.call-update
  9.2 1.0 constant_dynamic-update-slice_fusion.1
  10.2 0.9 constant_dynamic-update-slice_fusion.refs_0_
  11.2 0.0 copy-start.2
  11.2 0.0 copy-start.27
  11.2 5.1 %collective-permute-start.2 = (bf16[48,1536]{1,0:T(8,128)(2,1)S(1)}, bf16[48,1536]{1,0:T(8,128)(2,1)S(1)}, u32[]{:S(2)}, u32[]{:S(2)}) collective-permute-start(bf16[48,1536]{1,0:T(8,128)(2,1)S(1)} %dynamic_slice.12), channel_id=1, source_target_pairs={{0,6},{1,7},{2,4},{3,5},{4,2},{5,3},{6,0},{7,1},{8,14},{9,15},{10,... | collective-permute-start | bytes 442376 | tf_op jit(solution)/shard_map/ppermute | solution.py:545
  16.4 0.6 collective-permute-start
  17.0 1.7 collective-permute-start.3
  18.8 0.0 copy-start.4
  18.8 1.1 copy-done.4
  19.8 3.3 %assemble.1 = (bf16[2,1024,768]{2,1,0:T(8,128)(2,1)S(1)}, bf16[2,1024,768]{2,1,0:T(8,128)(2,1)S(1)}) custom-call(s32[2,4]{1,0:T(2,128)S(1)} %bitcast.25, bf16[2,1024,768]{2,1,0:T(8,128)(2,1)S(1)} %bitcast.22, bf16[400,768]{1,0:T(8,128)(2,1)S(1)} %bitcast.24, f32[1,768]{1,0:T(1,128)S(1)} %reshape.49.gain_ref.attn_gain_ref), custom_call_target="tpu_custom_call" | custom-call | flops 100000000 | bytes 10000000 | tf_op jit(solution)/shard_map/assemble/pallas_call | solution.py:135
  23.2 1.7 copy-done.1
  24.8 1.7 copy-done.7
  26.5 6.8 %collective-permute-done.1 = bf16[48,1536]{1,0:T(8,128)(2,1)S(1)} collective-permute-done((bf16[48,1536]{1,0:T(8,128)(2,1)S(1)}, bf16[48,1536]{1,0:T(8,128)(2,1)S(1)}, u32[]{:S(2)}, u32[]{:S(2)}) %collective-permute-start.1) | collective-permute-done | bytes 147488 | tf_op jit(solution)/shard_map/ppermute | solution.py:545
  33.4 1.9 %collective-permute-start.4 = (bf16[144,1536]{1,0:T(8,128)(2,1)S(1)}, bf16[144,1536]{1,0:T(8,128)(2,1)S(1)}, u32[]{:S(2)}, u32[]{:S(2)}) collective-permute-start(bf16[144,1536]{1,0:T(8,128)(2,1)S(1)} %pad_maximum_fusion.1.refs_2_), channel_id=1, source_target_pairs={{0,1},{1,0},{2,3},{3,2},{4,5},{5,4},{6,7},{7,6},{8,9},{9,8},{10,11... | collective-permute-start | bytes 1327112 | tf_op jit(solution)/shard_map/ppermute | solution.py:545
  35.3 1.7 collective-permute-start.5
  37.1 6.4 %collective-permute-done.4.refs_3_ = bf16[144,1536]{1,0:T(8,128)(2,1)S(1)} collective-permute-done((bf16[144,1536]{1,0:T(8,128)(2,1)S(1)}, bf16[144,1536]{1,0:T(8,128)(2,1)S(1)}, u32[]{:S(2)}, u32[]{:S(2)}) %collective-permute-start.4) | collective-permute-done | bytes 442400 | tf_op jit(solution)/shard_map/ppermute | solution.py:545
  43.5 1.9 %collective-permute-start.6 = (bf16[80,1536]{1,0:T(8,128)(2,1)S(1)}, bf16[80,1536]{1,0:T(8,128)(2,1)}, u32[]{:S(2)}, u32[]{:S(2)}) collective-permute-start(bf16[80,1536]{1,0:T(8,128)(2,1)S(1)} %slice.8), channel_id=1, source_target_pairs={{0,16},{1,17},{2,18},{3,19},{4,20},{5,21},{6,22},{7,23},{8,24},{9,... | collective-permute-start | bytes 737288 | tf_op jit(solution)/shard_map/ppermute | solution.py:545
  45.4 4.6 %collective-permute-done.5.refs_4_ = bf16[144,1536]{1,0:T(8,128)(2,1)S(1)} collective-permute-done((bf16[144,1536]{1,0:T(8,128)(2,1)S(1)}, bf16[144,1536]{1,0:T(8,128)(2,1)S(1)}, u32[]{:S(2)}, u32[]{:S(2)}) %collective-permute-start.5) | collective-permute-done | bytes 442400 | tf_op jit(solution)/shard_map/ppermute | solution.py:545
  50.0 0.5 collective-permute-start.10
  50.5 0.7 slice.9
  51.2 0.7 copy-done.13
  51.9 2.0 %collective-permute-done.6.refs_5_ = bf16[80,1536]{1,0:T(8,128)(2,1)} collective-permute-done((bf16[80,1536]{1,0:T(8,128)(2,1)S(1)}, bf16[80,1536]{1,0:T(8,128)(2,1)}, u32[]{:S(2)}, u32[]{:S(2)}) %collective-permute-start.6) | collective-permute-done | bytes 245792 | tf_op jit(solution)/shard_map/ppermute | solution.py:545
  53.9 0.5 broadcast.7
  54.4 0.7 reduce.5
  55.1 3.9 %collective-permute-done.7.refs_6_ = bf16[64,1536]{1,0:T(8,128)(2,1)} collective-permute-done((bf16[64,1536]{1,0:T(8,128)(2,1)}, bf16[64,1536]{1,0:T(8,128)(2,1)}, u32[]{:S(2)}, u32[]{:S(2)}) %collective-permute-start.7) | collective-permute-done | bytes 196640 | tf_op jit(solution)/shard_map/ppermute | solution.py:545
  59.0 0.1 convert_element_type.8
  59.1 0.1 reshape_reshape.4.ids_ref
  59.2 0.1 broadcast_in_dim.2
  59.3 0.1 pad_maximum_fusion.4.grads_ref
  59.4 1.4 collective-permute-done.13.refs_12_
  60.8 0.8 copy-done.9
  61.6 0.8 copy-done.11
  62.3 0.7 copy-done.15
  63.1 1.1 copy-done.3
  64.2 1.0 copy-done.10
  65.2 1.1 copy-done.12
  66.3 1.0 copy-done.14
  67.3 0.9 copy-done.16
  68.2 30.9 %attend.1 = (bf16[8,256,1536]{2,1,0:T(8,128)(2,1)}, bf16[8,16,768]{2,1,0:T(8,128)(2,1)S(1)}, f32[8,16,256]{2,1,0:T(8,128)S(1)}, f32[2048,768]{1,0:T(8,128)}, f32...) custom-call(bf16[2,1024,768]{2,1,0:T(8,128)(2,1)} %copy-done.7, ...), custom_call_target="tpu_custom_call" | custom-call | flops 16000000000 | bytes 30000000 | tf_op jit(solution)/shard_map/attend/pallas_call | solution.py:244
  99.2 2.1 %copy-done.17 = bf16[768,3072]{1,0:T(8,128)(2,1)} copy-done((bf16[768,3072]{1,0:T(8,128)(2,1)}, bf16[768,3072]{1,0:T(8,128)(2,1)S(1)}, u32[]{:S(2)}) %copy-start.17) | copy-done | bytes 4718616
  101.2 1.7 copy-done.18
  103.0 0.7 copy-done.19
  103.7 0.7 copy-done.21
  104.3 0.9 copy-done.20
  105.3 0.9 copy-done.22
  106.2 15.3 %class_path.1 = (bf16[8,3968]{1,0:T(8,128)(2,1)S(1)}, bf16[8,32,256]{2,1,0:T(8,128)(2,1)S(1)}, bf16[8,32,768]{2,1,0:T(8,128)(2,1)S(1)}, f32[8,768]{1,0:T(8,128)S...) custom-call(s32[8,1]{1,0:T(8,128)S(1)} %reshape_reshape.4.ids_ref, ...), custom_call_target="tpu_custom_call" | custom-call | flops 8000000000 | bytes 30000000 | tf_op jit(solution)/shard_map/class_path/pallas_call | solution.py:364
  121.5 2.7 %collective-permute-start.16 = (bf16[8,3968]{1,0:T(8,128)(2,1)S(1)}, bf16[8,3968]{1,0:T(8,128)(2,1)S(1)}, u32[]{:S(2)}, u32[]{:S(2)}) collective-permute-start(bf16[8,3968]{1,0:T(8,128)(2,1)S(1)} %get-tuple-element.44), channel_id=1, source_target_pairs={{0,6},{1,7},{2,4},{3,5},{4,2},{5,3},{6,0},{7,1},{8,14},{9,15},{10,... | collective-permute-start | bytes 190472 | tf_op jit(solution)/shard_map/ppermute | solution.py:545
  124.2 1.8 collective-permute-start.14
  126.0 7.8 %token_grads.1 = f32[2,1024,768]{2,1,0:T(8,128)} custom-call(bf16[2,1024,768]{2,1,0:T(8,128)(2,1)} %copy-done.1, bf16[8,32,256]{2,1,0:T(8,128)(2,1)S(1)} %get-tuple-element.45.weights_ref, bf16[8,32,768]{2,1,0:T(8,128)(2,1)S(1)} %get-tuple-element.46.routes_ref, f32[8,768]{1,0:T(8,128)S(1)} %get-tuple-element.47.d_class_ref, ...), custom_call_target="tpu_custom_call" | custom-call | flops 500000000 | bytes 20000000 | tf_op jit(solution)/shard_map/token_grads/pallas_call | solution.py:452
  133.9 0.3 collective-permute-start.17
  134.2 14.1 %feed.2.refs_0_ = bf16[2,1024,768]{2,1,0:T(8,128)(2,1)} custom-call(bf16[2048,768]{1,0:T(8,128)(2,1)} %copy-done.18, f32[2048,768]{1,0:T(8,128)} %get-tuple-element.52.middle_ref, bf16[768,3072]{1,0:T(8,128)(2,1)S(1)} %get-tuple-element.53.up_ref, bf16[3072,768]{1,0:T(8,128)(2,1)S(1)} %get-tuple-element.54.down_ref), custom_call_target="tpu_custom_call" | custom-call | flops 10000000000 | bytes 20000000 | tf_op jit(solution)/shard_map/feed/pallas_call | solution.py:414
  148.3 2.5 %collective-permute-start.18 = (bf16[64,3968]{1,0:T(8,128)(2,1)S(1)}, bf16[64,3968]{1,0:T(8,128)(2,1)S(1)}, u32[]{:S(2)}, u32[]{:S(2)}) collective-permute-start(bf16[64,3968]{1,0:T(8,128)(2,1)S(1)} %pad_maximum_fusion.refs_0_), channel_id=1, source_target_pairs={{0,16},{1,17},{2,18},{3,19},{4,20},{5,21},{6,22},{7,23},{8,24},{9,... | collective-permute-start | bytes 1523720 | tf_op jit(solution)/shard_map/ppermute | solution.py:545
  150.9 14.1 %feed.3 = bf16[2,1024,768]{2,1,0:T(8,128)(2,1)} custom-call(bf16[2048,768]{1,0:T(8,128)(2,1)} %copy-done.18, f32[2048,768]{1,0:T(8,128)} %get-tuple-element.52.middle_ref, bf16[768,3072]{1,0:T(8,128)(2,1)S(1)} %get-tuple-element.53.up_ref, bf16[3072,768]{1,0:T(8,128)(2,1)S(1)} %get-tuple-element.54.down_ref, ...), custom_call_target="tpu_custom_call", output_to_operand_aliasing={{}: (4, {})} | custom-call | flops 10000000000 | bytes 20000000 | tf_op jit(solution)/shard_map/feed/pallas_call | solution.py:414
  164.9 0.1 collective-permute-start.19
  165.0 0.5 collective-permute-start.20
  165.5 1.4 collective-permute-done.19.refs_2_
  166.9 0.7 collective-permute-done.20.refs_3_
  167.6 0.1 copy-done.29
  167.7 0.8 copy-done.30
  168.5 10.0 %sums.1 = (f32[400,768]{1,0:T(8,128)}, f32[800,768]{1,0:T(8,128)}) custom-call(bf16[768,3072]{1,0:T(8,128)(2,1)} %copy-done.17, bf16[400,768]{1,0:T(8,128)(2,1)} %bitcast.23, f32[1,768]{1,0:T(1,128)} %copy-done.5, bf16[64,3968]{1,0:T(8,128)(2,1)} %copy-done.23, bf16[64,3968]{1,0:T(8,128)(2,1)} %copy-done.28, bf16[64,3968]{1,0:T(8,128)(2,1)} %copy-done.29, ...), custom_call_target="tpu_custom_call" | custom-call | flops 5000000000 | bytes 15000000 | tf_op jit(solution)/shard_map/sums/pallas_call | solution.py:506
  (71 shorter events, 0.3 us)
Async XLA Ops:
  7.2 11.6 %copy-start.24 = (f32[768]{0:T(1024)S(1)}, f32[768]{0:T(1024)}, u32[]{:S(2)}) copy-start(f32[768]{0:T(1024)} %param.21) | copy-start | bytes 9220
  7.2 11.6 %copy-start.6 = (s32[2,1,4]{2,1,0:T(1,128)S(1)}, s32[2,1,4]{2,1,0:T(1,128)}, u32[]{:S(2)}) copy-start(s32[2,1,4]{2,1,0:T(1,128)} %param.13) | copy-start | bytes 100
  7.2 11.6 %copy-start = (bf16[2,1,1024,768]{3,2,1,0:T(8,128)(2,1)S(1)}, bf16[2,1,1024,768]{3,2,1,0:T(8,128)(2,1)}, u32[]{:S(2)}) copy-start(bf16[2,1,1024,768]{3,2,1,0:T(8,128)(2,1)} %param.12) | copy-start | bytes 9437188
  7.2 97.1 %all-gather.3.cloned.1.call-start = ((), (), s32[]{:S(2)}) async-start(), calls=%async_computation | async-start | bytes 9732096 | tf_op jit(solution)/shard_map/all_gather | solution.py:593
  11.2 7.6 %copy-start.2 = (bf16[96,3072]{1,0:T(8,128)(2,1)}, bf16[96,3072]{1,0:T(8,128)(2,1)S(1)}, u32[]{:S(2)}) copy-start(bf16[96,3072]{1,0:T(8,128)(2,1)S(1)} %constant_dynamic-update-slice_fusion.refs_0_) | copy-start | bytes 1769476
  11.2 47.9 %copy-start.25 = (f32[768]{0:T(1024)S(1)}, f32[768]{0:T(1024)}, u32[]{:S(2)}) copy-start(f32[768]{0:T(1024)} %param.22) | copy-start | bytes 9220
  11.2 48.0 %copy-start.26 = (f32[768]{0:T(1024)S(1)}, f32[768]{0:T(1024)}, u32[]{:S(2)}) copy-start(f32[768]{0:T(1024)} %param.23) | copy-start | bytes 9220
  11.2 48.1 %copy-start.27 = (bf16[2,1,4,100]{3,2,1,0:T(4,128)(2,1)S(1)}, bf16[2,1,4,100]{3,2,1,0:T(4,128)(2,1)}, u32[]{:S(2)}) copy-start(bf16[2,1,4,100]{3,2,1,0:T(4,128)(2,1)} %param.14) | copy-start | bytes 4804
  11.2 15.3 %collective-permute-start.2 = (bf16[48,1536]{1,0:T(8,128)(2,1)S(1)}, bf16[48,1536]{1,0:T(8,128)(2,1)S(1)}, u32[]{:S(2)}, u32[]{:S(2)}) collective-permute-start(bf16[48,1536]{1,0:T(8,128)(2,1)S(1)} %dynamic_slice.12), channel_id=1, source_target_pairs={{0,6},{1,7},{2,4},{3,5},{4,2},{5,3},{6,0},{7,1},{8,14},{9,15},{10,... | collective-permute-start | bytes 442376 | tf_op jit(solution)/shard_map/ppermute | solution.py:545
  16.4 17.0 %collective-permute-start.1 = (bf16[48,1536]{1,0:T(8,128)(2,1)S(1)}, bf16[48,1536]{1,0:T(8,128)(2,1)S(1)}, u32[]{:S(2)}, u32[]{:S(2)}) collective-permute-start(bf16[48,1536]{1,0:T(8,128)(2,1)S(1)} %dynamic_slice.12), channel_id=1, source_target_pairs={{0,4},{1,5},{2,6},{3,7},{4,0},{5,1},{6,2},{7,3},{8,12},{9,13},{10,... | collective-permute-start | bytes 442376 | tf_op jit(solution)/shard_map/ppermute | solution.py:545
  16.4 17.0 %collective-permute-start = (bf16[48,1536]{1,0:T(8,128)(2,1)S(1)}, bf16[48,1536]{1,0:T(8,128)(2,1)S(1)}, u32[]{:S(2)}, u32[]{:S(2)}) collective-permute-start(bf16[48,1536]{1,0:T(8,128)(2,1)S(1)} %dynamic_slice.12), channel_id=1, source_target_pairs={{0,2},{1,3},{2,0},{3,1},{4,6},{5,7},{6,4},{7,5},{8,10},{9,11},{10,... | collective-permute-start | bytes 442376 | tf_op jit(solution)/shard_map/ppermute | solution.py:545
  17.0 20.0 %collective-permute-start.3 = (bf16[96,1536]{1,0:T(8,128)(2,1)S(1)}, bf16[96,1536]{1,0:T(8,128)(2,1)S(1)}, u32[]{:S(2)}, u32[]{:S(2)}) collective-permute-start(bf16[96,1536]{1,0:T(8,128)(2,1)S(1)} %constant_dynamic-slice_fusion.2), channel_id=1, source_target_pairs={{0,1},{1,0},{2,3},{3,2},{4,5},{5,4},{6,7},{7,6},{8,9},{9,8},{10,11... | collective-permute-start | bytes 884744 | tf_op jit(solution)/shard_map/ppermute | solution.py:545
  18.7 107.3 %copy-start.5 = (f32[1,768]{1,0:T(1,128)}, f32[1,768]{1,0:T(1,128)S(1)}, u32[]{:S(2)}) copy-start(f32[1,768]{1,0:T(1,128)S(1)} %reshape.49.gain_ref.attn_gain_ref) | copy-start | bytes 9220
  18.8 1.1 copy-start.4
  23.2 1.7 copy-start.1
  24.8 1.7 copy-start.7
  33.4 10.1 %collective-permute-start.4 = (bf16[144,1536]{1,0:T(8,128)(2,1)S(1)}, bf16[144,1536]{1,0:T(8,128)(2,1)S(1)}, u32[]{:S(2)}, u32[]{:S(2)}) collective-permute-start(bf16[144,1536]{1,0:T(8,128)(2,1)S(1)} %pad_maximum_fusion.1.refs_2_), channel_id=1, source_target_pairs={{0,1},{1,0},{2,3},{3,2},{4,5},{5,4},{6,7},{7,6},{8,9},{9,8},{10,11... | collective-permute-start | bytes 1327112 | tf_op jit(solution)/shard_map/ppermute | solution.py:545
  35.3 14.7 %collective-permute-start.5 = (bf16[144,1536]{1,0:T(8,128)(2,1)S(1)}, bf16[144,1536]{1,0:T(8,128)(2,1)S(1)}, u32[]{:S(2)}, u32[]{:S(2)}) collective-permute-start(bf16[144,1536]{1,0:T(8,128)(2,1)S(1)} %pad_maximum_fusion.1.refs_2_), channel_id=1, source_target_pairs={{0,16},{1,17},{2,18},{3,19},{4,20},{5,21},{6,22},{7,23},{8,24},{9,... | collective-permute-start | bytes 1327112 | tf_op jit(solution)/shard_map/ppermute | solution.py:545
  37.1 14.1 %collective-permute-start.8 = (bf16[96,1536]{1,0:T(8,128)(2,1)S(1)}, bf16[96,1536]{1,0:T(8,128)(2,1)S(1)}, u32[]{:S(2)}, u32[]{:S(2)}) collective-permute-start(bf16[96,1536]{1,0:T(8,128)(2,1)S(1)} %collective-permute-done.3.refs_1_), channel_id=1, source_target_pairs={{0,8},{1,9},{2,10},{3,11},{4,12},{5,13},{6,14},{7,15},{8,0},{9,1},... | collective-permute-start | bytes 884744 | tf_op jit(solution)/shard_map/ppermute | solution.py:545
  43.5 10.4 %collective-permute-start.6 = (bf16[80,1536]{1,0:T(8,128)(2,1)S(1)}, bf16[80,1536]{1,0:T(8,128)(2,1)}, u32[]{:S(2)}, u32[]{:S(2)}) collective-permute-start(bf16[80,1536]{1,0:T(8,128)(2,1)S(1)} %slice.8), channel_id=1, source_target_pairs={{0,16},{1,17},{2,18},{3,19},{4,20},{5,21},{6,22},{7,23},{8,24},{9,... | collective-permute-start | bytes 737288 | tf_op jit(solution)/shard_map/ppermute | solution.py:545
  45.4 14.0 %collective-permute-start.9 = (bf16[144,1536]{1,0:T(8,128)(2,1)S(1)}, bf16[144,1536]{1,0:T(8,128)(2,1)S(1)}, u32[]{:S(2)}, u32[]{:S(2)}) collective-permute-start(bf16[144,1536]{1,0:T(8,128)(2,1)S(1)} %pad_maximum_fusion.1.refs_2_), channel_id=1, source_target_pairs={{0,8},{1,9},{2,10},{3,11},{4,12},{5,13},{6,14},{7,15},{8,0},{9,1},... | collective-permute-start | bytes 1327112 | tf_op jit(solution)/shard_map/ppermute | solution.py:545
  50.0 10.8 %collective-permute-start.11 = (bf16[144,1536]{1,0:T(8,128)(2,1)S(1)}, bf16[144,1536]{1,0:T(8,128)(2,1)S(1)}, u32[]{:S(2)}, u32[]{:S(2)}) collective-permute-start(bf16[144,1536]{1,0:T(8,128)(2,1)S(1)} %collective-permute-done.5.refs_4_), channel_id=1, source_target_pairs={{0,8},{1,9},{2,10},{3,11},{4,12},{5,13},{6,14},{7,15},{8,0},{9,1},... | collective-permute-start | bytes 1327112 | tf_op jit(solution)/shard_map/ppermute | solution.py:545
  50.0 11.6 %collective-permute-start.10 = (bf16[144,1536]{1,0:T(8,128)(2,1)S(1)}, bf16[144,1536]{1,0:T(8,128)(2,1)S(1)}, u32[]{:S(2)}, u32[]{:S(2)}) collective-permute-start(bf16[144,1536]{1,0:T(8,128)(2,1)S(1)} %collective-permute-done.4.refs_3_), channel_id=1, source_target_pairs={{0,8},{1,9},{2,10},{3,11},{4,12},{5,13},{6,14},{7,15},{8,0},{9,1},... | collective-permute-start | bytes 1327112 | tf_op jit(solution)/shard_map/ppermute | solution.py:545
  51.2 0.7 copy-start.13
  51.9 7.1 %collective-permute-start.7 = (bf16[64,1536]{1,0:T(8,128)(2,1)}, bf16[64,1536]{1,0:T(8,128)(2,1)}, u32[]{:S(2)}, u32[]{:S(2)}) collective-permute-start(bf16[64,1536]{1,0:T(8,128)(2,1)} %slice.9), channel_id=1, source_target_pairs={{0,1},{1,0},{2,3},{3,2},{4,5},{5,4},{6,7},{7,6},{8,9},{9,8},{10,11... | collective-permute-start | bytes 589832 | tf_op jit(solution)/shard_map/ppermute | solution.py:545
  53.9 8.4 %collective-permute-start.12 = (bf16[80,1536]{1,0:T(8,128)(2,1)}, bf16[80,1536]{1,0:T(8,128)(2,1)S(1)}, u32[]{:S(2)}, u32[]{:S(2)}) collective-permute-start(bf16[80,1536]{1,0:T(8,128)(2,1)} %collective-permute-done.6.refs_5_), channel_id=1, source_target_pairs={{0,8},{1,9},{2,10},{3,11},{4,12},{5,13},{6,14},{7,15},{8,0},{9,1},... | collective-permute-start | bytes 737288 | tf_op jit(solution)/shard_map/ppermute | solution.py:545
  59.0 1.8 collective-permute-start.13
  60.8 0.8 copy-start.9
  61.6 0.8 copy-start.11
  62.3 0.7 copy-start.15
  63.1 1.1 copy-start.3
  64.2 1.0 copy-start.10
  65.2 1.1 copy-start.12
  66.3 1.0 copy-start.14
  67.3 0.9 copy-start.16
  68.2 36.1 %copy-start.8 = (bf16[8,768,100]{1,0,2:T(8,128)(2,1)S(1)}, bf16[8,768,100]{1,0,2:T(8,128)(2,1)}, u32[]{:S(2)}) copy-start(bf16[8,768,100]{1,0,2:T(8,128)(2,1)} %param.16) | copy-start | bytes 3686404
  99.2 2.1 %copy-start.17 = (bf16[768,3072]{1,0:T(8,128)(2,1)}, bf16[768,3072]{1,0:T(8,128)(2,1)S(1)}, u32[]{:S(2)}) copy-start(bf16[768,3072]{1,0:T(8,128)(2,1)S(1)} %get-tuple-element.43.front_hbm.front_ref) | copy-start | bytes 14155780
  101.2 1.7 copy-start.18
  103.0 0.7 copy-start.19
  103.7 0.7 copy-start.21
  104.3 0.9 copy-start.20
  105.3 0.9 copy-start.22
  121.5 12.3 %collective-permute-start.16 = (bf16[8,3968]{1,0:T(8,128)(2,1)S(1)}, bf16[8,3968]{1,0:T(8,128)(2,1)S(1)}, u32[]{:S(2)}, u32[]{:S(2)}) collective-permute-start(bf16[8,3968]{1,0:T(8,128)(2,1)S(1)} %get-tuple-element.44), channel_id=1, source_target_pairs={{0,6},{1,7},{2,4},{3,5},{4,2},{5,3},{6,0},{7,1},{8,14},{9,15},{10,... | collective-permute-start | bytes 190472 | tf_op jit(solution)/shard_map/ppermute | solution.py:545
  124.2 9.6 %collective-permute-start.15 = (bf16[8,3968]{1,0:T(8,128)(2,1)S(1)}, bf16[8,3968]{1,0:T(8,128)(2,1)S(1)}, u32[]{:S(2)}, u32[]{:S(2)}) collective-permute-start(bf16[8,3968]{1,0:T(8,128)(2,1)S(1)} %get-tuple-element.44), channel_id=1, source_target_pairs={{0,4},{1,5},{2,6},{3,7},{4,0},{5,1},{6,2},{7,3},{8,12},{9,13},{10,... | collective-permute-start | bytes 190472 | tf_op jit(solution)/shard_map/ppermute | solution.py:545
  124.2 9.6 %collective-permute-start.14 = (bf16[8,3968]{1,0:T(8,128)(2,1)S(1)}, bf16[8,3968]{1,0:T(8,128)(2,1)S(1)}, u32[]{:S(2)}, u32[]{:S(2)}) collective-permute-start(bf16[8,3968]{1,0:T(8,128)(2,1)S(1)} %get-tuple-element.44), channel_id=1, source_target_pairs={{0,2},{1,3},{2,0},{3,1},{4,6},{5,7},{6,4},{7,5},{8,10},{9,11},{10,... | collective-permute-start | bytes 190472 | tf_op jit(solution)/shard_map/ppermute | solution.py:545
  133.9 14.4 %collective-permute-start.17 = (bf16[32,3968]{1,0:T(8,128)(2,1)S(1)}, bf16[32,3968]{1,0:T(8,128)(2,1)S(1)}, u32[]{:S(2)}, u32[]{:S(2)}) collective-permute-start(bf16[32,3968]{1,0:T(8,128)(2,1)S(1)} %pad_maximum_fusion.3), channel_id=1, source_target_pairs={{0,1},{1,0},{2,3},{3,2},{4,5},{5,4},{6,7},{7,6},{8,9},{9,8},{10,11... | collective-permute-start | bytes 761864 | tf_op jit(solution)/shard_map/ppermute | solution.py:545
  148.3 16.6 %copy-start.23 = (bf16[64,3968]{1,0:T(8,128)(2,1)}, bf16[64,3968]{1,0:T(8,128)(2,1)S(1)}, u32[]{:S(2)}) copy-start(bf16[64,3968]{1,0:T(8,128)(2,1)S(1)} %pad_maximum_fusion.refs_0_) | copy-start | bytes 1523716
  148.3 16.6 %collective-permute-start.18 = (bf16[64,3968]{1,0:T(8,128)(2,1)S(1)}, bf16[64,3968]{1,0:T(8,128)(2,1)S(1)}, u32[]{:S(2)}, u32[]{:S(2)}) collective-permute-start(bf16[64,3968]{1,0:T(8,128)(2,1)S(1)} %pad_maximum_fusion.refs_0_), channel_id=1, source_target_pairs={{0,16},{1,17},{2,18},{3,19},{4,20},{5,21},{6,22},{7,23},{8,24},{9,... | collective-permute-start | bytes 1523720 | tf_op jit(solution)/shard_map/ppermute | solution.py:545
  164.9 2.7 %copy-start.28 = (bf16[64,3968]{1,0:T(8,128)(2,1)}, bf16[64,3968]{1,0:T(8,128)(2,1)S(1)}, u32[]{:S(2)}) copy-start(bf16[64,3968]{1,0:T(8,128)(2,1)S(1)} %collective-permute-done.18.refs_1_) | copy-start | bytes 1523716
  164.9 2.0 %collective-permute-start.19 = (bf16[64,3968]{1,0:T(8,128)(2,1)S(1)}, bf16[64,3968]{1,0:T(8,128)(2,1)S(1)}, u32[]{:S(2)}, u32[]{:S(2)}) collective-permute-start(bf16[64,3968]{1,0:T(8,128)(2,1)S(1)} %pad_maximum_fusion.refs_0_), channel_id=1, source_target_pairs={{0,8},{1,9},{2,10},{3,11},{4,12},{5,13},{6,14},{7,15},{8,0},{9,1},... | collective-permute-start | bytes 1523720 | tf_op jit(solution)/shard_map/ppermute | solution.py:545
  165.0 2.6 %collective-permute-start.20 = (bf16[64,3968]{1,0:T(8,128)(2,1)S(1)}, bf16[64,3968]{1,0:T(8,128)(2,1)S(1)}, u32[]{:S(2)}, u32[]{:S(2)}) collective-permute-start(bf16[64,3968]{1,0:T(8,128)(2,1)S(1)} %collective-permute-done.18.refs_1_), channel_id=1, source_target_pairs={{0,8},{1,9},{2,10},{3,11},{4,12},{5,13},{6,14},{7,15},{8,0},{9,1},... | collective-permute-start | bytes 1523720 | tf_op jit(solution)/shard_map/ppermute | solution.py:545
  166.9 0.8 copy-start.29
  167.7 0.8 copy-start.30
Sparse Core Ops, SparseCore 0:
  10.9 87.2 all-gather.2

commit v2 on v1

--- a/solution.py
+++ b/solution.py
@@ -137,13 +137,13 @@
         grid=(rows_n,),
         in_specs=[pl.BlockSpec(memory_space=pltpu.SMEM), row_spec, whole(prompts), whole(gain)],
         out_specs=[row_spec, row_spec],
-        out_shape=[jax.ShapeDtypeStruct(tokens.shape, BF16)] * 2,
+        out_shape=[pltpu.HBM(tokens.shape, BF16)] * 2,
         scratch_shapes=[
             pltpu.VMEM((ROW, D), F32),
             pltpu.VMEM((BLOCK, D), F32),
             pltpu.VMEM((len(LANE_BLOCKS), PROMPTS * TASKS, LANES), F32),
         ],
-        compiler_params=params(32),
+        compiler_params=params(20),
         cost_estimate=cost(0.1, 10),
         name="assemble",
     )(ids, tokens, prompts, gain)
@@ -161,10 +161,11 @@
 
 
 def attend_kernel(plan, normed_ref, resid_ref, gain_ref, *refs):
-    pieces, refs = refs[:-11], refs[-11:]
-    kv_ref, query_ref, probs_ref, middle_ref, class_ref, normed_two_ref, front_ref = refs[:7]
-    packed_buf, tail_buf, tail_context, sems = refs[7:]
+    pieces, refs = refs[:-12], refs[-12:]
+    query_ref, probs_ref, class_ref, kv_ref, middle_ref, normed_two_ref, front_out = refs[:7]
+    packed_buf, tail_buf, tail_context, front_ref, sems = refs[7:]
     img = pl.program_id(1)
+    at = pl.program_id(0) * IMGS_ROW + img
     lane = lax.broadcasted_iota(jnp.int32, (1, 128), 1)
     scale = HDIM ** (-0.5)
     halves = [
@@ -172,13 +173,20 @@
         jnp.where(lane < HDIM, 0.0, scale).astype(BF16),
     ]
 
-    @pl.when((pl.program_id(0) == 0) & (img == 0))
+    kept = pltpu.make_async_copy(front_ref, front_out, sems.at[0])
+
+    @pl.when(at == 0)
     def _():
         run_copies(plan(pieces, front_ref), sems)
+        kept.start()
+
+    @pl.when(at == pl.num_programs(0) * IMGS_ROW - 1)
+    def _():
+        kept.wait()
 
     @pl.when(img == 0)
     def _():
-        ends = [normed_ref[0, (at + 1) * BLOCK - 16 : (at + 1) * BLOCK, :] for at in range(IMGS_ROW)]
+        ends = [normed_ref[0, end - 16 : end, :] for end in range(BLOCK, ROW + 1, BLOCK)]
         tail_buf[...] = dot(jnp.concatenate(ends, axis=0), front_ref[:, : 3 * D]).astype(BF16)
         tail_at = lax.broadcasted_iota(jnp.int32, (1, 16 * IMGS_ROW), 1)
         tail_bias = jnp.where(tail_at % 16 >= 16 - TAIL, 0.0, MASKED_SCORE)
@@ -194,13 +202,13 @@
         cols = slice(part * D, (part + 1) * D)
         packed_buf[:, cols] = dot(tokens, front_ref[:, cols]).astype(BF16)
     kv_ref[0] = packed_buf[:, D:]
-    query_ref[0] = packed_buf[:16, :D]
+    query_ref[at] = packed_buf[:16, :D]
     key_at = lax.broadcasted_iota(jnp.int32, (1, BLOCK), 1)
     bias = jnp.where(key_at < IMG, 0.0, MASKED_SCORE)
     queries = packed_buf[0:1, :D] * head_rows_mask().astype(BF16) * np.float32(scale).astype(BF16)
     scores = dot_t(queries, packed_buf[:, D : 2 * D]) + bias
     probs = jnp.exp(scores - jnp.max(scores, axis=-1, keepdims=True))
-    probs_ref[0] = probs / jnp.sum(probs, axis=-1, keepdims=True)
+    probs_ref[at] = probs / jnp.sum(probs, axis=-1, keepdims=True)
     ones = jnp.ones((BLOCK, 128), BF16)
     is_tail = lax.broadcasted_iota(jnp.int32, (16, D), 0) >= 16 - TAIL
     context = []
@@ -213,7 +221,7 @@
     context = jnp.concatenate([context[: BLOCK - 16], last], axis=0).astype(BF16)
     middle = resid_ref[0].astype(F32) + dot(context, front_ref[:, 3 * D :])
     middle_ref[...] = middle
-    class_ref[0] = middle[:8]
+    class_ref[at] = middle[:8]
     normed_two_ref[...] = (unit_norm(middle)[0] * gain_ref[...]).astype(BF16)
 
 
@@ -227,20 +235,8 @@
 def attend(normed, resid, gain, pieces, plan, copies_n):
     rows_n = normed.shape[0]
     images = rows_n * IMGS_ROW
-    flat = lambda r, i: (r * IMGS_ROW + i, 0)
-    cube = lambda r, i: (r * IMGS_ROW + i, 0, 0)
-    front = jax.ShapeDtypeStruct((D, 4 * D), BF16)
-    outs = [
-        (images, BLOCK, 2 * D, BF16),
-        (images, 16, D, BF16),
-        (images, HEADS_PAD, BLOCK, F32),
-        (images * BLOCK, D, F32),
-        (images, 8, D, F32),
-        (images * BLOCK, D, BF16),
-    ]
-    specs = [
-        pl.BlockSpec((1, *o[1:-1]), cube) if len(o) == 4 else pl.BlockSpec((BLOCK, D), flat) for o in outs
-    ]
+    near = pl.BlockSpec(memory_space=pltpu.VMEM)
+    flat = pl.BlockSpec((BLOCK, D), lambda r, i: (r * IMGS_ROW + i, 0))
     return pl.pallas_call(
         functools.partial(attend_kernel, plan),
         grid=(rows_n, IMGS_ROW),
@@ -250,37 +246,48 @@
             whole(gain),
         ]
         + [pl.BlockSpec(memory_space=pltpu.HBM)] * len(pieces),
-        out_specs=[*specs, whole(front)],
-        out_shape=[*(jax.ShapeDtypeStruct(o[:-1], o[-1]) for o in outs), front],
+        out_specs=[near] * 3
+        + [
+            pl.BlockSpec((1, BLOCK, 2 * D), lambda r, i: (r * IMGS_ROW + i, 0, 0)),
+            flat,
+            flat,
+            pl.BlockSpec(memory_space=pltpu.HBM),
+        ],
+        out_shape=[
+            pltpu.VMEM((images, 16, D), BF16),
+            pltpu.VMEM((images, HEADS_PAD, BLOCK), F32),
+            pltpu.VMEM((images, 8, D), F32),
+            pltpu.HBM((images, BLOCK, 2 * D), BF16),
+            pltpu.HBM((rows_n * ROW, D), F32),
+            pltpu.HBM((rows_n * ROW, D), BF16),
+            pltpu.HBM((D, 4 * D), BF16),
+        ],
         scratch_shapes=[
             pltpu.VMEM((BLOCK, 3 * D), BF16),
             pltpu.VMEM((16 * IMGS_ROW, 3 * D), BF16),
             pltpu.VMEM((16 * IMGS_ROW, D), F32),
+            pltpu.VMEM((D, 4 * D), BF16),
             pltpu.SemaphoreType.DMA((copies_n,)),
         ],
-        compiler_params=params(40),
-        cost_estimate=cost(16, 30),
+        compiler_params=params(24),
+        cost_estimate=cost(8 * rows_n, 15 * rows_n),
         name="attend",
     )(far(normed), far(resid), gain, *pieces)
 
 
 def class_kernel(
-    plans, ids_ref, middle_ref, queries_ref, probs_ref, grads_ref, heads_ref,
-    attn_gain_ref, mlp_gain_ref, final_gain_ref, kv_hbm, front_hbm, *refs,
+    plans, ids_ref, grads_ref, heads_ref, mlp_gain_ref, final_gain_ref,
+    queries_ref, probs_ref, middles_ref, kv_hbm, front_hbm, *refs,
 ):
-    feed_refs = refs[:-16]
+    feed_refs = refs[:-17]
     (
         sent_ref, weights_ref, routes_ref, d_class_ref, d_middle_ref, up_ref, down_ref,
-        q_buf, c_buf, dq_buf, score_slots, prob_slots, front_ref, kv_ref, sems, feed_sems,
-    ) = refs[-16:]
-    images = middle_ref.shape[0]
-    up_plan, down_plan = plans
-    up_pairs, down_pairs = sum(up_plan(feed_refs, up_ref), []), sum(down_plan(feed_refs, down_ref), [])
-    feed_copies = start_copies(up_pairs + down_pairs, feed_sems)
-    front_copy = pltpu.make_async_copy(front_hbm, front_ref, sems.at[0])
-    front_copy.start()
-    kv_copy = pltpu.make_async_copy(kv_hbm, kv_ref, sems.at[1])
-    kv_copy.start()
+        q_buf, c_buf, dq_buf, score_slots, prob_slots, kv_ref, front_ref, sems, up_sems, down_sems,
+    ) = refs[-17:]
+    images = middles_ref.shape[0]
+    up_copies = start_copies(plans[0](feed_refs, up_ref), up_sems)
+    down_copies = start_copies(plans[1](feed_refs, down_ref), down_sems)
+    front_copy, kv_copy = start_copies([(front_hbm, front_ref), (kv_hbm, kv_ref)], sems)
     spread = (
         lax.broadcasted_iota(jnp.int32, (128, CLASSES * TASKS), 1) // TASKS
         == lax.broadcasted_iota(jnp.int32, (128, CLASSES * TASKS), 0)
@@ -289,13 +296,13 @@
     chosen = jnp.where(ids_ref[...] == task_at, dot(grads_ref[...], spread), 0.0).astype(BF16)
     d_final = dot(chosen, heads_ref[...])
     mlp_gain, final_gain = mlp_gain_ref[...], final_gain_ref[...]
-    middle = middle_ref[:, 0, :]
+    middle = middles_ref[:, 0, :]
     unit_mlp, inv_mlp = unit_norm(middle)
-    for copy in feed_copies[: len(up_pairs)]:
+    for copy in up_copies:
         copy.wait()
     pre = dot((unit_mlp * mlp_gain).astype(BF16), up_ref[...])
     activated = gelu(pre).astype(BF16)
-    for copy in feed_copies[len(up_pairs) :]:
+    for copy in down_copies:
         copy.wait()
     output = middle + dot(activated, down_ref[...])
     unit_fin, inv_fin = unit_norm(output)
@@ -348,37 +355,40 @@
 SENT = 5 * D + 128
 
 
-def class_path(ids, middle, queries, probs, grads, heads, gains, kv, front, feed_weights):
-    images = middle.shape[0]
-    operands = (ids, middle, queries, probs, grads, heads, *gains)
+def class_path(ids, grads, heads, gains, attended, feed_weights):
+    images = ids.shape[0]
+    *small, kv, front = attended
+    operands = (ids, grads, heads, *gains[1:], *small)
     feed_arrays, plans, copies_n = feed_weights
-    remote = (kv, front, *feed_arrays)
+    remote = (far(kv), far(front), *feed_arrays)
     outs = [
         jax.ShapeDtypeStruct((images, SENT), BF16),
         jax.ShapeDtypeStruct((images, 2 * HEADS_PAD, BLOCK), BF16),
         jax.ShapeDtypeStruct((images, 2 * HEADS_PAD, D), BF16),
         jax.ShapeDtypeStruct((images, D), F32),
         jax.ShapeDtypeStruct((images, D), F32),
+        pltpu.VMEM((D, FF), BF16),
+        pltpu.VMEM((FF, D), BF16),
     ]
-    near = [pltpu.VMEM((D, FF), BF16), pltpu.VMEM((FF, D), BF16)]
+    near = pl.BlockSpec(memory_space=pltpu.VMEM)
     return pl.pallas_call(
         functools.partial(class_kernel, plans),
-        in_specs=[pl.BlockSpec(memory_space=pltpu.VMEM)] * len(operands)
-        + [pl.BlockSpec(memory_space=pltpu.HBM)] * len(remote),
-        out_specs=[pl.BlockSpec(memory_space=pltpu.VMEM)] * (len(outs) + 2),
-        out_shape=outs + near,
+        in_specs=[near] * len(operands) + [pl.BlockSpec(memory_space=pltpu.HBM)] * len(remote),
+        out_specs=[near] * len(outs),
+        out_shape=outs,
         scratch_shapes=[
             pltpu.VMEM((images * HEADS_PAD, D), BF16),
             pltpu.VMEM((images * HEADS_PAD, D), BF16),
             pltpu.VMEM((images, D), F32),
             pltpu.VMEM((images * HEADS_PAD, 128), F32),
             pltpu.VMEM((images * HEADS_PAD, 128), F32),
+            pltpu.VMEM(kv.shape, BF16),
             pltpu.VMEM((D, 4 * D), BF16),
-            pltpu.VMEM((images, BLOCK, 2 * D), BF16),
             pltpu.SemaphoreType.DMA((2,)),
             pltpu.SemaphoreType.DMA((copies_n,)),
+            pltpu.SemaphoreType.DMA((copies_n,)),
         ],
-        compiler_params=params(40),
+        compiler_params=params(24),
         cost_estimate=cost(8, 30),
         name="class_path",
     )(*operands, *remote)
@@ -389,7 +399,7 @@
 
 def feed_kernel(normed_ref, middle_ref, up_ref, down_ref, *refs):
     out_ref, row_buf = refs[-2:]
-    img = pl.program_id(1)
+    img = pl.program_id(0)
     rows = normed_ref[...]
     total = middle_ref[...]
     for step in range(FF // FF_STEP):
@@ -407,22 +417,21 @@
         out_ref[0] = row_buf[...].astype(BF16)
 
 
-def feed(normed, middle, up_all, down_all, first, count, chain):
-    rows_n = normed.shape[0] // ROW
-    spec = pl.BlockSpec((BLOCK, D), lambda r, i: ((r + first) * IMGS_ROW + i, 0))
+def feed(normed, middle, up_all, down_all, row, rows_n, chain):
+    spec = pl.BlockSpec((BLOCK, D), lambda i: (row * IMGS_ROW + i, 0))
     chained = [] if chain is None else [chain]
     return pl.pallas_call(
         feed_kernel,
-        grid=(count, IMGS_ROW),
+        grid=(IMGS_ROW,),
         in_specs=[spec, spec]
         + [pl.BlockSpec(memory_space=pltpu.VMEM)] * 2
         + [pl.BlockSpec(memory_space=pltpu.HBM)] * len(chained),
-        out_specs=pl.BlockSpec((1, ROW, D), lambda r, i: (r + first, 0, 0)),
-        out_shape=jax.ShapeDtypeStruct((rows_n, ROW, D), BF16),
+        out_specs=pl.BlockSpec((1, ROW, D), lambda i: (row, 0, 0)),
+        out_shape=pltpu.HBM((rows_n, ROW, D), BF16),
         input_output_aliases={} if chain is None else {4: 0},
         scratch_shapes=[pltpu.VMEM((ROW, D), F32)],
-        compiler_params=params(24),
-        cost_estimate=cost(10 * count, 20),
+        compiler_params=params(18),
+        cost_estimate=cost(10, 20),
         name="feed",
     )(far(normed), far(middle), up_all, down_all, *chained)
 
@@ -454,15 +463,15 @@
         grid=(rows_n,),
         in_specs=[row_spec, img_spec(BLOCK), img_spec(D), whole(d_class), whole(d_middle), whole(gain)],
         out_specs=row_spec,
-        out_shape=jax.ShapeDtypeStruct(resid.shape, F32),
-        compiler_params=params(32),
+        out_shape=pltpu.HBM(resid.shape, F32),
+        compiler_params=params(20),
         cost_estimate=cost(0.5, 20),
         name="token_grads",
     )(far(resid), weights, routes, d_class, d_middle, gain)
 
 
 def sums_kernel(front_ref, prompts_ref, gain_ref, *refs):
-    parts, (prompt_out, head_out, all_buf, sum_buf, head_buf, prompt_buf, sems) = refs[:-7], refs[-7:]
+    parts, (prompt_out, head_out, all_buf, sum_buf, prompt_buf, sems) = refs[:-6], refs[-6:]
     rows = parts[0].shape[0]
     run_copies([(part, all_buf.at[pl.ds(at * rows, rows), :]) for at, part in enumerate(parts)], sems)
     scale = np.float32(HDIM ** (-0.5)).astype(BF16)
@@ -470,11 +479,9 @@
     by_class = all_buf[:, 5 * D :].T
     ids = by_class[CLASSES : CLASSES + 1].astype(F32)
     masks = [(ids == task).astype(F32).astype(BF16) for task in range(TASKS)]
-    finals = column(2)
-    for task in range(TASKS):
-        write_strided(head_buf, task, dot(by_class * masks[task], finals)[:CLASSES])
-    for block, lanes in enumerate(LANE_BLOCKS):
-        head_out[:, lanes] = head_buf[block]
+    of_task = (lax.broadcasted_iota(jnp.int32, (TASKS, 1), 0).astype(F32) == ids).astype(F32)
+    spread = by_class[:CLASSES].astype(F32)[:, None, :] * of_task[None]
+    head_out[...] = dot(spread.reshape(CLASSES * TASKS, -1).astype(BF16), column(2))
     lane = lax.broadcasted_iota(jnp.int32, (SLOTS, 128), 1)
     for side, (slots, lane_rows) in enumerate(((column(4), column(0) * scale), (column(1), column(3)))):
         slots = slots.T
@@ -506,17 +513,17 @@
     return pl.pallas_call(
         sums_kernel,
         grid=(1,),
-        in_specs=[whole(o) for o in operands] + [pl.BlockSpec(memory_space=pltpu.HBM)] * len(parts),
+        in_specs=[pl.BlockSpec(memory_space=pltpu.VMEM)] * len(operands)
+        + [pl.BlockSpec(memory_space=pl.ANY)] * len(parts),
         out_specs=[whole(o) for o in outs],
         out_shape=outs,
         scratch_shapes=[
             pltpu.VMEM((images, SENT), BF16),
             pltpu.VMEM((TASKS * SLOTS, 2 * D), BF16),
-            pltpu.VMEM((len(LANE_BLOCKS), CLASSES * TASKS, LANES), F32),
             pltpu.VMEM((len(LANE_BLOCKS), PROMPTS * TASKS, LANES), F32),
             pltpu.SemaphoreType.DMA((len(parts),)),
         ],
-        compiler_params=params(56),
+        compiler_params=params(28 if images <= 512 else 60),
         cost_estimate=cost(5, 15),
         name="sums",
     )(*operands, *parts)
@@ -548,42 +555,70 @@
 HALF_COLS = 2 * D
 
 
-def fetch_front(shard, beside):
+class Fetch:
+    def __init__(self, own, mine, both, cut):
+        self.own, self.mine, self.both, self.cut, self.half = own, mine, both, cut, mine.shape[0]
+
+    def along_z(self):
+        self.column = jnp.concatenate([exchange(self.mine, dz=r) for r in (1, 2, 3)], axis=0)
+
+    def beside(self):
+        self.own_x = exchange(self.both, dx=1)
+
+    def across(self):
+        self.over_x = exchange(self.column, dx=1)
+        self.over_y = exchange(self.column, dy=1)
+
+    def diagonal(self):
+        self.diag_y = exchange(self.over_x[: self.cut], dy=1)
+        self.diag_x = exchange(self.over_y[self.cut :], dx=1)
+
+    def pieces(self):
+        near = [self.own_x, self.column, self.over_x, self.over_y, self.diag_y, self.diag_x]
+        return self.own + near + [exchange(piece, dc=1) for piece in near]
+
+    def plan(self, refs, dst, put):
+        y, c, z, x = places()
+        half, cut = self.half, self.cut
+        pairs = []
+        for side in range(2):
+            own_x, column, over_x, over_y, diag_y, diag_x = refs[6 * side : 6 + 6 * side]
+
+            def add(ref, start, count, r, x_at, y_at, within=0):
+                return put(ref, start, count, dst, (z ^ r) * 2 + x_at, y_at, c ^ side, within)
+
+            for y_at in range(2):
+                pairs += add(own_x, y_at * half, half, 0, x ^ 1, y_at)
+            for r in (1, 2, 3):
+                start = (r - 1) * half
+                pairs += add(column, start, half, r, x, y)
+                pairs += add(over_x, start, half, r, x ^ 1, y)
+                pairs += add(over_y, start, half, r, x, y ^ 1)
+                first = min(max(cut - start, 0), half)
+                if first:
+                    pairs += add(diag_y, start, first, r, x ^ 1, y ^ 1)
+                if first < half:
+                    pairs += add(diag_x, start + first - cut, half - first, r, x ^ 1, y ^ 1, first)
+        return pairs
+
+
+def own_rows(ref, dst):
+    _, _, z, x = places()
+    count = ref.shape[0]
+    return [(ref, dst.at[pl.ds(pl.multiple_of((z * 2 + x) * count, count), count), :])]
+
+
+def put_front(ref, start, count, dst, place, y, c, within):
+    row = pl.multiple_of(place * 96 + y * 48 + within, 16)
+    cols = pl.ds(pl.multiple_of(c * HALF_COLS, 128), HALF_COLS)
+    return [(ref.at[pl.ds(start, count), :], dst.at[pl.ds(row, count), cols])]
+
+
+def front_bundle(shard):
     y, c, _, _ = places()
     mine = lax.dynamic_slice(shard, (y * 48, c * HALF_COLS), (48, HALF_COLS))
-    along_z = [exchange(mine, dz=r) for r in (1, 2, 3)]
-    half = lax.dynamic_slice(shard, (0, c * HALF_COLS), (96, HALF_COLS))
-    own_x = exchange(half, dx=1)
-    column, *beside = lax.optimization_barrier((jnp.concatenate(along_z, axis=0), *beside))
-    over_x, over_y = exchange(column, dx=1), exchange(column, dy=1)
-    diag_y, diag_x = exchange(over_x[:80], dy=1), exchange(over_y[80:], dx=1)
-    near = [own_x, column, over_x, over_y, diag_y, diag_x]
-    pieces = [shard] + near + [exchange(piece, dc=1) for piece in near]
-
-    def plan(refs, dst):
-        y, c, z, x = places()
-        pairs = [(refs[0], dst.at[pl.ds(pl.multiple_of((z * 2 + x) * 96, 96), 96), :])]
-        for side in range(2):
-            cols = pl.ds(pl.multiple_of((c ^ side) * HALF_COLS, 128), HALF_COLS)
-            own_x, column, over_x, over_y, diag_y, diag_x = refs[1 + 6 * side : 7 + 6 * side]
-
-            def add(ref, start, count, r, x_at, y_at, within=0):
-                row = ((z ^ r) * 2 + x_at) * 96 + y_at * 48 + within
-                pairs.append((ref.at[pl.ds(start, count), :], dst.at[pl.ds(pl.multiple_of(row, 16), count), cols]))
-
-            add(own_x, 0, 96, 0, x ^ 1, 0)
-            for r in (1, 2, 3):
-                start = (r - 1) * 48
-                add(column, start, 48, r, x, y)
-                add(over_x, start, 48, r, x ^ 1, y)
-                add(over_y, start, 48, r, x, y ^ 1)
-            add(diag_y, 0, 48, 1, x ^ 1, y ^ 1)
-            add(diag_y, 48, 32, 2, x ^ 1, y ^ 1)
-            add(diag_x, 0, 16, 2, x ^ 1, y ^ 1, 32)
-            add(diag_x, 16, 48, 3, x ^ 1, y ^ 1)
-        return pairs
-
-    return (pieces, plan, 29), beside
+    both = lax.dynamic_slice(shard, (0, c * HALF_COLS), (96, HALF_COLS))
+    return Fetch([shard], mine, both, 80)
 
 
 def fetch_rest(up_shard, down_shard):
@@ -591,20 +626,16 @@
     up_part = lax.dynamic_slice(up_shard, (0, d * D), (96, D))
     down_part = lax.dynamic_slice_in_dim(down_shard, d * 96, 96, 0)
     gathered = lax.all_gather(jnp.concatenate([up_part, down_part], axis=0), ("fsdp", "dp"), axis=0)
+    gathered = gathered.reshape(8, 4, 192, D)
 
     def up_plan(refs, dst):
-        return [
-            [(refs[0].at[4 * f + d, 0:96, :], dst.at[96 * f : 96 * f + 96, D * d : D * d + D]) for f in range(8)]
-            for d in range(4)
-        ]
+        dst = dst.reshape(8, 96, FF)
+        return [(refs[0].at[:, d, 0:96, :], dst.at[:, :, D * d : D * d + D]) for d in range(4)]
 
     def down_plan(refs, dst):
-        return [
-            [(refs[0].at[at, 96:192, :], dst.at[96 * at : 96 * at + 96]) for at in range(8 * d, 8 * d + 8)]
-            for d in range(4)
-        ]
-
-    return [gathered], (up_plan, down_plan), 64
+        return [(refs[0].at[:, :, 96:192, :], dst.reshape(8, 4, 96, D))]
+
+    return [far(gathered)], (up_plan, down_plan), 4
 
 
 def share_rows(rows, works):
@@ -630,31 +661,43 @@
     ids = task_ids.reshape(rows_n, IMGS_ROW)
     prompt_rows = prompts.transpose(1, 0, 2).reshape(PROMPTS * TASKS, D)
     resid, normed = assemble(ids, tokens.reshape(rows_n, ROW, D), prompt_rows, gains[0])
-    if tuned:
-        front_pieces, (resid, normed) = fetch_front(front_shard, (resid, normed))
-        feed_weights = fetch_rest(up_weight, down_weight)
-    else:
-        front_pieces = [gather_rows(front_shard, dp)], copy_whole(0), 1
-        plans = tuple(lambda refs, dst, at=at: [copy_whole(at)(refs, dst)] for at in range(2))
-        feed_weights = [gather_rows(w, dp) for w in (up_weight, down_weight)], plans, 2
+    token_rows = tokens.reshape(rows_n, ROW, D)
     ids_col = ids.reshape(images, 1)
     head_rows = head_weights.transpose(2, 0, 1).reshape(CLASSES * TASKS, D)
     grads = jnp.concatenate(
         [logit_grads.reshape(images, CLASSES), jnp.broadcast_to(ids_col, (images, 128 - CLASSES)).astype(BF16)], axis=1
     )
-    kv, queries, probs, middle, class_middle, normed_two, front = attend(normed, resid, gains[1], *front_pieces)
+    tie = lambda *values: lax.optimization_barrier(values)
+    if tuned:
+        feed_weights = fetch_rest(up_weight, down_weight)
+        front_in = front_bundle(front_shard)
+        front_in.along_z()
+        front_in.beside()
+        resid, normed = assemble(ids, token_rows, prompt_rows, gains[0])
+        front_in.column, normed = tie(front_in.column, normed)
+        front_in.across()
+        front_in.diagonal()
+        plan_front = lambda refs, dst: own_rows(refs[0], dst) + front_in.plan(refs[1:], dst, put_front)
+        fetched = [far(piece) for piece in front_in.pieces()], plan_front, 1 + 2 * (2 + 9 + 4)
+    else:
+        feed_weights = [gather_rows(w, dp) for w in (up_weight, down_weight)], (copy_whole(0), copy_whole(1)), 1
+        resid, normed = assemble(ids, token_rows, prompt_rows, gains[0])
+        fetched = [gather_rows(front_shard, dp)], copy_whole(0), 1
+    *attended, middle, normed_two, front = attend(normed, resid, gains[1], *fetched)
     sent, weights, routes, d_class, d_middle, up_all, down_all = class_path(
-        ids_col, class_middle, queries, probs, grads, head_rows, gains, kv, front, feed_weights
+        ids_col, grads, head_rows, gains, [*attended, front], feed_weights
     )
-    first_n = rows_n // 2
-
-    def grads_work(done):
-        return token_grads(resid, weights, routes, d_class, d_middle, gains[0]), None
-
-    def feed_work(start, count):
-        return lambda done: (done[0], feed(normed_two, middle, up_all, down_all, start, count, done[1]))
-
-    works = grads_work, feed_work(0, first_n), feed_work(first_n, rows_n - first_n)
+
+    def feed_rows(rows, chain):
+        for row in rows:
+            chain = feed(normed_two, middle, up_all, down_all, row, rows_n, chain)
+        return chain
+
+    works = (
+        lambda done: (token_grads(resid, weights, routes, d_class, d_middle, gains[0]), None),
+        lambda done: (done[0], feed_rows(range(rows_n // 2), None)),
+        lambda done: (done[0], feed_rows(range(rows_n // 2, rows_n), done[1])),
+    )
     if tuned:
         parts, (input_grads, activations) = share_rows(sent, works)
     else:

time: 186 us -> 175 us (0.941)
  local copies, waits for them, and re-layouts: 25.1 us -> 6 us
  waiting for transfers between devices: 27.4 us -> 37.3 us
    unnamed x64 -> x42, local copies, waits for them, and re-layouts: 22 us -> 3.6 us
    all_gather x1, waiting for transfers between devices: 0.01 us -> 7.82 us  [fetch_rest(): lax.all_gather(jnp.concatenate([up_part, down_part], axis=0), ('fsdp', 'd...]
    ppermute x21, waiting for transfers between devices: 27.4 us -> 29.4 us  [exchange(): return lax.ppermute(value, ('dp', 'fsdp'), pairs)]
  transfers between devices with their start and end apart: 22 -> 22, of which waited for: 8 -> 9; matrix products, arithmetic and copies ran while one was open for 2% -> 2% of each run, Pallas kernels for 38% -> 41%
where the time goes in v2:
time: 175 us
  Pallas kernels  95.3 us (54%)
  waiting for transfers between devices  37.3 us (21%)
  starting transfers between devices  20.5 us (12%)
  between operations  14.4 us (8%)
  local copies, waits for them, and re-layouts  6 us (3%)
    pallas_call x1, Pallas kernels, attend(): pl.pallas_call(functools.partial(attend_kernel, plan), grid=(rows_n, IMGS...  31 us
    ppermute x21, waiting for transfers between devices, exchange(): return lax.ppermute(value, ('dp', 'fsdp'), pairs)  29.4 us
    pallas_call x2, Pallas kernels, feed(): pl.pallas_call(feed_kernel, grid=(IMGS_ROW,), in_specs=[spec, spec] + [pl...  28.1 us
    ppermute x21, starting transfers between devices, exchange(): return lax.ppermute(value, ('dp', 'fsdp'), pairs)  20.5 us
    pallas_call x1, Pallas kernels, class_path(): pl.pallas_call(functools.partial(class_kernel, plans), in_specs=[near] *...  16.6 us
    pallas_call x1, Pallas kernels, token_grads(): pl.pallas_call(token_grads_kernel, grid=(rows_n,), in_specs=[row_spec, im...  7.86 us
    all_gather x1, waiting for transfers between devices, fetch_rest(): lax.all_gather(jnp.concatenate([up_part, down_part], axis=0), ('fsdp', 'd...  7.82 us
    pallas_call x1, Pallas kernels, sums(): pl.pallas_call(sums_kernel, grid=(1,), in_specs=[pl.BlockSpec(memory_spac...  7.15 us
  transfers between devices with their start and end apart: 22, of which 9 were waited for; matrix products, arithmetic and copies ran while one was open for 2% of the time, Pallas kernels for 41%

profile of v2, /device:TPU:0, one launch (start us, length us, event | category | flops | bytes accessed | tf_op | source)
XLA Modules:
  0.0 175.1 jit_solution(10233470062779531717)
XLA Ops:
  7.2 0.0 all-gather.3.cloned.1.call-start
  7.2 1.2 constant_dynamic-slice_fusion
  8.4 0.8 pad_maximum_fusion.2
  9.2 0.0 all-gather.3.cloned.1.call-update
  9.2 1.0 constant_dynamic-update-slice_fusion.1
  10.3 0.9 constant_dynamic-update-slice_fusion.refs_0_
  11.2 0.0 copy-start.5
  11.2 0.0 copy-start.10
  11.3 0.0 copy-start.11
  11.3 0.0 copy-start.12
  11.3 5.1 %collective-permute-start.2 = (bf16[48,1536]{1,0:T(8,128)(2,1)S(1)}, bf16[48,1536]{1,0:T(8,128)(2,1)S(1)}, u32[]{:S(2)}, u32[]{:S(2)}) collective-permute-start(bf16[48,1536]{1,0:T(8,128)(2,1)S(1)} %dynamic_slice.12), channel_id=1, source_target_pairs={{0,6},{1,7},{2,4},{3,5},{4,2},{5,3},{6,0},{7,1},{8,14},{9,15},{10,... | collective-permute-start | bytes 442376 | tf_op jit(solution)/shard_map/ppermute | solution.py:552
  16.4 0.6 collective-permute-start
  17.1 1.7 collective-permute-start.3
  18.8 0.0 copy-start.1
  18.8 1.1 copy-done.1
  19.9 4.7 %assemble.1 = (bf16[2,1024,768]{2,1,0:T(8,128)(2,1)}, bf16[2,1024,768]{2,1,0:T(8,128)(2,1)}) custom-call(s32[2,4]{1,0:T(2,128)S(1)} %bitcast.25, bf16[2,1024,768]{2,1,0:T(8,128)(2,1)S(1)} %bitcast.22, bf16[400,768]{1,0:T(8,128)(2,1)S(1)} %bitcast.23, f32[1,768]{1,0:T(1,128)S(1)} %reshape.56.gain_ref), custom_call_target="tpu_custom_call" | custom-call | flops 100000000 | bytes 10000000 | tf_op jit(solution)/shard_map/assemble/pallas_call | solution.py:135
  24.5 0.0 collective-permute-done.2
  24.5 8.8 %collective-permute-done.1 = bf16[48,1536]{1,0:T(8,128)(2,1)S(1)} collective-permute-done((bf16[48,1536]{1,0:T(8,128)(2,1)S(1)}, bf16[48,1536]{1,0:T(8,128)(2,1)S(1)}, u32[]{:S(2)}, u32[]{:S(2)}) %collective-permute-start.1) | collective-permute-done | bytes 147488 | tf_op jit(solution)/shard_map/ppermute | solution.py:552
  33.4 0.0 collective-permute-done
  33.4 0.0 copy-start.6
  33.4 1.9 %collective-permute-start.4 = (bf16[144,1536]{1,0:T(8,128)(2,1)S(1)}, bf16[144,1536]{1,0:T(8,128)(2,1)S(1)}, u32[]{:S(2)}, u32[]{:S(2)}) collective-permute-start(bf16[144,1536]{1,0:T(8,128)(2,1)S(1)} %pad_maximum_fusion.1.refs_2_), channel_id=1, source_target_pairs={{0,1},{1,0},{2,3},{3,2},{4,5},{5,4},{6,7},{7,6},{8,9},{9,8},{10,11... | collective-permute-start | bytes 1327112 | tf_op jit(solution)/shard_map/ppermute | solution.py:552
  35.4 1.7 collective-permute-start.5
  37.1 0.0 collective-permute-done.3.refs_1_
  37.1 0.0 collective-permute-start.8
  37.1 6.8 %collective-permute-done.4.refs_3_ = bf16[144,1536]{1,0:T(8,128)(2,1)S(1)} collective-permute-done((bf16[144,1536]{1,0:T(8,128)(2,1)S(1)}, bf16[144,1536]{1,0:T(8,128)(2,1)S(1)}, u32[]{:S(2)}, u32[]{:S(2)}) %collective-permute-start.4) | collective-permute-done | bytes 442400 | tf_op jit(solution)/shard_map/ppermute | solution.py:552
  44.0 1.7 collective-permute-start.6
  45.7 4.5 %collective-permute-done.5.refs_4_ = bf16[144,1536]{1,0:T(8,128)(2,1)S(1)} collective-permute-done((bf16[144,1536]{1,0:T(8,128)(2,1)S(1)}, bf16[144,1536]{1,0:T(8,128)(2,1)S(1)}, u32[]{:S(2)}, u32[]{:S(2)}) %collective-permute-start.5) | collective-permute-done | bytes 442400 | tf_op jit(solution)/shard_map/ppermute | solution.py:552
  50.1 0.5 collective-permute-start.10
  50.7 0.0 collective-permute-done.8.refs_7_
  50.7 0.1 collective-permute-start.7
  50.8 3.2 %collective-permute-done.6.refs_5_ = bf16[80,1536]{1,0:T(8,128)(2,1)} collective-permute-done((bf16[80,1536]{1,0:T(8,128)(2,1)S(1)}, bf16[80,1536]{1,0:T(8,128)(2,1)}, u32[]{:S(2)}, u32[]{:S(2)}) %collective-permute-start.6) | collective-permute-done | bytes 245792 | tf_op jit(solution)/shard_map/ppermute | solution.py:552
  54.0 0.5 broadcast.7
  54.5 0.7 reduce.5
  55.2 2.5 %collective-permute-done.7.refs_6_ = bf16[64,1536]{1,0:T(8,128)(2,1)} collective-permute-done((bf16[64,1536]{1,0:T(8,128)(2,1)S(1)}, bf16[64,1536]{1,0:T(8,128)(2,1)}, u32[]{:S(2)}, u32[]{:S(2)}) %collective-permute-start.7) | collective-permute-done | bytes 196640 | tf_op jit(solution)/shard_map/ppermute | solution.py:552
  57.7 0.0 collective-permute-start.13
  57.7 0.1 convert_element_type.8
  57.8 0.1 reshape_reshape.4.ids_ref
  57.9 0.1 broadcast_in_dim.2
  57.9 0.1 pad_maximum_fusion.4.grads_ref
  58.0 0.0 collective-permute-done.9.refs_8_
  58.0 1.4 collective-permute-done.13.refs_12_
  59.4 0.0 collective-permute-done.11.refs_10_
  59.5 0.0 collective-permute-done.10.refs_9_
  59.5 0.7 copy-done.14
  60.2 0.2 copy-done.15
  60.4 0.0 copy-start.4
  60.4 31.0 %attend.1 = (bf16[8,16,768]{2,1,0:T(8,128)(2,1)S(1)}, f32[8,16,256]{2,1,0:T(8,128)S(1)}, f32[8,8,768]{2,1,0:T(8,128)S(1)}, bf16[8,256,1536]{2,1,0:T(8,128)(2,1)}...) custom-call(bf16[2,1024,768]{2,1,0:T(8,128)(2,1)} %get-tuple-element.34.normed_ref, ...), custom_call_target="tpu_custom_call" | custom-call | flops 16000000000 | bytes 30000000 | tf_op jit(solution)/shard_map/attend/pallas_call | solution.py:240
  91.4 7.8 %all-gather.3.cloned.1.call-done = bf16[6144,768]{1,0:T(8,128)(2,1)} async-done(((bf16[192,768]{1,0:T(8,128)(2,1)}), bf16[6144,768]{1,0:T(8,128)(2,1)}) %all-gather.3.cloned.1.call-update) | async-done | bytes 9437200 | tf_op jit(solution)/shard_map/all_gather | solution.py:628
  99.2 16.6 %class_path.1 = (bf16[8,3968]{1,0:T(8,128)(2,1)S(1)}, bf16[8,32,256]{2,1,0:T(8,128)(2,1)S(1)}, bf16[8,32,768]{2,1,0:T(8,128)(2,1)S(1)}, f32[8,768]{1,0:T(8,128)S...) custom-call(s32[8,1]{1,0:T(8,128)S(1)} %reshape_reshape.4.ids_ref, ...), custom_call_target="tpu_custom_call" | custom-call | flops 8000000000 | bytes 30000000 | tf_op jit(solution)/shard_map/class_path/pallas_call | solution.py:374
  115.9 2.0 %collective-permute-start.16 = (bf16[8,3968]{1,0:T(8,128)(2,1)S(1)}, bf16[8,3968]{1,0:T(8,128)(2,1)S(1)}, u32[]{:S(2)}, u32[]{:S(2)}) collective-permute-start(bf16[8,3968]{1,0:T(8,128)(2,1)S(1)} %get-tuple-element.42), channel_id=1, source_target_pairs={{0,6},{1,7},{2,4},{3,5},{4,2},{5,3},{6,0},{7,1},{8,14},{9,15},{10,... | collective-permute-start | bytes 190472 | tf_op jit(solution)/shard_map/ppermute | solution.py:552
  117.9 0.9 collective-permute-start.15
  118.8 1.5 collective-permute-start.14
  120.3 7.9 %token_grads.1 = f32[2,1024,768]{2,1,0:T(8,128)} custom-call(bf16[2,1024,768]{2,1,0:T(8,128)(2,1)} %get-tuple-element.35.resid_ref, bf16[8,32,256]{2,1,0:T(8,128)(2,1)S(1)} %get-tuple-element.43.weights_ref, bf16[8,32,768]{2,1,0:T(8,128)(2,1)S(1)} %get-tuple-element.44.routes_ref, f32[8,768]{1,0:T(8,128)S(1)} %get-tuple-element.45.d_class_ref, ...), custom_call_target="tpu_custom_call" | custom-call | flops 500000000 | bytes 20000000 | tf_op jit(solution)/shard_map/token_grads/pallas_call | solution.py:461
  128.2 0.0 collective-permute-done.16
  128.2 0.0 collective-permute-done.15
  128.2 1.5 collective-permute-start.17
  129.7 13.9 %feed.2.refs_0_ = bf16[2,1024,768]{2,1,0:T(8,128)(2,1)} custom-call(bf16[2048,768]{1,0:T(8,128)(2,1)} %get-tuple-element.49.normed_ref, f32[2048,768]{1,0:T(8,128)} %get-tuple-element.50.middle_ref, bf16[768,3072]{1,0:T(8,128)(2,1)S(1)} %get-tuple-element.51.up_ref, bf16[3072,768]{1,0:T(8,128)(2,1)S(1)} %get-tuple-element.52.down_ref), custom_call_target="tpu_custom_call" | custom-call | flops 10000000000 | bytes 20000000 | tf_op jit(solution)/shard_map/feed/pallas_call | solution.py:423
  143.6 0.0 copy-start.2
  143.6 0.7 collective-permute-start.18
  144.3 14.2 %feed.3 = bf16[2,1024,768]{2,1,0:T(8,128)(2,1)} custom-call(bf16[2048,768]{1,0:T(8,128)(2,1)} %get-tuple-element.49.normed_ref, f32[2048,768]{1,0:T(8,128)} %get-tuple-element.50.middle_ref, bf16[768,3072]{1,0:T(8,128)(2,1)S(1)} %get-tuple-element.51.up_ref, bf16[3072,768]{1,0:T(8,128)(2,1)S(1)} %get-tuple-element.52.down_ref, ...), custom_call_target="tpu_custom_call", output_to_operand_aliasing={{}: (4, {})} | custom-call | flops 10000000000 | bytes 20000000 | tf_op jit(solution)/shard_map/feed/pallas_call | solution.py:423
  158.5 0.5 collective-permute-start.20
  159.0 1.4 collective-permute-done.19.refs_2_
  160.4 0.7 collective-permute-done.20.refs_3_
  161.1 7.1 %sums.1 = (f32[400,768]{1,0:T(8,128)}, f32[800,768]{1,0:T(8,128)}) custom-call(bf16[768,3072]{1,0:T(8,128)(2,1)S(1)} %bitcast.28, bf16[400,768]{1,0:T(8,128)(2,1)S(1)} %bitcast.24, f32[1,768]{1,0:T(1,128)S(1)} %reshape.56.gain_ref, bf16[64,3968]{1,0:T(8,128)(2,1)S(1)} %pad_maximum_fusion.refs_0_, bf16[64,3968]{1,0:T(8,128)(2,1)S(1)} %collective-permute-done.18.refs_1_, ...), custom_call_target="tpu_custom_call" | custom-call | flops 5000000000 | bytes 15000000 | tf_op jit(solution)/shard_map/sums/pallas_call | solution.py:513
  (50 shorter events, 0.3 us)
Async XLA Ops:
  7.2 11.6 %copy-start.9 = (f32[768]{0:T(1024)S(1)}, f32[768]{0:T(1024)}, u32[]{:S(2)}) copy-start(f32[768]{0:T(1024)} %param.21) | copy-start | bytes 9220
  7.2 11.6 %copy-start.3 = (s32[2,1,4]{2,1,0:T(1,128)S(1)}, s32[2,1,4]{2,1,0:T(1,128)}, u32[]{:S(2)}) copy-start(s32[2,1,4]{2,1,0:T(1,128)} %param.13) | copy-start | bytes 100
  7.2 11.6 %copy-start = (bf16[2,1,1024,768]{3,2,1,0:T(8,128)(2,1)S(1)}, bf16[2,1,1024,768]{3,2,1,0:T(8,128)(2,1)}, u32[]{:S(2)}) copy-start(bf16[2,1,1024,768]{3,2,1,0:T(8,128)(2,1)} %param.12) | copy-start | bytes 9437188
  7.2 92.0 %all-gather.3.cloned.1.call-start = ((), (), s32[]{:S(2)}) async-start(), calls=%async_computation | async-start | bytes 9732096 | tf_op jit(solution)/shard_map/all_gather | solution.py:628
  11.2 7.6 %copy-start.5 = (bf16[96,3072]{1,0:T(8,128)(2,1)}, bf16[96,3072]{1,0:T(8,128)(2,1)S(1)}, u32[]{:S(2)}) copy-start(bf16[96,3072]{1,0:T(8,128)(2,1)S(1)} %constant_dynamic-update-slice_fusion.refs_0_) | copy-start | bytes 1769476
  11.2 46.5 %copy-start.10 = (f32[768]{0:T(1024)S(1)}, f32[768]{0:T(1024)}, u32[]{:S(2)}) copy-start(f32[768]{0:T(1024)} %param.22) | copy-start | bytes 9220
  11.3 46.6 %copy-start.11 = (f32[768]{0:T(1024)S(1)}, f32[768]{0:T(1024)}, u32[]{:S(2)}) copy-start(f32[768]{0:T(1024)} %param.23) | copy-start | bytes 9220
  11.3 46.7 %copy-start.12 = (bf16[2,1,4,100]{3,2,1,0:T(4,128)(2,1)S(1)}, bf16[2,1,4,100]{3,2,1,0:T(4,128)(2,1)}, u32[]{:S(2)}) copy-start(bf16[2,1,4,100]{3,2,1,0:T(4,128)(2,1)} %param.14) | copy-start | bytes 4804
  11.3 13.3 %collective-permute-start.2 = (bf16[48,1536]{1,0:T(8,128)(2,1)S(1)}, bf16[48,1536]{1,0:T(8,128)(2,1)S(1)}, u32[]{:S(2)}, u32[]{:S(2)}) collective-permute-start(bf16[48,1536]{1,0:T(8,128)(2,1)S(1)} %dynamic_slice.12), channel_id=1, source_target_pairs={{0,6},{1,7},{2,4},{3,5},{4,2},{5,3},{6,0},{7,1},{8,14},{9,15},{10,... | collective-permute-start | bytes 442376 | tf_op jit(solution)/shard_map/ppermute | solution.py:552
  16.4 17.0 %collective-permute-start.1 = (bf16[48,1536]{1,0:T(8,128)(2,1)S(1)}, bf16[48,1536]{1,0:T(8,128)(2,1)S(1)}, u32[]{:S(2)}, u32[]{:S(2)}) collective-permute-start(bf16[48,1536]{1,0:T(8,128)(2,1)S(1)} %dynamic_slice.12), channel_id=1, source_target_pairs={{0,4},{1,5},{2,6},{3,7},{4,0},{5,1},{6,2},{7,3},{8,12},{9,13},{10,... | collective-permute-start | bytes 442376 | tf_op jit(solution)/shard_map/ppermute | solution.py:552
  16.4 17.0 %collective-permute-start = (bf16[48,1536]{1,0:T(8,128)(2,1)S(1)}, bf16[48,1536]{1,0:T(8,128)(2,1)S(1)}, u32[]{:S(2)}, u32[]{:S(2)}) collective-permute-start(bf16[48,1536]{1,0:T(8,128)(2,1)S(1)} %dynamic_slice.12), channel_id=1, source_target_pairs={{0,2},{1,3},{2,0},{3,1},{4,6},{5,7},{6,4},{7,5},{8,10},{9,11},{10,... | collective-permute-start | bytes 442376 | tf_op jit(solution)/shard_map/ppermute | solution.py:552
  17.1 20.0 %collective-permute-start.3 = (bf16[96,1536]{1,0:T(8,128)(2,1)S(1)}, bf16[96,1536]{1,0:T(8,128)(2,1)S(1)}, u32[]{:S(2)}, u32[]{:S(2)}) collective-permute-start(bf16[96,1536]{1,0:T(8,128)(2,1)S(1)} %constant_dynamic-slice_fusion.2), channel_id=1, source_target_pairs={{0,1},{1,0},{2,3},{3,2},{4,5},{5,4},{6,7},{7,6},{8,9},{9,8},{10,11... | collective-permute-start | bytes 884744 | tf_op jit(solution)/shard_map/ppermute | solution.py:552
  18.8 1.1 copy-start.1
  33.4 27.0 %copy-start.6 = (bf16[144,1536]{1,0:T(8,128)(2,1)}, bf16[144,1536]{1,0:T(8,128)(2,1)S(1)}, u32[]{:S(2)}) copy-start(bf16[144,1536]{1,0:T(8,128)(2,1)S(1)} %pad_maximum_fusion.1.refs_2_) | copy-start | bytes 1327108
  33.4 10.5 %collective-permute-start.4 = (bf16[144,1536]{1,0:T(8,128)(2,1)S(1)}, bf16[144,1536]{1,0:T(8,128)(2,1)S(1)}, u32[]{:S(2)}, u32[]{:S(2)}) collective-permute-start(bf16[144,1536]{1,0:T(8,128)(2,1)S(1)} %pad_maximum_fusion.1.refs_2_), channel_id=1, source_target_pairs={{0,1},{1,0},{2,3},{3,2},{4,5},{5,4},{6,7},{7,6},{8,9},{9,8},{10,11... | collective-permute-start | bytes 1327112 | tf_op jit(solution)/shard_map/ppermute | solution.py:552
  35.4 14.8 %collective-permute-start.5 = (bf16[144,1536]{1,0:T(8,128)(2,1)S(1)}, bf16[144,1536]{1,0:T(8,128)(2,1)S(1)}, u32[]{:S(2)}, u32[]{:S(2)}) collective-permute-start(bf16[144,1536]{1,0:T(8,128)(2,1)S(1)} %pad_maximum_fusion.1.refs_2_), channel_id=1, source_target_pairs={{0,16},{1,17},{2,18},{3,19},{4,20},{5,21},{6,22},{7,23},{8,24},{9,... | collective-permute-start | bytes 1327112 | tf_op jit(solution)/shard_map/ppermute | solution.py:552
  37.1 23.3 %copy-start.16 = (bf16[96,1536]{1,0:T(8,128)(2,1)}, bf16[96,1536]{1,0:T(8,128)(2,1)S(1)}, u32[]{:S(2)}) copy-start(bf16[96,1536]{1,0:T(8,128)(2,1)S(1)} %collective-permute-done.3.refs_1_) | copy-start | bytes 884740
  37.1 13.6 %collective-permute-start.8 = (bf16[96,1536]{1,0:T(8,128)(2,1)S(1)}, bf16[96,1536]{1,0:T(8,128)(2,1)S(1)}, u32[]{:S(2)}, u32[]{:S(2)}) collective-permute-start(bf16[96,1536]{1,0:T(8,128)(2,1)S(1)} %collective-permute-done.3.refs_1_), channel_id=1, source_target_pairs={{0,8},{1,9},{2,10},{3,11},{4,12},{5,13},{6,14},{7,15},{8,0},{9,1},... | collective-permute-start | bytes 884744 | tf_op jit(solution)/shard_map/ppermute | solution.py:552
  44.0 16.4 %copy-start.7 = (bf16[144,1536]{1,0:T(8,128)(2,1)}, bf16[144,1536]{1,0:T(8,128)(2,1)S(1)}, u32[]{:S(2)}) copy-start(bf16[144,1536]{1,0:T(8,128)(2,1)S(1)} %collective-permute-done.4.refs_3_) | copy-start | bytes 1327108
  44.0 10.0 %collective-permute-start.6 = (bf16[80,1536]{1,0:T(8,128)(2,1)S(1)}, bf16[80,1536]{1,0:T(8,128)(2,1)}, u32[]{:S(2)}, u32[]{:S(2)}) collective-permute-start(bf16[80,1536]{1,0:T(8,128)(2,1)S(1)} %slice.8), channel_id=1, source_target_pairs={{0,16},{1,17},{2,18},{3,19},{4,20},{5,21},{6,22},{7,23},{8,24},{9,... | collective-permute-start | bytes 737288 | tf_op jit(solution)/shard_map/ppermute | solution.py:552
  45.7 12.4 %collective-permute-start.9 = (bf16[144,1536]{1,0:T(8,128)(2,1)S(1)}, bf16[144,1536]{1,0:T(8,128)(2,1)S(1)}, u32[]{:S(2)}, u32[]{:S(2)}) collective-permute-start(bf16[144,1536]{1,0:T(8,128)(2,1)S(1)} %pad_maximum_fusion.1.refs_2_), channel_id=1, source_target_pairs={{0,8},{1,9},{2,10},{3,11},{4,12},{5,13},{6,14},{7,15},{8,0},{9,1},... | collective-permute-start | bytes 1327112 | tf_op jit(solution)/shard_map/ppermute | solution.py:552
  50.1 10.3 %copy-start.8 = (bf16[144,1536]{1,0:T(8,128)(2,1)}, bf16[144,1536]{1,0:T(8,128)(2,1)S(1)}, u32[]{:S(2)}) copy-start(bf16[144,1536]{1,0:T(8,128)(2,1)S(1)} %collective-permute-done.5.refs_4_) | copy-start | bytes 1327108
  50.1 9.3 %collective-permute-start.11 = (bf16[144,1536]{1,0:T(8,128)(2,1)S(1)}, bf16[144,1536]{1,0:T(8,128)(2,1)S(1)}, u32[]{:S(2)}, u32[]{:S(2)}) collective-permute-start(bf16[144,1536]{1,0:T(8,128)(2,1)S(1)} %collective-permute-done.5.refs_4_), channel_id=1, source_target_pairs={{0,8},{1,9},{2,10},{3,11},{4,12},{5,13},{6,14},{7,15},{8,0},{9,1},... | collective-permute-start | bytes 1327112 | tf_op jit(solution)/shard_map/ppermute | solution.py:552
  50.1 9.3 %collective-permute-start.10 = (bf16[144,1536]{1,0:T(8,128)(2,1)S(1)}, bf16[144,1536]{1,0:T(8,128)(2,1)S(1)}, u32[]{:S(2)}, u32[]{:S(2)}) collective-permute-start(bf16[144,1536]{1,0:T(8,128)(2,1)S(1)} %collective-permute-done.4.refs_3_), channel_id=1, source_target_pairs={{0,8},{1,9},{2,10},{3,11},{4,12},{5,13},{6,14},{7,15},{8,0},{9,1},... | collective-permute-start | bytes 1327112 | tf_op jit(solution)/shard_map/ppermute | solution.py:552
  50.7 8.8 %copy-start.17 = (bf16[96,1536]{1,0:T(8,128)(2,1)}, bf16[96,1536]{1,0:T(8,128)(2,1)S(1)}, u32[]{:S(2)}) copy-start(bf16[96,1536]{1,0:T(8,128)(2,1)S(1)} %collective-permute-done.8.refs_7_) | copy-start | bytes 884740
  50.7 7.0 %collective-permute-start.7 = (bf16[64,1536]{1,0:T(8,128)(2,1)S(1)}, bf16[64,1536]{1,0:T(8,128)(2,1)}, u32[]{:S(2)}, u32[]{:S(2)}) collective-permute-start(bf16[64,1536]{1,0:T(8,128)(2,1)S(1)} %slice.9), channel_id=1, source_target_pairs={{0,1},{1,0},{2,3},{3,2},{4,5},{5,4},{6,7},{7,6},{8,9},{9,8},{10,11... | collective-permute-start | bytes 589832 | tf_op jit(solution)/shard_map/ppermute | solution.py:552
  54.0 5.5 %collective-permute-start.12 = (bf16[80,1536]{1,0:T(8,128)(2,1)}, bf16[80,1536]{1,0:T(8,128)(2,1)}, u32[]{:S(2)}, u32[]{:S(2)}) collective-permute-start(bf16[80,1536]{1,0:T(8,128)(2,1)} %collective-permute-done.6.refs_5_), channel_id=1, source_target_pairs={{0,8},{1,9},{2,10},{3,11},{4,12},{5,13},{6,14},{7,15},{8,0},{9,1},... | collective-permute-start | bytes 737288 | tf_op jit(solution)/shard_map/ppermute | solution.py:552
  57.7 1.8 %collective-permute-start.13 = (bf16[64,1536]{1,0:T(8,128)(2,1)}, bf16[64,1536]{1,0:T(8,128)(2,1)}, u32[]{:S(2)}, u32[]{:S(2)}) collective-permute-start(bf16[64,1536]{1,0:T(8,128)(2,1)} %collective-permute-done.7.refs_6_), channel_id=1, source_target_pairs={{0,8},{1,9},{2,10},{3,11},{4,12},{5,13},{6,14},{7,15},{8,0},{9,1},... | collective-permute-start | bytes 589832 | tf_op jit(solution)/shard_map/ppermute | solution.py:552
  58.0 1.5 copy-start.13
  59.5 0.8 copy-start.14
  59.5 0.9 copy-start.15
  60.4 38.8 %copy-start.4 = (bf16[8,768,100]{1,0,2:T(8,128)(2,1)S(1)}, bf16[8,768,100]{1,0,2:T(8,128)(2,1)}, u32[]{:S(2)}) copy-start(bf16[8,768,100]{1,0,2:T(8,128)(2,1)} %param.16) | copy-start | bytes 3686404
  115.9 12.3 %collective-permute-start.16 = (bf16[8,3968]{1,0:T(8,128)(2,1)S(1)}, bf16[8,3968]{1,0:T(8,128)(2,1)S(1)}, u32[]{:S(2)}, u32[]{:S(2)}) collective-permute-start(bf16[8,3968]{1,0:T(8,128)(2,1)S(1)} %get-tuple-element.42), channel_id=1, source_target_pairs={{0,6},{1,7},{2,4},{3,5},{4,2},{5,3},{6,0},{7,1},{8,14},{9,15},{10,... | collective-permute-start | bytes 190472 | tf_op jit(solution)/shard_map/ppermute | solution.py:552
  117.9 10.3 %collective-permute-start.15 = (bf16[8,3968]{1,0:T(8,128)(2,1)S(1)}, bf16[8,3968]{1,0:T(8,128)(2,1)S(1)}, u32[]{:S(2)}, u32[]{:S(2)}) collective-permute-start(bf16[8,3968]{1,0:T(8,128)(2,1)S(1)} %get-tuple-element.42), channel_id=1, source_target_pairs={{0,4},{1,5},{2,6},{3,7},{4,0},{5,1},{6,2},{7,3},{8,12},{9,13},{10,... | collective-permute-start | bytes 190472 | tf_op jit(solution)/shard_map/ppermute | solution.py:552
  118.8 9.4 %collective-permute-start.14 = (bf16[8,3968]{1,0:T(8,128)(2,1)S(1)}, bf16[8,3968]{1,0:T(8,128)(2,1)S(1)}, u32[]{:S(2)}, u32[]{:S(2)}) collective-permute-start(bf16[8,3968]{1,0:T(8,128)(2,1)S(1)} %get-tuple-element.42), channel_id=1, source_target_pairs={{0,2},{1,3},{2,0},{3,1},{4,6},{5,7},{6,4},{7,5},{8,10},{9,11},{10,... | collective-permute-start | bytes 190472 | tf_op jit(solution)/shard_map/ppermute | solution.py:552
  128.2 15.3 %collective-permute-start.17 = (bf16[32,3968]{1,0:T(8,128)(2,1)S(1)}, bf16[32,3968]{1,0:T(8,128)(2,1)S(1)}, u32[]{:S(2)}, u32[]{:S(2)}) collective-permute-start(bf16[32,3968]{1,0:T(8,128)(2,1)S(1)} %pad_maximum_fusion.3), channel_id=1, source_target_pairs={{0,1},{1,0},{2,3},{3,2},{4,5},{5,4},{6,7},{7,6},{8,9},{9,8},{10,11... | collective-permute-start | bytes 761864 | tf_op jit(solution)/shard_map/ppermute | solution.py:552
  143.5 17.6 %slice-start = ((s8[4718592]{0:T(1024)(128)(4,1)}), s8[4194304]{0:T(1024)(128)(4,1)S(1)}, s32[]{:S(2)}) async-start(s8[4718592]{0:T(1024)(128)(4,1)} %bitcast.27), calls=%async_computation.1 | async-start | bytes 8388608
  143.6 17.5 %copy-start.2 = (bf16[8,50,768]{2,0,1:T(8,128)(2,1)S(1)}, bf16[8,50,768]{2,0,1:T(8,128)(2,1)}, u32[]{:S(2)}) copy-start(bf16[8,50,768]{2,0,1:T(8,128)(2,1)} %param.15) | copy-start | bytes 1843204
  143.6 17.5 %slice-start.1 = ((s8[4718592]{0:T(1024)(128)(4,1)}), s8[524288]{0:T(1024)(128)(4,1)S(1)}, s32[]{:S(2)}) async-start(s8[4718592]{0:T(1024)(128)(4,1)} %bitcast.27), calls=%async_computation.2 | async-start | bytes 1048576
  143.6 14.9 %collective-permute-start.18 = (bf16[64,3968]{1,0:T(8,128)(2,1)S(1)}, bf16[64,3968]{1,0:T(8,128)(2,1)S(1)}, u32[]{:S(2)}, u32[]{:S(2)}) collective-permute-start(bf16[64,3968]{1,0:T(8,128)(2,1)S(1)} %pad_maximum_fusion.refs_0_), channel_id=1, source_target_pairs={{0,16},{1,17},{2,18},{3,19},{4,20},{5,21},{6,22},{7,23},{8,24},{9,... | collective-permute-start | bytes 1523720 | tf_op jit(solution)/shard_map/ppermute | solution.py:552
  158.5 1.9 %collective-permute-start.19 = (bf16[64,3968]{1,0:T(8,128)(2,1)S(1)}, bf16[64,3968]{1,0:T(8,128)(2,1)S(1)}, u32[]{:S(2)}, u32[]{:S(2)}) collective-permute-start(bf16[64,3968]{1,0:T(8,128)(2,1)S(1)} %pad_maximum_fusion.refs_0_), channel_id=1, source_target_pairs={{0,8},{1,9},{2,10},{3,11},{4,12},{5,13},{6,14},{7,15},{8,0},{9,1},... | collective-permute-start | bytes 1523720 | tf_op jit(solution)/shard_map/ppermute | solution.py:552
  158.5 2.6 %collective-permute-start.20 = (bf16[64,3968]{1,0:T(8,128)(2,1)S(1)}, bf16[64,3968]{1,0:T(8,128)(2,1)S(1)}, u32[]{:S(2)}, u32[]{:S(2)}) collective-permute-start(bf16[64,3968]{1,0:T(8,128)(2,1)S(1)} %collective-permute-done.18.refs_1_), channel_id=1, source_target_pairs={{0,8},{1,9},{2,10},{3,11},{4,12},{5,13},{6,14},{7,15},{8,0},{9,1},... | collective-permute-start | bytes 1523720 | tf_op jit(solution)/shard_map/ppermute | solution.py:552
Sparse Core Ops, SparseCore 0:
  10.9 88.2 all-gather.2

commit v3 on v2

--- a/solution.py
+++ b/solution.py
@@ -275,39 +275,64 @@
     )(far(normed), far(resid), gain, *pieces)
 
 
-def class_kernel(
-    plans, ids_ref, grads_ref, heads_ref, mlp_gain_ref, final_gain_ref,
-    queries_ref, probs_ref, middles_ref, kv_hbm, front_hbm, *refs,
-):
-    feed_refs = refs[:-17]
-    (
-        sent_ref, weights_ref, routes_ref, d_class_ref, d_middle_ref, up_ref, down_ref,
-        q_buf, c_buf, dq_buf, score_slots, prob_slots, kv_ref, front_ref, sems, up_sems, down_sems,
-    ) = refs[-17:]
-    images = middles_ref.shape[0]
-    up_copies = start_copies(plans[0](feed_refs, up_ref), up_sems)
-    down_copies = start_copies(plans[1](feed_refs, down_ref), down_sems)
-    front_copy, kv_copy = start_copies([(front_hbm, front_ref), (kv_hbm, kv_ref)], sems)
+def loss_kernel(ids_ref, grads_ref, heads_ref, d_final_ref):
+    images = ids_ref.shape[0]
     spread = (
         lax.broadcasted_iota(jnp.int32, (128, CLASSES * TASKS), 1) // TASKS
         == lax.broadcasted_iota(jnp.int32, (128, CLASSES * TASKS), 0)
     ).astype(F32).astype(BF16)
     task_at = lax.broadcasted_iota(jnp.int32, (images, CLASSES * TASKS), 1) % TASKS
     chosen = jnp.where(ids_ref[...] == task_at, dot(grads_ref[...], spread), 0.0).astype(BF16)
-    d_final = dot(chosen, heads_ref[...])
+    d_final_ref[...] = dot(chosen, heads_ref[...])
+
+
+def loss_grads(ids, grads, heads):
+    operands = (ids, grads, heads)
+    out = jax.ShapeDtypeStruct((ids.shape[0], D), F32)
+    return pl.pallas_call(
+        loss_kernel,
+        grid=(1,),
+        in_specs=[whole(o) for o in operands],
+        out_specs=whole(out),
+        out_shape=out,
+        compiler_params=params(12),
+        cost_estimate=cost(0.1, 2),
+        name="loss_grads",
+    )(*operands)
+
+
+def class_kernel(
+    plans, d_final_ref, grads_ref, mlp_gain_ref, final_gain_ref,
+    queries_ref, probs_ref, middles_ref, kv_hbm, front_hbm, *refs,
+):
+    feed_refs = refs[:-14]
+    (
+        sent_ref, weights_ref, routes_ref, d_class_ref, d_middle_ref, up_ref, down_ref,
+        score_slots, prob_slots, kv_ref, front_ref, sems, up_sems, down_sems,
+    ) = refs[-14:]
+    images = middles_ref.shape[0]
+    up_copies = make_copies(plans[0](feed_refs, up_ref), up_sems)
+    down_copies = make_copies(plans[1](feed_refs, down_ref), down_sems)
+    for pair in zip(up_copies, down_copies):
+        for copy in pair:
+            copy.start()
+    front_copy, kv_copy = start_copies([(front_hbm, front_ref), (kv_hbm, kv_ref)], sems)
     mlp_gain, final_gain = mlp_gain_ref[...], final_gain_ref[...]
     middle = middles_ref[:, 0, :]
     unit_mlp, inv_mlp = unit_norm(middle)
-    for copy in up_copies:
-        copy.wait()
-    pre = dot((unit_mlp * mlp_gain).astype(BF16), up_ref[...])
-    activated = gelu(pre).astype(BF16)
-    for copy in down_copies:
-        copy.wait()
-    output = middle + dot(activated, down_ref[...])
+    normed = (unit_mlp * mlp_gain).astype(BF16)
+    output, pre = middle, []
+    width = FF // len(up_copies)
+    for at, (up_copy, down_copy) in enumerate(zip(up_copies, down_copies)):
+        cols = slice(at * width, (at + 1) * width)
+        up_copy.wait()
+        pre.append(dot(normed, up_ref[:, cols]))
+        down_copy.wait()
+        output = output + dot(gelu(pre[-1]).astype(BF16), down_ref[cols, :])
+    pre = jnp.concatenate(pre, axis=1)
     unit_fin, inv_fin = unit_norm(output)
     sent_ref[:, 2 * D : 3 * D] = (unit_fin * final_gain).astype(BF16)
-    d_output = norm_back(d_final, unit_fin, inv_fin, final_gain)
+    d_output = norm_back(d_final_ref[...], unit_fin, inv_fin, final_gain)
     d_act = dot_t(d_output.astype(BF16), down_ref[...])
     d_pre = (d_act * gelu_slope(pre)).astype(BF16)
     d_middle = d_output + norm_back(dot_t(d_pre, up_ref[...]), unit_mlp, inv_mlp, mlp_gain)
@@ -316,26 +341,30 @@
     d_context = dot_t(d_middle.astype(BF16), front_ref[:, 3 * D :]).astype(BF16)
     sent_ref[:, 3 * D : 4 * D] = d_context
     of_head = head_rows_mask()
-    own = of_head.astype(BF16)
     scale = HDIM ** (-0.5)
     kv_copy.wait()
-    for img in range(images):
-        at = slice(img * HEADS_PAD, (img + 1) * HEADS_PAD)
-        query = queries_ref[img, 0:1, :]
-        sent_ref[img : img + 1, :D] = query
-        q_buf[at] = query * own * np.float32(scale).astype(BF16)
-        d_rows = d_context[img : img + 1] * own
-        c_buf[at] = d_rows
-        keys, values = kv_ref[img, :, :D], kv_ref[img, :, D:]
-        probs = probs_ref[img]
-        d_probs = dot_t(d_rows, values)
-        d_scores = probs * (d_probs - jnp.sum(probs * d_probs, axis=-1, keepdims=True))
-        score_slots[at] = d_scores[:, :128]
-        prob_slots[at] = probs[:, :128]
-        d_scores = d_scores.astype(BF16)
-        weights_ref[img, :HEADS_PAD] = d_scores
-        weights_ref[img, HEADS_PAD:] = probs.astype(BF16)
-        dq_buf[img : img + 1] = jnp.sum(dot(d_scores, keys) * of_head, axis=0, keepdims=True) * scale
+    queries = jnp.concatenate([queries_ref[img, 0:1, :] for img in range(images)], axis=0)
+    sent_ref[:, :D] = queries
+    spread_heads = lambda rows: (rows[:, None, :] * of_head[None]).reshape(images * HEADS_PAD, D).astype(BF16)
+    by_head = spread_heads(d_context.astype(F32))
+    probs = probs_ref[...].reshape(images * HEADS_PAD, BLOCK)
+    rows_of = lambda array, img: array[img * HEADS_PAD : (img + 1) * HEADS_PAD]
+    d_probs = jnp.concatenate(
+        [dot_t(rows_of(by_head, img), kv_ref[img, :, D:]) for img in range(images)], axis=0
+    )
+    d_scores = probs * (d_probs - jnp.sum(probs * d_probs, axis=-1, keepdims=True))
+    score_slots[...] = d_scores[:, :128]
+    prob_slots[...] = probs[:, :128]
+    d_scores = d_scores.astype(BF16)
+    weights_ref[:, :HEADS_PAD] = d_scores.reshape(images, HEADS_PAD, BLOCK)
+    weights_ref[:, HEADS_PAD:] = probs.astype(BF16).reshape(images, HEADS_PAD, BLOCK)
+    d_queries = jnp.concatenate(
+        [
+            jnp.sum(dot(rows_of(d_scores, img), kv_ref[img, :, :D]) * of_head, axis=0, keepdims=True)
+            for img in range(images)
+        ],
+        axis=0,
+    )
     lane = lax.broadcasted_iota(jnp.int32, (images, 128), 1)
     for slots, start in ((prob_slots, D), (score_slots, 4 * D)):
         for pair in range(HEADS // 2):
@@ -343,22 +372,20 @@
             both = jnp.where(lane < SLOTS, first, pltpu.roll(second, SLOTS, 1))
             sent_ref[:, start + pair * 128 : start + (pair + 1) * 128] = both.astype(BF16)
     sent_ref[:, 5 * D :] = grads_ref[...]
-    by_key = dot_t(q_buf[...], front_ref[:, D : 2 * D]).astype(BF16)
-    by_value = dot_t(c_buf[...], front_ref[:, 2 * D : 3 * D]).astype(BF16)
-    for img in range(images):
-        at = slice(img * HEADS_PAD, (img + 1) * HEADS_PAD)
-        routes_ref[img, :HEADS_PAD] = by_key[at]
-        routes_ref[img, HEADS_PAD:] = by_value[at]
-    d_class_ref[...] = dot_t(dq_buf[...].astype(BF16), front_ref[:, :D])
+    by_key = dot_t(spread_heads(queries.astype(F32) * scale), front_ref[:, D : 2 * D]).astype(BF16)
+    by_value = dot_t(by_head, front_ref[:, 2 * D : 3 * D]).astype(BF16)
+    routes_ref[:, :HEADS_PAD] = by_key.reshape(images, HEADS_PAD, D)
+    routes_ref[:, HEADS_PAD:] = by_value.reshape(images, HEADS_PAD, D)
+    d_class_ref[...] = dot_t((d_queries * scale).astype(BF16), front_ref[:, :D])
 
 
 SENT = 5 * D + 128
 
 
-def class_path(ids, grads, heads, gains, attended, feed_weights):
-    images = ids.shape[0]
+def class_path(d_final, grads, gains, attended, feed_weights):
+    images = d_final.shape[0]
     *small, kv, front = attended
-    operands = (ids, grads, heads, *gains[1:], *small)
+    operands = (d_final, grads, *gains[1:], *small)
     feed_arrays, plans, copies_n = feed_weights
     remote = (far(kv), far(front), *feed_arrays)
     outs = [
@@ -377,9 +404,6 @@
         out_specs=[near] * len(outs),
         out_shape=outs,
         scratch_shapes=[
-            pltpu.VMEM((images * HEADS_PAD, D), BF16),
-            pltpu.VMEM((images * HEADS_PAD, D), BF16),
-            pltpu.VMEM((images, D), F32),
             pltpu.VMEM((images * HEADS_PAD, 128), F32),
             pltpu.VMEM((images * HEADS_PAD, 128), F32),
             pltpu.VMEM(kv.shape, BF16),
@@ -633,21 +657,23 @@
         return [(refs[0].at[:, d, 0:96, :], dst.at[:, :, D * d : D * d + D]) for d in range(4)]
 
     def down_plan(refs, dst):
-        return [(refs[0].at[:, :, 96:192, :], dst.reshape(8, 4, 96, D))]
+        dst = dst.reshape(8, 4, 96, D)
+        return [(refs[0].at[2 * d : 2 * d + 2, :, 96:192, :], dst.at[2 * d : 2 * d + 2]) for d in range(4)]
 
     return [far(gathered)], (up_plan, down_plan), 4
 
 
 def share_rows(rows, works):
-    done, parts = None, [rows]
-    for work, shifts in zip(works, ([dict(dz=r) for r in (1, 2, 3)], [dict(dx=1)], [dict(dy=1)])):
+    parts, done = [rows], None
+    for work, shifts in zip(works, ([dict(dz=r) for r in (1, 2, 3)], [dict(dx=1)], [dict(dy=1), dict(dc=1)])):
         rows = jnp.concatenate(parts, axis=0) if len(parts) > 1 else rows
         if done is not None:
             rows, done = lax.optimization_barrier((rows, done))
         parts = [rows] + [exchange(rows, **shift) for shift in shifts]
         done = work(done)
-    *parts, done = lax.optimization_barrier((*parts, done))
-    return parts + [exchange(part, dc=1) for part in parts], done
+    near, across, core = parts
+    across, done = lax.optimization_barrier((across, done))
+    return [near, across, core, exchange(across, dc=1)], done
 
 
 def body(
@@ -685,7 +711,7 @@
         fetched = [gather_rows(front_shard, dp)], copy_whole(0), 1
     *attended, middle, normed_two, front = attend(normed, resid, gains[1], *fetched)
     sent, weights, routes, d_class, d_middle, up_all, down_all = class_path(
-        ids_col, grads, head_rows, gains, [*attended, front], feed_weights
+        loss_grads(ids_col, grads, head_rows), grads, gains, [*attended, front], feed_weights
     )
 
     def feed_rows(rows, chain):

time: 175 us -> 170 us (0.971)
  Pallas kernels: 95.3 us -> 90.8 us
  waiting for transfers between devices: 37.3 us -> 35.5 us
    pallas_call x1, Pallas kernels: 16.6 us -> 11.7 us  [class_path(): pl.pallas_call(functools.partial(class_kernel, plans), in_specs=[near] *...]
  transfers between devices with their start and end apart: 22 -> 22, of which waited for: 9 -> 7; matrix products, arithmetic and copies ran while one was open for 2% -> 2% of each run, Pallas kernels for 41% -> 42%
where the time goes in v3:
time: 170 us
  Pallas kernels  90.8 us (53%)
  waiting for transfers between devices  35.5 us (21%)
  starting transfers between devices  20.1 us (12%)
  between operations  14.4 us (8%)
  local copies, waits for them, and re-layouts  7.25 us (4%)
    pallas_call x1, Pallas kernels, attend(): pl.pallas_call(functools.partial(attend_kernel, plan), grid=(rows_n, IMGS...  30.9 us
    pallas_call x2, Pallas kernels, feed(): pl.pallas_call(feed_kernel, grid=(IMGS_ROW,), in_specs=[spec, spec] + [pl...  28.1 us
    ppermute x21, waiting for transfers between devices, exchange(): return lax.ppermute(value, ('dp', 'fsdp'), pairs)  27.7 us
    ppermute x21, starting transfers between devices, exchange(): return lax.ppermute(value, ('dp', 'fsdp'), pairs)  20.1 us
    pallas_call x1, Pallas kernels, class_path(): pl.pallas_call(functools.partial(class_kernel, plans), in_specs=[near] *...  11.7 us
    pallas_call x1, Pallas kernels, token_grads(): pl.pallas_call(token_grads_kernel, grid=(rows_n,), in_specs=[row_spec, im...  7.86 us
    all_gather x1, waiting for transfers between devices, fetch_rest(): lax.all_gather(jnp.concatenate([up_part, down_part], axis=0), ('fsdp', 'd...  7.69 us
    pallas_call x1, Pallas kernels, sums(): pl.pallas_call(sums_kernel, grid=(1,), in_specs=[pl.BlockSpec(memory_spac...  7.15 us
  transfers between devices with their start and end apart: 22, of which 7 were waited for; matrix products, arithmetic and copies ran while one was open for 2% of the time, Pallas kernels for 42%

profile of v3, /device:TPU:0, one launch (start us, length us, event | category | flops | bytes accessed | tf_op | source)
XLA Modules:
  0.0 169.7 jit_solution(8315708054293865988)
XLA Ops:
  7.2 0.0 all-gather.3.cloned.1.call-start
  7.2 1.2 constant_dynamic-slice_fusion
  8.4 0.8 pad_maximum_fusion.2
  9.2 0.0 all-gather.3.cloned.1.call-update
  9.2 1.0 constant_dynamic-update-slice_fusion.1
  10.3 0.9 constant_dynamic-update-slice_fusion.refs_0_
  11.2 0.0 copy-start.5
  11.2 0.0 copy-start.10
  11.3 0.0 copy-start.11
  11.3 0.0 copy-start.12
  11.3 5.1 %collective-permute-start.2 = (bf16[48,1536]{1,0:T(8,128)(2,1)S(1)}, bf16[48,1536]{1,0:T(8,128)(2,1)S(1)}, u32[]{:S(2)}, u32[]{:S(2)}) collective-permute-start(bf16[48,1536]{1,0:T(8,128)(2,1)S(1)} %dynamic_slice.12), channel_id=1, source_target_pairs={{0,6},{1,7},{2,4},{3,5},{4,2},{5,3},{6,0},{7,1},{8,14},{9,15},{10,... | collective-permute-start | bytes 442376 | tf_op jit(solution)/shard_map/ppermute | solution.py:576
  16.4 0.6 collective-permute-start
  17.1 1.7 %collective-permute-start.3 = (bf16[96,1536]{1,0:T(8,128)(2,1)S(1)}, bf16[96,1536]{1,0:T(8,128)(2,1)S(1)}, u32[]{:S(2)}, u32[]{:S(2)}) collective-permute-start(bf16[96,1536]{1,0:T(8,128)(2,1)S(1)} %constant_dynamic-slice_fusion.2), channel_id=1, source_target_pairs={{0,1},{1,0},{2,3},{3,2},{4,5},{5,4},{6,7},{7,6},{8,9},{9,8},{10,11... | collective-permute-start | bytes 884744 | tf_op jit(solution)/shard_map/ppermute | solution.py:576
  18.8 0.0 copy-start.2
  18.8 1.1 copy-done.2
  19.9 4.7 %assemble.1 = (bf16[2,1024,768]{2,1,0:T(8,128)(2,1)}, bf16[2,1024,768]{2,1,0:T(8,128)(2,1)}) custom-call(s32[2,4]{1,0:T(2,128)S(1)} %bitcast.26, bf16[2,1024,768]{2,1,0:T(8,128)(2,1)S(1)} %bitcast.22, bf16[400,768]{1,0:T(8,128)(2,1)S(1)} %bitcast.24, f32[1,768]{1,0:T(1,128)S(1)} %reshape.56.gain_ref), custom_call_target="tpu_custom_call" | custom-call | flops 100000000 | bytes 10000000 | tf_op jit(solution)/shard_map/assemble/pallas_call | solution.py:135
  24.5 0.0 collective-permute-done.2
  24.5 8.8 %collective-permute-done.1 = bf16[48,1536]{1,0:T(8,128)(2,1)S(1)} collective-permute-done((bf16[48,1536]{1,0:T(8,128)(2,1)S(1)}, bf16[48,1536]{1,0:T(8,128)(2,1)S(1)}, u32[]{:S(2)}, u32[]{:S(2)}) %collective-permute-start.1) | collective-permute-done | bytes 147488 | tf_op jit(solution)/shard_map/ppermute | solution.py:576
  33.4 0.0 collective-permute-done
  33.4 0.0 copy-start.6
  33.4 1.9 %collective-permute-start.4 = (bf16[144,1536]{1,0:T(8,128)(2,1)S(1)}, bf16[144,1536]{1,0:T(8,128)(2,1)S(1)}, u32[]{:S(2)}, u32[]{:S(2)}) collective-permute-start(bf16[144,1536]{1,0:T(8,128)(2,1)S(1)} %pad_maximum_fusion.1.refs_2_), channel_id=1, source_target_pairs={{0,1},{1,0},{2,3},{3,2},{4,5},{5,4},{6,7},{7,6},{8,9},{9,8},{10,11... | collective-permute-start | bytes 1327112 | tf_op jit(solution)/shard_map/ppermute | solution.py:576
  35.4 1.7 %collective-permute-start.5 = (bf16[144,1536]{1,0:T(8,128)(2,1)S(1)}, bf16[144,1536]{1,0:T(8,128)(2,1)S(1)}, u32[]{:S(2)}, u32[]{:S(2)}) collective-permute-start(bf16[144,1536]{1,0:T(8,128)(2,1)S(1)} %pad_maximum_fusion.1.refs_2_), channel_id=1, source_target_pairs={{0,16},{1,17},{2,18},{3,19},{4,20},{5,21},{6,22},{7,23},{8,24},{9,... | collective-permute-start | bytes 1327112 | tf_op jit(solution)/shard_map/ppermute | solution.py:576
  37.1 0.0 collective-permute-start.8
  37.1 6.8 %collective-permute-done.4.refs_3_ = bf16[144,1536]{1,0:T(8,128)(2,1)S(1)} collective-permute-done((bf16[144,1536]{1,0:T(8,128)(2,1)S(1)}, bf16[144,1536]{1,0:T(8,128)(2,1)S(1)}, u32[]{:S(2)}, u32[]{:S(2)}) %collective-permute-start.4) | collective-permute-done | bytes 442400 | tf_op jit(solution)/shard_map/ppermute | solution.py:576
  44.0 1.7 collective-permute-start.6
  45.7 4.5 %collective-permute-done.5.refs_4_ = bf16[144,1536]{1,0:T(8,128)(2,1)S(1)} collective-permute-done((bf16[144,1536]{1,0:T(8,128)(2,1)S(1)}, bf16[144,1536]{1,0:T(8,128)(2,1)S(1)}, u32[]{:S(2)}, u32[]{:S(2)}) %collective-permute-start.5) | collective-permute-done | bytes 442400 | tf_op jit(solution)/shard_map/ppermute | solution.py:576
  50.1 0.0 collective-permute-start.11
  50.1 0.5 collective-permute-start.10
  50.7 0.0 collective-permute-done.8.refs_7_
  50.7 0.1 collective-permute-start.7
  50.8 3.1 %collective-permute-done.6.refs_5_ = bf16[80,1536]{1,0:T(8,128)(2,1)S(1)} collective-permute-done((bf16[80,1536]{1,0:T(8,128)(2,1)S(1)}, bf16[80,1536]{1,0:T(8,128)(2,1)S(1)}, u32[]{:S(2)}, u32[]{:S(2)}) %collective-permute-start.6) | collective-permute-done | bytes 245792 | tf_op jit(solution)/shard_map/ppermute | solution.py:576
  53.9 0.5 broadcast.7
  54.4 0.7 reduce.5
  55.1 2.6 %collective-permute-done.7.refs_6_ = bf16[64,1536]{1,0:T(8,128)(2,1)} collective-permute-done((bf16[64,1536]{1,0:T(8,128)(2,1)S(1)}, bf16[64,1536]{1,0:T(8,128)(2,1)}, u32[]{:S(2)}, u32[]{:S(2)}) %collective-permute-start.7) | collective-permute-done | bytes 196640 | tf_op jit(solution)/shard_map/ppermute | solution.py:576
  57.7 0.0 collective-permute-start.13
  57.7 0.1 convert_element_type.8
  57.8 0.1 reshape_reshape.4.ids_ref
  57.9 0.1 broadcast_in_dim.2
  57.9 0.1 pad_maximum_fusion.4.grads_ref
  58.0 1.3 copy-done.1
  59.3 0.4 loss_grads.1.d_final_ref
  59.7 0.0 collective-permute-done.9.refs_8_
  59.7 0.0 collective-permute-done.13.refs_12_
  59.7 0.0 collective-permute-done.11.refs_10_
  59.7 0.0 collective-permute-done.12.refs_11_
  59.8 0.7 copy-done.13
  60.5 0.2 copy-done.14
  60.6 30.9 %attend.1 = (bf16[8,16,768]{2,1,0:T(8,128)(2,1)S(1)}, f32[8,16,256]{2,1,0:T(8,128)S(1)}, f32[8,8,768]{2,1,0:T(8,128)S(1)}, bf16[8,256,1536]{2,1,0:T(8,128)(2,1)}...) custom-call(bf16[2,1024,768]{2,1,0:T(8,128)(2,1)} %get-tuple-element.33.normed_ref, ...), custom_call_target="tpu_custom_call" | custom-call | flops 16000000000 | bytes 30000000 | tf_op jit(solution)/shard_map/attend/pallas_call | solution.py:240
  91.5 7.7 %all-gather.3.cloned.1.call-done = bf16[6144,768]{1,0:T(8,128)(2,1)} async-done(((bf16[192,768]{1,0:T(8,128)(2,1)}), bf16[6144,768]{1,0:T(8,128)(2,1)}) %all-gather.3.cloned.1.call-update) | async-done | bytes 9437200 | tf_op jit(solution)/shard_map/all_gather | solution.py:652
  99.2 11.7 %class_path.1 = (bf16[8,3968]{1,0:T(8,128)(2,1)S(1)}, bf16[8,32,256]{2,1,0:T(8,128)(2,1)S(1)}, bf16[8,32,768]{2,1,0:T(8,128)(2,1)S(1)}, f32[8,768]{1,0:T(8,128)S...) custom-call(f32[8,768]{1,0:T(8,128)S(1)} %loss_grads.1.d_final_ref, ...), custom_call_target="tpu_custom_call" | custom-call | flops 8000000000 | bytes 30000000 | tf_op jit(solution)/shard_map/class_path/pallas_call | solution.py:401
  110.9 2.0 %collective-permute-start.16 = (bf16[8,3968]{1,0:T(8,128)(2,1)S(1)}, bf16[8,3968]{1,0:T(8,128)(2,1)S(1)}, u32[]{:S(2)}, u32[]{:S(2)}) collective-permute-start(bf16[8,3968]{1,0:T(8,128)(2,1)S(1)} %get-tuple-element.41), channel_id=1, source_target_pairs={{0,6},{1,7},{2,4},{3,5},{4,2},{5,3},{6,0},{7,1},{8,14},{9,15},{10,... | collective-permute-start | bytes 190472 | tf_op jit(solution)/shard_map/ppermute | solution.py:576
  112.9 0.9 collective-permute-start.15
  113.9 1.5 collective-permute-start.14
  115.4 7.9 %token_grads.1 = f32[2,1024,768]{2,1,0:T(8,128)} custom-call(bf16[2,1024,768]{2,1,0:T(8,128)(2,1)} %get-tuple-element.34.resid_ref, bf16[8,32,256]{2,1,0:T(8,128)(2,1)S(1)} %get-tuple-element.42.weights_ref, bf16[8,32,768]{2,1,0:T(8,128)(2,1)S(1)} %get-tuple-element.43.routes_ref, f32[8,768]{1,0:T(8,128)S(1)} %get-tuple-element.44.d_class_ref, ...), custom_call_target="tpu_custom_call" | custom-call | flops 500000000 | bytes 20000000 | tf_op jit(solution)/shard_map/token_grads/pallas_call | solution.py:485
  123.3 0.0 collective-permute-done.16
  123.3 0.0 collective-permute-done.15
  123.3 1.5 collective-permute-start.17
  124.8 13.9 %feed.2.refs_0_ = bf16[2,1024,768]{2,1,0:T(8,128)(2,1)} custom-call(bf16[2048,768]{1,0:T(8,128)(2,1)} %get-tuple-element.48.normed_ref, f32[2048,768]{1,0:T(8,128)} %get-tuple-element.49.middle_ref, bf16[768,3072]{1,0:T(8,128)(2,1)S(1)} %get-tuple-element.50.up_ref, bf16[3072,768]{1,0:T(8,128)(2,1)S(1)} %get-tuple-element.51.down_ref), custom_call_target="tpu_custom_call" | custom-call | flops 10000000000 | bytes 20000000 | tf_op jit(solution)/shard_map/feed/pallas_call | solution.py:447
  138.7 0.0 copy-start.3
  138.7 0.1 collective-permute-start.19
  138.8 0.7 collective-permute-start.18
  139.5 14.3 %feed.3 = bf16[2,1024,768]{2,1,0:T(8,128)(2,1)} custom-call(bf16[2048,768]{1,0:T(8,128)(2,1)} %get-tuple-element.48.normed_ref, f32[2048,768]{1,0:T(8,128)} %get-tuple-element.49.middle_ref, bf16[768,3072]{1,0:T(8,128)(2,1)S(1)} %get-tuple-element.50.up_ref, bf16[3072,768]{1,0:T(8,128)(2,1)S(1)} %get-tuple-element.51.down_ref, ...), custom_call_target="tpu_custom_call", output_to_operand_aliasing={{}: (4, {})} | custom-call | flops 10000000000 | bytes 20000000 | tf_op jit(solution)/shard_map/feed/pallas_call | solution.py:447
  153.8 1.9 %collective-permute-done.20.refs_3_ = bf16[64,3968]{1,0:T(8,128)(2,1)S(1)} collective-permute-done((bf16[64,3968]{1,0:T(8,128)(2,1)S(1)}, bf16[64,3968]{1,0:T(8,128)(2,1)S(1)}, u32[]{:S(2)}, u32[]{:S(2)}) %collective-permute-start.20) | collective-permute-done | bytes 507936 | tf_op jit(solution)/shard_map/ppermute | solution.py:576
  155.6 7.1 %sums.1 = (f32[400,768]{1,0:T(8,128)}, f32[800,768]{1,0:T(8,128)}) custom-call(bf16[768,3072]{1,0:T(8,128)(2,1)S(1)} %bitcast.28, bf16[400,768]{1,0:T(8,128)(2,1)S(1)} %bitcast.25, f32[1,768]{1,0:T(1,128)S(1)} %reshape.56.gain_ref, bf16[64,3968]{1,0:T(8,128)(2,1)S(1)} %pad_maximum_fusion.refs_0_, bf16[64,3968]{1,0:T(8,128)(2,1)S(1)} %collective-permute-done.18.refs_1_, ...), custom_call_target="tpu_custom_call" | custom-call | flops 5000000000 | bytes 15000000 | tf_op jit(solution)/shard_map/sums/pallas_call | solution.py:537
  (51 shorter events, 0.3 us)
Async XLA Ops:
  7.2 11.6 %copy-start.9 = (f32[768]{0:T(1024)S(1)}, f32[768]{0:T(1024)}, u32[]{:S(2)}) copy-start(f32[768]{0:T(1024)} %param.21) | copy-start | bytes 9220
  7.2 11.6 %copy-start.4 = (s32[2,1,4]{2,1,0:T(1,128)S(1)}, s32[2,1,4]{2,1,0:T(1,128)}, u32[]{:S(2)}) copy-start(s32[2,1,4]{2,1,0:T(1,128)} %param.13) | copy-start | bytes 100
  7.2 11.6 %copy-start = (bf16[2,1,1024,768]{3,2,1,0:T(8,128)(2,1)S(1)}, bf16[2,1,1024,768]{3,2,1,0:T(8,128)(2,1)}, u32[]{:S(2)}) copy-start(bf16[2,1,1024,768]{3,2,1,0:T(8,128)(2,1)} %param.12) | copy-start | bytes 9437188
  7.2 92.0 %all-gather.3.cloned.1.call-start = ((), (), s32[]{:S(2)}) async-start(), calls=%async_computation | async-start | bytes 9732096 | tf_op jit(solution)/shard_map/all_gather | solution.py:652
  11.2 7.6 %copy-start.5 = (bf16[96,3072]{1,0:T(8,128)(2,1)}, bf16[96,3072]{1,0:T(8,128)(2,1)S(1)}, u32[]{:S(2)}) copy-start(bf16[96,3072]{1,0:T(8,128)(2,1)S(1)} %constant_dynamic-update-slice_fusion.refs_0_) | copy-start | bytes 1769476
  11.2 46.5 %copy-start.10 = (f32[768]{0:T(1024)S(1)}, f32[768]{0:T(1024)}, u32[]{:S(2)}) copy-start(f32[768]{0:T(1024)} %param.22) | copy-start | bytes 9220
  11.3 46.6 %copy-start.11 = (f32[768]{0:T(1024)S(1)}, f32[768]{0:T(1024)}, u32[]{:S(2)}) copy-start(f32[768]{0:T(1024)} %param.23) | copy-start | bytes 9220
  11.3 46.7 %copy-start.12 = (bf16[2,1,4,100]{3,2,1,0:T(4,128)(2,1)S(1)}, bf16[2,1,4,100]{3,2,1,0:T(4,128)(2,1)}, u32[]{:S(2)}) copy-start(bf16[2,1,4,100]{3,2,1,0:T(4,128)(2,1)} %param.14) | copy-start | bytes 4804
  11.3 13.3 %collective-permute-start.2 = (bf16[48,1536]{1,0:T(8,128)(2,1)S(1)}, bf16[48,1536]{1,0:T(8,128)(2,1)S(1)}, u32[]{:S(2)}, u32[]{:S(2)}) collective-permute-start(bf16[48,1536]{1,0:T(8,128)(2,1)S(1)} %dynamic_slice.12), channel_id=1, source_target_pairs={{0,6},{1,7},{2,4},{3,5},{4,2},{5,3},{6,0},{7,1},{8,14},{9,15},{10,... | collective-permute-start | bytes 442376 | tf_op jit(solution)/shard_map/ppermute | solution.py:576
  16.4 17.0 %collective-permute-start.1 = (bf16[48,1536]{1,0:T(8,128)(2,1)S(1)}, bf16[48,1536]{1,0:T(8,128)(2,1)S(1)}, u32[]{:S(2)}, u32[]{:S(2)}) collective-permute-start(bf16[48,1536]{1,0:T(8,128)(2,1)S(1)} %dynamic_slice.12), channel_id=1, source_target_pairs={{0,4},{1,5},{2,6},{3,7},{4,0},{5,1},{6,2},{7,3},{8,12},{9,13},{10,... | collective-permute-start | bytes 442376 | tf_op jit(solution)/shard_map/ppermute | solution.py:576
  16.4 17.0 %collective-permute-start = (bf16[48,1536]{1,0:T(8,128)(2,1)S(1)}, bf16[48,1536]{1,0:T(8,128)(2,1)S(1)}, u32[]{:S(2)}, u32[]{:S(2)}) collective-permute-start(bf16[48,1536]{1,0:T(8,128)(2,1)S(1)} %dynamic_slice.12), channel_id=1, source_target_pairs={{0,2},{1,3},{2,0},{3,1},{4,6},{5,7},{6,4},{7,5},{8,10},{9,11},{10,... | collective-permute-start | bytes 442376 | tf_op jit(solution)/shard_map/ppermute | solution.py:576
  17.1 20.0 %collective-permute-start.3 = (bf16[96,1536]{1,0:T(8,128)(2,1)S(1)}, bf16[96,1536]{1,0:T(8,128)(2,1)S(1)}, u32[]{:S(2)}, u32[]{:S(2)}) collective-permute-start(bf16[96,1536]{1,0:T(8,128)(2,1)S(1)} %constant_dynamic-slice_fusion.2), channel_id=1, source_target_pairs={{0,1},{1,0},{2,3},{3,2},{4,5},{5,4},{6,7},{7,6},{8,9},{9,8},{10,11... | collective-permute-start | bytes 884744 | tf_op jit(solution)/shard_map/ppermute | solution.py:576
  18.8 1.1 copy-start.2
  33.4 26.4 %copy-start.6 = (bf16[144,1536]{1,0:T(8,128)(2,1)}, bf16[144,1536]{1,0:T(8,128)(2,1)S(1)}, u32[]{:S(2)}) copy-start(bf16[144,1536]{1,0:T(8,128)(2,1)S(1)} %pad_maximum_fusion.1.refs_2_) | copy-start | bytes 1327108
  33.4 10.5 %collective-permute-start.4 = (bf16[144,1536]{1,0:T(8,128)(2,1)S(1)}, bf16[144,1536]{1,0:T(8,128)(2,1)S(1)}, u32[]{:S(2)}, u32[]{:S(2)}) collective-permute-start(bf16[144,1536]{1,0:T(8,128)(2,1)S(1)} %pad_maximum_fusion.1.refs_2_), channel_id=1, source_target_pairs={{0,1},{1,0},{2,3},{3,2},{4,5},{5,4},{6,7},{7,6},{8,9},{9,8},{10,11... | collective-permute-start | bytes 1327112 | tf_op jit(solution)/shard_map/ppermute | solution.py:576
  35.4 14.8 %collective-permute-start.5 = (bf16[144,1536]{1,0:T(8,128)(2,1)S(1)}, bf16[144,1536]{1,0:T(8,128)(2,1)S(1)}, u32[]{:S(2)}, u32[]{:S(2)}) collective-permute-start(bf16[144,1536]{1,0:T(8,128)(2,1)S(1)} %pad_maximum_fusion.1.refs_2_), channel_id=1, source_target_pairs={{0,16},{1,17},{2,18},{3,19},{4,20},{5,21},{6,22},{7,23},{8,24},{9,... | collective-permute-start | bytes 1327112 | tf_op jit(solution)/shard_map/ppermute | solution.py:576
  37.1 22.7 %copy-start.15 = (bf16[96,1536]{1,0:T(8,128)(2,1)}, bf16[96,1536]{1,0:T(8,128)(2,1)S(1)}, u32[]{:S(2)}) copy-start(bf16[96,1536]{1,0:T(8,128)(2,1)S(1)} %collective-permute-done.3.refs_1_) | copy-start | bytes 884740
  37.1 13.6 %collective-permute-start.8 = (bf16[96,1536]{1,0:T(8,128)(2,1)S(1)}, bf16[96,1536]{1,0:T(8,128)(2,1)S(1)}, u32[]{:S(2)}, u32[]{:S(2)}) collective-permute-start(bf16[96,1536]{1,0:T(8,128)(2,1)S(1)} %collective-permute-done.3.refs_1_), channel_id=1, source_target_pairs={{0,8},{1,9},{2,10},{3,11},{4,12},{5,13},{6,14},{7,15},{8,0},{9,1},... | collective-permute-start | bytes 884744 | tf_op jit(solution)/shard_map/ppermute | solution.py:576
  44.0 15.8 %copy-start.7 = (bf16[144,1536]{1,0:T(8,128)(2,1)}, bf16[144,1536]{1,0:T(8,128)(2,1)S(1)}, u32[]{:S(2)}) copy-start(bf16[144,1536]{1,0:T(8,128)(2,1)S(1)} %collective-permute-done.4.refs_3_) | copy-start | bytes 1327108
  44.0 9.9 %collective-permute-start.6 = (bf16[80,1536]{1,0:T(8,128)(2,1)S(1)}, bf16[80,1536]{1,0:T(8,128)(2,1)S(1)}, u32[]{:S(2)}, u32[]{:S(2)}) collective-permute-start(bf16[80,1536]{1,0:T(8,128)(2,1)S(1)} %slice.8), channel_id=1, source_target_pairs={{0,16},{1,17},{2,18},{3,19},{4,20},{5,21},{6,22},{7,23},{8,24},{9,... | collective-permute-start | bytes 737288 | tf_op jit(solution)/shard_map/ppermute | solution.py:576
  45.7 14.0 %collective-permute-start.9 = (bf16[144,1536]{1,0:T(8,128)(2,1)S(1)}, bf16[144,1536]{1,0:T(8,128)(2,1)S(1)}, u32[]{:S(2)}, u32[]{:S(2)}) collective-permute-start(bf16[144,1536]{1,0:T(8,128)(2,1)S(1)} %pad_maximum_fusion.1.refs_2_), channel_id=1, source_target_pairs={{0,8},{1,9},{2,10},{3,11},{4,12},{5,13},{6,14},{7,15},{8,0},{9,1},... | collective-permute-start | bytes 1327112 | tf_op jit(solution)/shard_map/ppermute | solution.py:576
  50.1 9.7 %copy-start.8 = (bf16[144,1536]{1,0:T(8,128)(2,1)}, bf16[144,1536]{1,0:T(8,128)(2,1)S(1)}, u32[]{:S(2)}) copy-start(bf16[144,1536]{1,0:T(8,128)(2,1)S(1)} %collective-permute-done.5.refs_4_) | copy-start | bytes 1327108
  50.1 9.6 %collective-permute-start.11 = (bf16[144,1536]{1,0:T(8,128)(2,1)S(1)}, bf16[144,1536]{1,0:T(8,128)(2,1)S(1)}, u32[]{:S(2)}, u32[]{:S(2)}) collective-permute-start(bf16[144,1536]{1,0:T(8,128)(2,1)S(1)} %collective-permute-done.5.refs_4_), channel_id=1, source_target_pairs={{0,8},{1,9},{2,10},{3,11},{4,12},{5,13},{6,14},{7,15},{8,0},{9,1},... | collective-permute-start | bytes 1327112 | tf_op jit(solution)/shard_map/ppermute | solution.py:576
  50.1 9.6 %collective-permute-start.10 = (bf16[144,1536]{1,0:T(8,128)(2,1)S(1)}, bf16[144,1536]{1,0:T(8,128)(2,1)}, u32[]{:S(2)}, u32[]{:S(2)}) collective-permute-start(bf16[144,1536]{1,0:T(8,128)(2,1)S(1)} %collective-permute-done.4.refs_3_), channel_id=1, source_target_pairs={{0,8},{1,9},{2,10},{3,11},{4,12},{5,13},{6,14},{7,15},{8,0},{9,1},... | collective-permute-start | bytes 1327112 | tf_op jit(solution)/shard_map/ppermute | solution.py:576
  50.7 9.1 %copy-start.16 = (bf16[96,1536]{1,0:T(8,128)(2,1)}, bf16[96,1536]{1,0:T(8,128)(2,1)S(1)}, u32[]{:S(2)}) copy-start(bf16[96,1536]{1,0:T(8,128)(2,1)S(1)} %collective-permute-done.8.refs_7_) | copy-start | bytes 884740
  50.7 7.0 %collective-permute-start.7 = (bf16[64,1536]{1,0:T(8,128)(2,1)S(1)}, bf16[64,1536]{1,0:T(8,128)(2,1)}, u32[]{:S(2)}, u32[]{:S(2)}) collective-permute-start(bf16[64,1536]{1,0:T(8,128)(2,1)S(1)} %slice.9), channel_id=1, source_target_pairs={{0,1},{1,0},{2,3},{3,2},{4,5},{5,4},{6,7},{7,6},{8,9},{9,8},{10,11... | collective-permute-start | bytes 589832 | tf_op jit(solution)/shard_map/ppermute | solution.py:576
  53.9 5.9 %copy-start.17 = (bf16[80,1536]{1,0:T(8,128)(2,1)}, bf16[80,1536]{1,0:T(8,128)(2,1)S(1)}, u32[]{:S(2)}) copy-start(bf16[80,1536]{1,0:T(8,128)(2,1)S(1)} %collective-permute-done.6.refs_5_) | copy-start | bytes 737284
  53.9 5.8 %collective-permute-start.12 = (bf16[80,1536]{1,0:T(8,128)(2,1)S(1)}, bf16[80,1536]{1,0:T(8,128)(2,1)}, u32[]{:S(2)}, u32[]{:S(2)}) collective-permute-start(bf16[80,1536]{1,0:T(8,128)(2,1)S(1)} %collective-permute-done.6.refs_5_), channel_id=1, source_target_pairs={{0,8},{1,9},{2,10},{3,11},{4,12},{5,13},{6,14},{7,15},{8,0},{9,1},... | collective-permute-start | bytes 737288 | tf_op jit(solution)/shard_map/ppermute | solution.py:576
  57.7 2.0 %collective-permute-start.13 = (bf16[64,1536]{1,0:T(8,128)(2,1)}, bf16[64,1536]{1,0:T(8,128)(2,1)}, u32[]{:S(2)}, u32[]{:S(2)}) collective-permute-start(bf16[64,1536]{1,0:T(8,128)(2,1)} %collective-permute-done.7.refs_6_), channel_id=1, source_target_pairs={{0,8},{1,9},{2,10},{3,11},{4,12},{5,13},{6,14},{7,15},{8,0},{9,1},... | collective-permute-start | bytes 589832 | tf_op jit(solution)/shard_map/ppermute | solution.py:576
  58.0 1.3 copy-start.1
  59.7 0.8 copy-start.13
  59.7 0.9 copy-start.14
  110.9 12.3 %collective-permute-start.16 = (bf16[8,3968]{1,0:T(8,128)(2,1)S(1)}, bf16[8,3968]{1,0:T(8,128)(2,1)S(1)}, u32[]{:S(2)}, u32[]{:S(2)}) collective-permute-start(bf16[8,3968]{1,0:T(8,128)(2,1)S(1)} %get-tuple-element.41), channel_id=1, source_target_pairs={{0,6},{1,7},{2,4},{3,5},{4,2},{5,3},{6,0},{7,1},{8,14},{9,15},{10,... | collective-permute-start | bytes 190472 | tf_op jit(solution)/shard_map/ppermute | solution.py:576
  112.9 10.3 %collective-permute-start.15 = (bf16[8,3968]{1,0:T(8,128)(2,1)S(1)}, bf16[8,3968]{1,0:T(8,128)(2,1)S(1)}, u32[]{:S(2)}, u32[]{:S(2)}) collective-permute-start(bf16[8,3968]{1,0:T(8,128)(2,1)S(1)} %get-tuple-element.41), channel_id=1, source_target_pairs={{0,4},{1,5},{2,6},{3,7},{4,0},{5,1},{6,2},{7,3},{8,12},{9,13},{10,... | collective-permute-start | bytes 190472 | tf_op jit(solution)/shard_map/ppermute | solution.py:576
  113.9 9.4 %collective-permute-start.14 = (bf16[8,3968]{1,0:T(8,128)(2,1)S(1)}, bf16[8,3968]{1,0:T(8,128)(2,1)S(1)}, u32[]{:S(2)}, u32[]{:S(2)}) collective-permute-start(bf16[8,3968]{1,0:T(8,128)(2,1)S(1)} %get-tuple-element.41), channel_id=1, source_target_pairs={{0,2},{1,3},{2,0},{3,1},{4,6},{5,7},{6,4},{7,5},{8,10},{9,11},{10,... | collective-permute-start | bytes 190472 | tf_op jit(solution)/shard_map/ppermute | solution.py:576
  123.3 15.4 %collective-permute-start.17 = (bf16[32,3968]{1,0:T(8,128)(2,1)S(1)}, bf16[32,3968]{1,0:T(8,128)(2,1)S(1)}, u32[]{:S(2)}, u32[]{:S(2)}) collective-permute-start(bf16[32,3968]{1,0:T(8,128)(2,1)S(1)} %pad_maximum_fusion.3), channel_id=1, source_target_pairs={{0,1},{1,0},{2,3},{3,2},{4,5},{5,4},{6,7},{7,6},{8,9},{9,8},{10,11... | collective-permute-start | bytes 761864 | tf_op jit(solution)/shard_map/ppermute | solution.py:576
  138.6 17.0 %slice-start = ((s8[4718592]{0:T(1024)(128)(4,1)}), s8[4194304]{0:T(1024)(128)(4,1)S(1)}, s32[]{:S(2)}) async-start(s8[4718592]{0:T(1024)(128)(4,1)} %bitcast.27), calls=%async_computation.1 | async-start | bytes 8388608
  138.7 16.9 %copy-start.3 = (bf16[8,50,768]{2,0,1:T(8,128)(2,1)S(1)}, bf16[8,50,768]{2,0,1:T(8,128)(2,1)}, u32[]{:S(2)}) copy-start(bf16[8,50,768]{2,0,1:T(8,128)(2,1)} %param.15) | copy-start | bytes 1843204
  138.7 16.9 %slice-start.1 = ((s8[4718592]{0:T(1024)(128)(4,1)}), s8[524288]{0:T(1024)(128)(4,1)S(1)}, s32[]{:S(2)}) async-start(s8[4718592]{0:T(1024)(128)(4,1)} %bitcast.27), calls=%async_computation.2 | async-start | bytes 1048576
  138.7 15.0 %collective-permute-start.19 = (bf16[64,3968]{1,0:T(8,128)(2,1)S(1)}, bf16[64,3968]{1,0:T(8,128)(2,1)S(1)}, u32[]{:S(2)}, u32[]{:S(2)}) collective-permute-start(bf16[64,3968]{1,0:T(8,128)(2,1)S(1)} %pad_maximum_fusion.refs_0_), channel_id=1, source_target_pairs={{0,8},{1,9},{2,10},{3,11},{4,12},{5,13},{6,14},{7,15},{8,0},{9,1},... | collective-permute-start | bytes 1523720 | tf_op jit(solution)/shard_map/ppermute | solution.py:576
  138.8 14.9 %collective-permute-start.18 = (bf16[64,3968]{1,0:T(8,128)(2,1)S(1)}, bf16[64,3968]{1,0:T(8,128)(2,1)S(1)}, u32[]{:S(2)}, u32[]{:S(2)}) collective-permute-start(bf16[64,3968]{1,0:T(8,128)(2,1)S(1)} %pad_maximum_fusion.refs_0_), channel_id=1, source_target_pairs={{0,16},{1,17},{2,18},{3,19},{4,20},{5,21},{6,22},{7,23},{8,24},{9,... | collective-permute-start | bytes 1523720 | tf_op jit(solution)/shard_map/ppermute | solution.py:576
  153.7 1.9 %collective-permute-start.20 = (bf16[64,3968]{1,0:T(8,128)(2,1)S(1)}, bf16[64,3968]{1,0:T(8,128)(2,1)S(1)}, u32[]{:S(2)}, u32[]{:S(2)}) collective-permute-start(bf16[64,3968]{1,0:T(8,128)(2,1)S(1)} %collective-permute-done.18.refs_1_), channel_id=1, source_target_pairs={{0,8},{1,9},{2,10},{3,11},{4,12},{5,13},{6,14},{7,15},{8,0},{9,1},... | collective-permute-start | bytes 1523720 | tf_op jit(solution)/shard_map/ppermute | solution.py:576
Sparse Core Ops, SparseCore 0:
  10.9 88.1 all-gather.2

commit v4 on v3

--- a/solution.py
+++ b/solution.py
@@ -23,6 +23,7 @@
 BLOCK = 256
 TAIL = BLOCK - IMG
 TAIL_AT = IMGS_ROW * IMG
+SPARE = 8
 HEADS_PAD = 16
 SLOTS = 64
 EPSILON = 1e-06
@@ -93,12 +94,13 @@
 
 
 LANES = 128
+STRIDED_ROWS = -(-PROMPTS // 8) * 8 * TASKS
 LANE_BLOCKS = [slice(at, at + LANES) for at in range(0, D, LANES)]
 
 
 def by_lanes(buf, rows):
     for block, lanes in enumerate(LANE_BLOCKS):
-        buf[block] = rows[:, lanes]
+        buf[block, : rows.shape[0]] = rows[:, lanes]
 
 
 def read_strided(buf, start, count):
@@ -117,12 +119,12 @@
 ):
     row_at = pl.program_id(0)
     by_lanes(prompt_buf, prompts_ref[...].astype(F32))
-    row_buf[...] = tokens_ref[0].astype(F32)
+    row_buf[:ROW] = tokens_ref[0].astype(F32)
     for img in range(IMGS_ROW):
         img_buf[0 : IMG + 1] = row_buf[img * IMG : img * IMG + IMG + 1]
         img_buf[IMG:BLOCK] = row_buf[TAIL_AT + img * TAIL : TAIL_AT + (img + 1) * TAIL]
         img_buf[1 : 1 + PROMPTS] = read_strided(prompt_buf, ids_ref[row_at, img], PROMPTS)
-        rows = img_buf[...]
+        rows = img_buf[:BLOCK]
         at = slice(img * BLOCK, (img + 1) * BLOCK)
         resid_ref[0, at] = rows.astype(BF16)
         unit_rows, _ = unit_norm(rows)
@@ -139,9 +141,9 @@
         out_specs=[row_spec, row_spec],
         out_shape=[pltpu.HBM(tokens.shape, BF16)] * 2,
         scratch_shapes=[
-            pltpu.VMEM((ROW, D), F32),
-            pltpu.VMEM((BLOCK, D), F32),
-            pltpu.VMEM((len(LANE_BLOCKS), PROMPTS * TASKS, LANES), F32),
+            pltpu.VMEM((ROW + SPARE, D), F32),
+            pltpu.VMEM((BLOCK + SPARE, D), F32),
+            pltpu.VMEM((len(LANE_BLOCKS), STRIDED_ROWS, LANES), F32),
         ],
         compiler_params=params(20),
         cost_estimate=cost(0.1, 10),
@@ -336,7 +338,7 @@
     d_act = dot_t(d_output.astype(BF16), down_ref[...])
     d_pre = (d_act * gelu_slope(pre)).astype(BF16)
     d_middle = d_output + norm_back(dot_t(d_pre, up_ref[...]), unit_mlp, inv_mlp, mlp_gain)
-    d_middle_ref[...] = d_middle
+    d_middle_ref[:images] = d_middle
     front_copy.wait()
     d_context = dot_t(d_middle.astype(BF16), front_ref[:, 3 * D :]).astype(BF16)
     sent_ref[:, 3 * D : 4 * D] = d_context
@@ -376,7 +378,7 @@
     by_value = dot_t(by_head, front_ref[:, 2 * D : 3 * D]).astype(BF16)
     routes_ref[:, :HEADS_PAD] = by_key.reshape(images, HEADS_PAD, D)
     routes_ref[:, HEADS_PAD:] = by_value.reshape(images, HEADS_PAD, D)
-    d_class_ref[...] = dot_t((d_queries * scale).astype(BF16), front_ref[:, :D])
+    d_class_ref[:images] = dot_t((d_queries * scale).astype(BF16), front_ref[:, :D])
 
 
 SENT = 5 * D + 128
@@ -392,8 +394,8 @@
         jax.ShapeDtypeStruct((images, SENT), BF16),
         jax.ShapeDtypeStruct((images, 2 * HEADS_PAD, BLOCK), BF16),
         jax.ShapeDtypeStruct((images, 2 * HEADS_PAD, D), BF16),
-        jax.ShapeDtypeStruct((images, D), F32),
-        jax.ShapeDtypeStruct((images, D), F32),
+        jax.ShapeDtypeStruct((images + SPARE, D), F32),
+        jax.ShapeDtypeStruct((images + SPARE, D), F32),
         pltpu.VMEM((D, FF), BF16),
         pltpu.VMEM((FF, D), BF16),
     ]
@@ -438,7 +440,7 @@
 
     @pl.when(img == IMGS_ROW - 1)
     def _():
-        out_ref[0] = row_buf[...].astype(BF16)
+        out_ref[0] = row_buf[:ROW].astype(BF16)
 
 
 def feed(normed, middle, up_all, down_all, row, rows_n, chain):
@@ -453,7 +455,7 @@
         out_specs=pl.BlockSpec((1, ROW, D), lambda i: (row, 0, 0)),
         out_shape=pltpu.HBM((rows_n, ROW, D), BF16),
         input_output_aliases={} if chain is None else {4: 0},
-        scratch_shapes=[pltpu.VMEM((ROW, D), F32)],
+        scratch_shapes=[pltpu.VMEM((ROW + SPARE, D), F32)],
         compiler_params=params(18),
         cost_estimate=cost(10, 20),
         name="feed",
@@ -466,6 +468,8 @@
     place = lax.broadcasted_iota(jnp.int32, (BLOCK, 1), 0)
     is_class = (place == 0).astype(F32)
     keep = jnp.where((place == 0) | (place > PROMPTS), 1.0, 0.0)
+    zeros_at = TAIL_AT // 8 * 8
+    out_ref[0, zeros_at:] = jnp.zeros((ROW - zeros_at, D), F32)
     for img in range(IMGS_ROW):
         one = pl.ds(row_at * IMGS_ROW + img, 1)
         unit_rows, inv_std = unit_norm(resid_ref[0, img * BLOCK : (img + 1) * BLOCK].astype(F32))
@@ -475,7 +479,6 @@
         d_normed = d_normed + is_class * d_class_ref[one]
         d_resid = norm_back(d_normed, unit_rows, inv_std, gain) + is_class * d_middle_ref[one]
         out_ref[0, img * IMG : (img + 1) * IMG] = (d_resid * keep)[:IMG]
-    out_ref[0, TAIL_AT:] = jnp.zeros((ROW - TAIL_AT, D), F32)
 
 
 def token_grads(resid, weights, routes, d_class, d_middle, gain):
@@ -524,7 +527,7 @@
         d_task = d_normed[task * SLOTS + 1 : task * SLOTS + 1 + PROMPTS]
         write_strided(prompt_buf, task, norm_back(d_task, unit_rows, inv_std, gain_ref[...]))
     for block, lanes in enumerate(LANE_BLOCKS):
-        prompt_out[:, lanes] = prompt_buf[block]
+        prompt_out[:, lanes] = prompt_buf[block, : PROMPTS * TASKS]
 
 
 def sums(front, prompts, gain, parts):
@@ -544,7 +547,7 @@
         scratch_shapes=[
             pltpu.VMEM((images, SENT), BF16),
             pltpu.VMEM((TASKS * SLOTS, 2 * D), BF16),
-            pltpu.VMEM((len(LANE_BLOCKS), PROMPTS * TASKS, LANES), F32),
+            pltpu.VMEM((len(LANE_BLOCKS), STRIDED_ROWS, LANES), F32),
             pltpu.SemaphoreType.DMA((len(parts),)),
         ],
         compiler_params=params(28 if images <= 512 else 60),
@@ -686,7 +689,6 @@
     gains = [gain.reshape(1, D) for gain in (attn_gain, mlp_gain, final_gain)]
     ids = task_ids.reshape(rows_n, IMGS_ROW)
     prompt_rows = prompts.transpose(1, 0, 2).reshape(PROMPTS * TASKS, D)
-    resid, normed = assemble(ids, tokens.reshape(rows_n, ROW, D), prompt_rows, gains[0])
     token_rows = tokens.reshape(rows_n, ROW, D)
     ids_col = ids.reshape(images, 1)
     head_rows = head_weights.transpose(2, 0, 1).reshape(CLASSES * TASKS, D)

time: 170 us -> 170 us (level)
  no operation moved by 1% of the time
where the time goes in v4:
time: 170 us
  Pallas kernels  90.8 us (53%)
  waiting for transfers between devices  35.4 us (21%)
  starting transfers between devices  20.1 us (12%)
  between operations  14.4 us (8%)
  local copies, waits for them, and re-layouts  7.25 us (4%)
    pallas_call x1, Pallas kernels, attend(): pl.pallas_call(functools.partial(attend_kernel, plan), grid=(rows_n, IMGS...  30.9 us
    pallas_call x2, Pallas kernels, feed(): pl.pallas_call(feed_kernel, grid=(IMGS_ROW,), in_specs=[spec, spec] + [pl...  28.1 us
    ppermute x21, waiting for transfers between devices, exchange(): return lax.ppermute(value, ('dp', 'fsdp'), pairs)  27.7 us
    ppermute x21, starting transfers between devices, exchange(): return lax.ppermute(value, ('dp', 'fsdp'), pairs)  20.1 us
    pallas_call x1, Pallas kernels, class_path(): pl.pallas_call(functools.partial(class_kernel, plans), in_specs=[near] *...  11.7 us
    pallas_call x1, Pallas kernels, token_grads(): pl.pallas_call(token_grads_kernel, grid=(rows_n,), in_specs=[row_spec, im...  7.86 us
    all_gather x1, waiting for transfers between devices, fetch_rest(): lax.all_gather(jnp.concatenate([up_part, down_part], axis=0), ('fsdp', 'd...  7.69 us
    pallas_call x1, Pallas kernels, sums(): pl.pallas_call(sums_kernel, grid=(1,), in_specs=[pl.BlockSpec(memory_spac...  7.15 us
  transfers between devices with their start and end apart: 22, of which 7 were waited for; matrix products, arithmetic and copies ran while one was open for 2% of the time, Pallas kernels for 42%

profile of v4, /device:TPU:0, one launch (start us, length us, event | category | flops | bytes accessed | tf_op | source)
XLA Modules:
  0.0 169.6 jit_solution(15536924879925396127)
XLA Ops:
  7.2 0.0 all-gather.3.cloned.1.call-start
  7.2 1.2 constant_dynamic-slice_fusion
  8.4 0.8 pad_maximum_fusion.2
  9.2 0.0 all-gather.3.cloned.1.call-update
  9.2 1.0 constant_dynamic-update-slice_fusion.1
  10.3 0.9 constant_dynamic-update-slice_fusion.refs_0_
  11.2 0.0 copy-start.5
  11.2 0.0 copy-start.10
  11.3 0.0 copy-start.11
  11.3 0.0 copy-start.12
  11.3 5.1 %collective-permute-start.2 = (bf16[48,1536]{1,0:T(8,128)(2,1)S(1)}, bf16[48,1536]{1,0:T(8,128)(2,1)S(1)}, u32[]{:S(2)}, u32[]{:S(2)}) collective-permute-start(bf16[48,1536]{1,0:T(8,128)(2,1)S(1)} %dynamic_slice.12), channel_id=1, source_target_pairs={{0,6},{1,7},{2,4},{3,5},{4,2},{5,3},{6,0},{7,1},{8,14},{9,15},{10,... | collective-permute-start | bytes 442376 | tf_op jit(solution)/shard_map/ppermute | solution.py:579
  16.4 0.0 collective-permute-start.1
  16.4 0.6 collective-permute-start
  17.1 1.7 %collective-permute-start.3 = (bf16[96,1536]{1,0:T(8,128)(2,1)S(1)}, bf16[96,1536]{1,0:T(8,128)(2,1)S(1)}, u32[]{:S(2)}, u32[]{:S(2)}) collective-permute-start(bf16[96,1536]{1,0:T(8,128)(2,1)S(1)} %constant_dynamic-slice_fusion.2), channel_id=1, source_target_pairs={{0,1},{1,0},{2,3},{3,2},{4,5},{5,4},{6,7},{7,6},{8,9},{9,8},{10,11... | collective-permute-start | bytes 884744 | tf_op jit(solution)/shard_map/ppermute | solution.py:579
  18.8 0.0 copy-start.2
  18.8 1.1 copy-done.2
  19.9 4.7 %assemble.1 = (bf16[2,1024,768]{2,1,0:T(8,128)(2,1)}, bf16[2,1024,768]{2,1,0:T(8,128)(2,1)}) custom-call(s32[2,4]{1,0:T(2,128)S(1)} %bitcast.26, bf16[2,1024,768]{2,1,0:T(8,128)(2,1)S(1)} %bitcast.22, bf16[400,768]{1,0:T(8,128)(2,1)S(1)} %bitcast.24, f32[1,768]{1,0:T(1,128)S(1)} %reshape.56.gain_ref), custom_call_target="tpu_custom_call" | custom-call | flops 100000000 | bytes 10000000 | tf_op jit(solution)/shard_map/assemble/pallas_call | solution.py:137
  24.6 8.8 %collective-permute-done.1 = bf16[48,1536]{1,0:T(8,128)(2,1)S(1)} collective-permute-done((bf16[48,1536]{1,0:T(8,128)(2,1)S(1)}, bf16[48,1536]{1,0:T(8,128)(2,1)S(1)}, u32[]{:S(2)}, u32[]{:S(2)}) %collective-permute-start.1) | collective-permute-done | bytes 147488 | tf_op jit(solution)/shard_map/ppermute | solution.py:579
  33.4 0.0 copy-start.6
  33.4 1.9 %collective-permute-start.4 = (bf16[144,1536]{1,0:T(8,128)(2,1)S(1)}, bf16[144,1536]{1,0:T(8,128)(2,1)S(1)}, u32[]{:S(2)}, u32[]{:S(2)}) collective-permute-start(bf16[144,1536]{1,0:T(8,128)(2,1)S(1)} %pad_maximum_fusion.1.refs_2_), channel_id=1, source_target_pairs={{0,1},{1,0},{2,3},{3,2},{4,5},{5,4},{6,7},{7,6},{8,9},{9,8},{10,11... | collective-permute-start | bytes 1327112 | tf_op jit(solution)/shard_map/ppermute | solution.py:579
  35.4 1.7 %collective-permute-start.5 = (bf16[144,1536]{1,0:T(8,128)(2,1)S(1)}, bf16[144,1536]{1,0:T(8,128)(2,1)S(1)}, u32[]{:S(2)}, u32[]{:S(2)}) collective-permute-start(bf16[144,1536]{1,0:T(8,128)(2,1)S(1)} %pad_maximum_fusion.1.refs_2_), channel_id=1, source_target_pairs={{0,16},{1,17},{2,18},{3,19},{4,20},{5,21},{6,22},{7,23},{8,24},{9,... | collective-permute-start | bytes 1327112 | tf_op jit(solution)/shard_map/ppermute | solution.py:579
  37.1 0.0 collective-permute-done.3.refs_1_
  37.1 6.8 %collective-permute-done.4.refs_3_ = bf16[144,1536]{1,0:T(8,128)(2,1)S(1)} collective-permute-done((bf16[144,1536]{1,0:T(8,128)(2,1)S(1)}, bf16[144,1536]{1,0:T(8,128)(2,1)S(1)}, u32[]{:S(2)}, u32[]{:S(2)}) %collective-permute-start.4) | collective-permute-done | bytes 442400 | tf_op jit(solution)/shard_map/ppermute | solution.py:579
  44.0 1.7 collective-permute-start.6
  45.7 0.0 collective-permute-start.9
  45.7 4.5 %collective-permute-done.5.refs_4_ = bf16[144,1536]{1,0:T(8,128)(2,1)S(1)} collective-permute-done((bf16[144,1536]{1,0:T(8,128)(2,1)S(1)}, bf16[144,1536]{1,0:T(8,128)(2,1)S(1)}, u32[]{:S(2)}, u32[]{:S(2)}) %collective-permute-start.5) | collective-permute-done | bytes 442400 | tf_op jit(solution)/shard_map/ppermute | solution.py:579
  50.1 0.0 collective-permute-start.11
  50.1 0.5 collective-permute-start.10
  50.7 0.1 collective-permute-start.7
  50.8 3.1 %collective-permute-done.6.refs_5_ = bf16[80,1536]{1,0:T(8,128)(2,1)S(1)} collective-permute-done((bf16[80,1536]{1,0:T(8,128)(2,1)S(1)}, bf16[80,1536]{1,0:T(8,128)(2,1)S(1)}, u32[]{:S(2)}, u32[]{:S(2)}) %collective-permute-start.6) | collective-permute-done | bytes 245792 | tf_op jit(solution)/shard_map/ppermute | solution.py:579
  53.9 0.0 collective-permute-start.12
  53.9 0.5 broadcast.7
  54.4 0.7 reduce.5
  55.1 2.6 %collective-permute-done.7.refs_6_ = bf16[64,1536]{1,0:T(8,128)(2,1)} collective-permute-done((bf16[64,1536]{1,0:T(8,128)(2,1)S(1)}, bf16[64,1536]{1,0:T(8,128)(2,1)}, u32[]{:S(2)}, u32[]{:S(2)}) %collective-permute-start.7) | collective-permute-done | bytes 196640 | tf_op jit(solution)/shard_map/ppermute | solution.py:579
  57.7 0.1 convert_element_type.8
  57.8 0.1 reshape_reshape.4.ids_ref
  57.9 0.1 broadcast_in_dim.2
  57.9 0.1 pad_maximum_fusion.4.grads_ref
  58.0 1.3 copy-done.1
  59.3 0.4 loss_grads.1.d_final_ref
  59.7 0.0 collective-permute-done.13.refs_12_
  59.7 0.0 collective-permute-done.10.refs_9_
  59.8 0.7 copy-done.13
  60.5 0.2 copy-done.14
  60.6 30.9 %attend.1 = (bf16[8,16,768]{2,1,0:T(8,128)(2,1)S(1)}, f32[8,16,256]{2,1,0:T(8,128)S(1)}, f32[8,8,768]{2,1,0:T(8,128)S(1)}, bf16[8,256,1536]{2,1,0:T(8,128)(2,1)}...) custom-call(bf16[2,1024,768]{2,1,0:T(8,128)(2,1)} %get-tuple-element.33.normed_ref, ...), custom_call_target="tpu_custom_call" | custom-call | flops 16000000000 | bytes 30000000 | tf_op jit(solution)/shard_map/attend/pallas_call | solution.py:242
  91.5 7.7 %all-gather.3.cloned.1.call-done = bf16[6144,768]{1,0:T(8,128)(2,1)} async-done(((bf16[192,768]{1,0:T(8,128)(2,1)}), bf16[6144,768]{1,0:T(8,128)(2,1)}) %all-gather.3.cloned.1.call-update) | async-done | bytes 9437200 | tf_op jit(solution)/shard_map/all_gather | solution.py:655
  99.2 11.7 %class_path.1 = (bf16[8,3968]{1,0:T(8,128)(2,1)S(1)}, bf16[8,32,256]{2,1,0:T(8,128)(2,1)S(1)}, bf16[8,32,768]{2,1,0:T(8,128)(2,1)S(1)}, f32[16,768]{1,0:T(8,128)...) custom-call(f32[8,768]{1,0:T(8,128)S(1)} %loss_grads.1.d_final_ref, ...), custom_call_target="tpu_custom_call" | custom-call | flops 8000000000 | bytes 30000000 | tf_op jit(solution)/shard_map/class_path/pallas_call | solution.py:403
  110.9 2.0 %collective-permute-start.16 = (bf16[8,3968]{1,0:T(8,128)(2,1)S(1)}, bf16[8,3968]{1,0:T(8,128)(2,1)S(1)}, u32[]{:S(2)}, u32[]{:S(2)}) collective-permute-start(bf16[8,3968]{1,0:T(8,128)(2,1)S(1)} %get-tuple-element.41), channel_id=1, source_target_pairs={{0,6},{1,7},{2,4},{3,5},{4,2},{5,3},{6,0},{7,1},{8,14},{9,15},{10,... | collective-permute-start | bytes 190472 | tf_op jit(solution)/shard_map/ppermute | solution.py:579
  112.9 0.9 collective-permute-start.15
  113.9 1.5 collective-permute-start.14
  115.4 7.9 %token_grads.1 = f32[2,1024,768]{2,1,0:T(8,128)} custom-call(bf16[2,1024,768]{2,1,0:T(8,128)(2,1)} %get-tuple-element.34.resid_ref, bf16[8,32,256]{2,1,0:T(8,128)(2,1)S(1)} %get-tuple-element.42.weights_ref, bf16[8,32,768]{2,1,0:T(8,128)(2,1)S(1)} %get-tuple-element.43.routes_ref, f32[16,768]{1,0:T(8,128)S(1)} %get-tuple-element.44.d_class_ref, ...), custom_call_target="tpu_custom_call" | custom-call | flops 500000000 | bytes 20000000 | tf_op jit(solution)/shard_map/token_grads/pallas_call | solution.py:488
  123.3 0.0 collective-permute-done.16
  123.3 0.0 collective-permute-done.15
  123.3 0.0 collective-permute-done.14
  123.3 1.5 collective-permute-start.17
  124.8 13.9 %feed.2.refs_0_ = bf16[2,1024,768]{2,1,0:T(8,128)(2,1)} custom-call(bf16[2048,768]{1,0:T(8,128)(2,1)} %get-tuple-element.48.normed_ref, f32[2048,768]{1,0:T(8,128)} %get-tuple-element.49.middle_ref, bf16[768,3072]{1,0:T(8,128)(2,1)S(1)} %get-tuple-element.50.up_ref, bf16[3072,768]{1,0:T(8,128)(2,1)S(1)} %get-tuple-element.51.down_ref), custom_call_target="tpu_custom_call" | custom-call | flops 10000000000 | bytes 20000000 | tf_op jit(solution)/shard_map/feed/pallas_call | solution.py:449
  138.6 0.0 collective-permute-done.17
  138.7 0.0 copy-start.3
  138.7 0.1 collective-permute-start.19
  138.8 0.7 collective-permute-start.18
  139.5 14.3 %feed.3 = bf16[2,1024,768]{2,1,0:T(8,128)(2,1)} custom-call(bf16[2048,768]{1,0:T(8,128)(2,1)} %get-tuple-element.48.normed_ref, f32[2048,768]{1,0:T(8,128)} %get-tuple-element.49.middle_ref, bf16[768,3072]{1,0:T(8,128)(2,1)S(1)} %get-tuple-element.50.up_ref, bf16[3072,768]{1,0:T(8,128)(2,1)S(1)} %get-tuple-element.51.down_ref, ...), custom_call_target="tpu_custom_call", output_to_operand_aliasing={{}: (4, {})} | custom-call | flops 10000000000 | bytes 20000000 | tf_op jit(solution)/shard_map/feed/pallas_call | solution.py:449
  153.7 0.0 collective-permute-done.19.refs_2_
  153.7 1.9 %collective-permute-done.20.refs_3_ = bf16[64,3968]{1,0:T(8,128)(2,1)S(1)} collective-permute-done((bf16[64,3968]{1,0:T(8,128)(2,1)S(1)}, bf16[64,3968]{1,0:T(8,128)(2,1)S(1)}, u32[]{:S(2)}, u32[]{:S(2)}) %collective-permute-start.20) | collective-permute-done | bytes 507936 | tf_op jit(solution)/shard_map/ppermute | solution.py:579
  155.6 7.2 %sums.1 = (f32[400,768]{1,0:T(8,128)}, f32[800,768]{1,0:T(8,128)}) custom-call(bf16[768,3072]{1,0:T(8,128)(2,1)S(1)} %bitcast.28, bf16[400,768]{1,0:T(8,128)(2,1)S(1)} %bitcast.25, f32[1,768]{1,0:T(1,128)S(1)} %reshape.56.gain_ref, bf16[64,3968]{1,0:T(8,128)(2,1)S(1)} %pad_maximum_fusion.refs_0_, bf16[64,3968]{1,0:T(8,128)(2,1)S(1)} %collective-permute-done.18.refs_1_, ...), custom_call_target="tpu_custom_call" | custom-call | flops 5000000000 | bytes 15000000 | tf_op jit(solution)/shard_map/sums/pallas_call | solution.py:540
  (51 shorter events, 0.3 us)
Async XLA Ops:
  7.2 11.6 %copy-start.9 = (f32[768]{0:T(1024)S(1)}, f32[768]{0:T(1024)}, u32[]{:S(2)}) copy-start(f32[768]{0:T(1024)} %param.21) | copy-start | bytes 9220
  7.2 11.6 %copy-start.4 = (s32[2,1,4]{2,1,0:T(1,128)S(1)}, s32[2,1,4]{2,1,0:T(1,128)}, u32[]{:S(2)}) copy-start(s32[2,1,4]{2,1,0:T(1,128)} %param.13) | copy-start | bytes 100
  7.2 11.6 %copy-start = (bf16[2,1,1024,768]{3,2,1,0:T(8,128)(2,1)S(1)}, bf16[2,1,1024,768]{3,2,1,0:T(8,128)(2,1)}, u32[]{:S(2)}) copy-start(bf16[2,1,1024,768]{3,2,1,0:T(8,128)(2,1)} %param.12) | copy-start | bytes 9437188
  7.2 92.0 %all-gather.3.cloned.1.call-start = ((), (), s32[]{:S(2)}) async-start(), calls=%async_computation | async-start | bytes 9732096 | tf_op jit(solution)/shard_map/all_gather | solution.py:655
  11.2 7.6 %copy-start.5 = (bf16[96,3072]{1,0:T(8,128)(2,1)}, bf16[96,3072]{1,0:T(8,128)(2,1)S(1)}, u32[]{:S(2)}) copy-start(bf16[96,3072]{1,0:T(8,128)(2,1)S(1)} %constant_dynamic-update-slice_fusion.refs_0_) | copy-start | bytes 1769476
  11.2 46.5 %copy-start.10 = (f32[768]{0:T(1024)S(1)}, f32[768]{0:T(1024)}, u32[]{:S(2)}) copy-start(f32[768]{0:T(1024)} %param.22) | copy-start | bytes 9220
  11.3 46.6 %copy-start.11 = (f32[768]{0:T(1024)S(1)}, f32[768]{0:T(1024)}, u32[]{:S(2)}) copy-start(f32[768]{0:T(1024)} %param.23) | copy-start | bytes 9220
  11.3 46.7 %copy-start.12 = (bf16[2,1,4,100]{3,2,1,0:T(4,128)(2,1)S(1)}, bf16[2,1,4,100]{3,2,1,0:T(4,128)(2,1)}, u32[]{:S(2)}) copy-start(bf16[2,1,4,100]{3,2,1,0:T(4,128)(2,1)} %param.14) | copy-start | bytes 4804
  11.3 13.3 %collective-permute-start.2 = (bf16[48,1536]{1,0:T(8,128)(2,1)S(1)}, bf16[48,1536]{1,0:T(8,128)(2,1)S(1)}, u32[]{:S(2)}, u32[]{:S(2)}) collective-permute-start(bf16[48,1536]{1,0:T(8,128)(2,1)S(1)} %dynamic_slice.12), channel_id=1, source_target_pairs={{0,6},{1,7},{2,4},{3,5},{4,2},{5,3},{6,0},{7,1},{8,14},{9,15},{10,... | collective-permute-start | bytes 442376 | tf_op jit(solution)/shard_map/ppermute | solution.py:579
  16.4 17.0 %collective-permute-start.1 = (bf16[48,1536]{1,0:T(8,128)(2,1)S(1)}, bf16[48,1536]{1,0:T(8,128)(2,1)S(1)}, u32[]{:S(2)}, u32[]{:S(2)}) collective-permute-start(bf16[48,1536]{1,0:T(8,128)(2,1)S(1)} %dynamic_slice.12), channel_id=1, source_target_pairs={{0,4},{1,5},{2,6},{3,7},{4,0},{5,1},{6,2},{7,3},{8,12},{9,13},{10,... | collective-permute-start | bytes 442376 | tf_op jit(solution)/shard_map/ppermute | solution.py:579
  16.4 17.0 %collective-permute-start = (bf16[48,1536]{1,0:T(8,128)(2,1)S(1)}, bf16[48,1536]{1,0:T(8,128)(2,1)S(1)}, u32[]{:S(2)}, u32[]{:S(2)}) collective-permute-start(bf16[48,1536]{1,0:T(8,128)(2,1)S(1)} %dynamic_slice.12), channel_id=1, source_target_pairs={{0,2},{1,3},{2,0},{3,1},{4,6},{5,7},{6,4},{7,5},{8,10},{9,11},{10,... | collective-permute-start | bytes 442376 | tf_op jit(solution)/shard_map/ppermute | solution.py:579
  17.1 20.0 %collective-permute-start.3 = (bf16[96,1536]{1,0:T(8,128)(2,1)S(1)}, bf16[96,1536]{1,0:T(8,128)(2,1)S(1)}, u32[]{:S(2)}, u32[]{:S(2)}) collective-permute-start(bf16[96,1536]{1,0:T(8,128)(2,1)S(1)} %constant_dynamic-slice_fusion.2), channel_id=1, source_target_pairs={{0,1},{1,0},{2,3},{3,2},{4,5},{5,4},{6,7},{7,6},{8,9},{9,8},{10,11... | collective-permute-start | bytes 884744 | tf_op jit(solution)/shard_map/ppermute | solution.py:579
  18.8 1.1 copy-start.2
  33.4 26.4 %copy-start.6 = (bf16[144,1536]{1,0:T(8,128)(2,1)}, bf16[144,1536]{1,0:T(8,128)(2,1)S(1)}, u32[]{:S(2)}) copy-start(bf16[144,1536]{1,0:T(8,128)(2,1)S(1)} %pad_maximum_fusion.1.refs_2_) | copy-start | bytes 1327108
  33.4 10.5 %collective-permute-start.4 = (bf16[144,1536]{1,0:T(8,128)(2,1)S(1)}, bf16[144,1536]{1,0:T(8,128)(2,1)S(1)}, u32[]{:S(2)}, u32[]{:S(2)}) collective-permute-start(bf16[144,1536]{1,0:T(8,128)(2,1)S(1)} %pad_maximum_fusion.1.refs_2_), channel_id=1, source_target_pairs={{0,1},{1,0},{2,3},{3,2},{4,5},{5,4},{6,7},{7,6},{8,9},{9,8},{10,11... | collective-permute-start | bytes 1327112 | tf_op jit(solution)/shard_map/ppermute | solution.py:579
  35.4 14.8 %collective-permute-start.5 = (bf16[144,1536]{1,0:T(8,128)(2,1)S(1)}, bf16[144,1536]{1,0:T(8,128)(2,1)S(1)}, u32[]{:S(2)}, u32[]{:S(2)}) collective-permute-start(bf16[144,1536]{1,0:T(8,128)(2,1)S(1)} %pad_maximum_fusion.1.refs_2_), channel_id=1, source_target_pairs={{0,16},{1,17},{2,18},{3,19},{4,20},{5,21},{6,22},{7,23},{8,24},{9,... | collective-permute-start | bytes 1327112 | tf_op jit(solution)/shard_map/ppermute | solution.py:579
  37.1 22.7 %copy-start.15 = (bf16[96,1536]{1,0:T(8,128)(2,1)}, bf16[96,1536]{1,0:T(8,128)(2,1)S(1)}, u32[]{:S(2)}) copy-start(bf16[96,1536]{1,0:T(8,128)(2,1)S(1)} %collective-permute-done.3.refs_1_) | copy-start | bytes 884740
  37.1 13.6 %collective-permute-start.8 = (bf16[96,1536]{1,0:T(8,128)(2,1)S(1)}, bf16[96,1536]{1,0:T(8,128)(2,1)S(1)}, u32[]{:S(2)}, u32[]{:S(2)}) collective-permute-start(bf16[96,1536]{1,0:T(8,128)(2,1)S(1)} %collective-permute-done.3.refs_1_), channel_id=1, source_target_pairs={{0,8},{1,9},{2,10},{3,11},{4,12},{5,13},{6,14},{7,15},{8,0},{9,1},... | collective-permute-start | bytes 884744 | tf_op jit(solution)/shard_map/ppermute | solution.py:579
  44.0 15.8 %copy-start.7 = (bf16[144,1536]{1,0:T(8,128)(2,1)}, bf16[144,1536]{1,0:T(8,128)(2,1)S(1)}, u32[]{:S(2)}) copy-start(bf16[144,1536]{1,0:T(8,128)(2,1)S(1)} %collective-permute-done.4.refs_3_) | copy-start | bytes 1327108
  44.0 9.9 %collective-permute-start.6 = (bf16[80,1536]{1,0:T(8,128)(2,1)S(1)}, bf16[80,1536]{1,0:T(8,128)(2,1)S(1)}, u32[]{:S(2)}, u32[]{:S(2)}) collective-permute-start(bf16[80,1536]{1,0:T(8,128)(2,1)S(1)} %slice.8), channel_id=1, source_target_pairs={{0,16},{1,17},{2,18},{3,19},{4,20},{5,21},{6,22},{7,23},{8,24},{9,... | collective-permute-start | bytes 737288 | tf_op jit(solution)/shard_map/ppermute | solution.py:579
  45.7 14.0 %collective-permute-start.9 = (bf16[144,1536]{1,0:T(8,128)(2,1)S(1)}, bf16[144,1536]{1,0:T(8,128)(2,1)S(1)}, u32[]{:S(2)}, u32[]{:S(2)}) collective-permute-start(bf16[144,1536]{1,0:T(8,128)(2,1)S(1)} %pad_maximum_fusion.1.refs_2_), channel_id=1, source_target_pairs={{0,8},{1,9},{2,10},{3,11},{4,12},{5,13},{6,14},{7,15},{8,0},{9,1},... | collective-permute-start | bytes 1327112 | tf_op jit(solution)/shard_map/ppermute | solution.py:579
  50.1 9.7 %copy-start.8 = (bf16[144,1536]{1,0:T(8,128)(2,1)}, bf16[144,1536]{1,0:T(8,128)(2,1)S(1)}, u32[]{:S(2)}) copy-start(bf16[144,1536]{1,0:T(8,128)(2,1)S(1)} %collective-permute-done.5.refs_4_) | copy-start | bytes 1327108
  50.1 9.6 %collective-permute-start.11 = (bf16[144,1536]{1,0:T(8,128)(2,1)S(1)}, bf16[144,1536]{1,0:T(8,128)(2,1)S(1)}, u32[]{:S(2)}, u32[]{:S(2)}) collective-permute-start(bf16[144,1536]{1,0:T(8,128)(2,1)S(1)} %collective-permute-done.5.refs_4_), channel_id=1, source_target_pairs={{0,8},{1,9},{2,10},{3,11},{4,12},{5,13},{6,14},{7,15},{8,0},{9,1},... | collective-permute-start | bytes 1327112 | tf_op jit(solution)/shard_map/ppermute | solution.py:579
  50.1 9.6 %collective-permute-start.10 = (bf16[144,1536]{1,0:T(8,128)(2,1)S(1)}, bf16[144,1536]{1,0:T(8,128)(2,1)}, u32[]{:S(2)}, u32[]{:S(2)}) collective-permute-start(bf16[144,1536]{1,0:T(8,128)(2,1)S(1)} %collective-permute-done.4.refs_3_), channel_id=1, source_target_pairs={{0,8},{1,9},{2,10},{3,11},{4,12},{5,13},{6,14},{7,15},{8,0},{9,1},... | collective-permute-start | bytes 1327112 | tf_op jit(solution)/shard_map/ppermute | solution.py:579
  50.7 9.1 %copy-start.16 = (bf16[96,1536]{1,0:T(8,128)(2,1)}, bf16[96,1536]{1,0:T(8,128)(2,1)S(1)}, u32[]{:S(2)}) copy-start(bf16[96,1536]{1,0:T(8,128)(2,1)S(1)} %collective-permute-done.8.refs_7_) | copy-start | bytes 884740
  50.7 7.0 %collective-permute-start.7 = (bf16[64,1536]{1,0:T(8,128)(2,1)S(1)}, bf16[64,1536]{1,0:T(8,128)(2,1)}, u32[]{:S(2)}, u32[]{:S(2)}) collective-permute-start(bf16[64,1536]{1,0:T(8,128)(2,1)S(1)} %slice.9), channel_id=1, source_target_pairs={{0,1},{1,0},{2,3},{3,2},{4,5},{5,4},{6,7},{7,6},{8,9},{9,8},{10,11... | collective-permute-start | bytes 589832 | tf_op jit(solution)/shard_map/ppermute | solution.py:579
  53.9 5.9 %copy-start.17 = (bf16[80,1536]{1,0:T(8,128)(2,1)}, bf16[80,1536]{1,0:T(8,128)(2,1)S(1)}, u32[]{:S(2)}) copy-start(bf16[80,1536]{1,0:T(8,128)(2,1)S(1)} %collective-permute-done.6.refs_5_) | copy-start | bytes 737284
  53.9 5.8 %collective-permute-start.12 = (bf16[80,1536]{1,0:T(8,128)(2,1)S(1)}, bf16[80,1536]{1,0:T(8,128)(2,1)}, u32[]{:S(2)}, u32[]{:S(2)}) collective-permute-start(bf16[80,1536]{1,0:T(8,128)(2,1)S(1)} %collective-permute-done.6.refs_5_), channel_id=1, source_target_pairs={{0,8},{1,9},{2,10},{3,11},{4,12},{5,13},{6,14},{7,15},{8,0},{9,1},... | collective-permute-start | bytes 737288 | tf_op jit(solution)/shard_map/ppermute | solution.py:579
  57.7 2.0 %collective-permute-start.13 = (bf16[64,1536]{1,0:T(8,128)(2,1)}, bf16[64,1536]{1,0:T(8,128)(2,1)}, u32[]{:S(2)}, u32[]{:S(2)}) collective-permute-start(bf16[64,1536]{1,0:T(8,128)(2,1)} %collective-permute-done.7.refs_6_), channel_id=1, source_target_pairs={{0,8},{1,9},{2,10},{3,11},{4,12},{5,13},{6,14},{7,15},{8,0},{9,1},... | collective-permute-start | bytes 589832 | tf_op jit(solution)/shard_map/ppermute | solution.py:579
  58.0 1.3 copy-start.1
  59.7 0.8 copy-start.13
  59.7 0.9 copy-start.14
  110.9 12.3 %collective-permute-start.16 = (bf16[8,3968]{1,0:T(8,128)(2,1)S(1)}, bf16[8,3968]{1,0:T(8,128)(2,1)S(1)}, u32[]{:S(2)}, u32[]{:S(2)}) collective-permute-start(bf16[8,3968]{1,0:T(8,128)(2,1)S(1)} %get-tuple-element.41), channel_id=1, source_target_pairs={{0,6},{1,7},{2,4},{3,5},{4,2},{5,3},{6,0},{7,1},{8,14},{9,15},{10,... | collective-permute-start | bytes 190472 | tf_op jit(solution)/shard_map/ppermute | solution.py:579
  112.9 10.3 %collective-permute-start.15 = (bf16[8,3968]{1,0:T(8,128)(2,1)S(1)}, bf16[8,3968]{1,0:T(8,128)(2,1)S(1)}, u32[]{:S(2)}, u32[]{:S(2)}) collective-permute-start(bf16[8,3968]{1,0:T(8,128)(2,1)S(1)} %get-tuple-element.41), channel_id=1, source_target_pairs={{0,4},{1,5},{2,6},{3,7},{4,0},{5,1},{6,2},{7,3},{8,12},{9,13},{10,... | collective-permute-start | bytes 190472 | tf_op jit(solution)/shard_map/ppermute | solution.py:579
  113.9 9.4 %collective-permute-start.14 = (bf16[8,3968]{1,0:T(8,128)(2,1)S(1)}, bf16[8,3968]{1,0:T(8,128)(2,1)S(1)}, u32[]{:S(2)}, u32[]{:S(2)}) collective-permute-start(bf16[8,3968]{1,0:T(8,128)(2,1)S(1)} %get-tuple-element.41), channel_id=1, source_target_pairs={{0,2},{1,3},{2,0},{3,1},{4,6},{5,7},{6,4},{7,5},{8,10},{9,11},{10,... | collective-permute-start | bytes 190472 | tf_op jit(solution)/shard_map/ppermute | solution.py:579
  123.3 15.3 %collective-permute-start.17 = (bf16[32,3968]{1,0:T(8,128)(2,1)S(1)}, bf16[32,3968]{1,0:T(8,128)(2,1)S(1)}, u32[]{:S(2)}, u32[]{:S(2)}) collective-permute-start(bf16[32,3968]{1,0:T(8,128)(2,1)S(1)} %pad_maximum_fusion.3), channel_id=1, source_target_pairs={{0,1},{1,0},{2,3},{3,2},{4,5},{5,4},{6,7},{7,6},{8,9},{9,8},{10,11... | collective-permute-start | bytes 761864 | tf_op jit(solution)/shard_map/ppermute | solution.py:579
  138.6 17.0 %slice-start = ((s8[4718592]{0:T(1024)(128)(4,1)}), s8[4194304]{0:T(1024)(128)(4,1)S(1)}, s32[]{:S(2)}) async-start(s8[4718592]{0:T(1024)(128)(4,1)} %bitcast.27), calls=%async_computation.1 | async-start | bytes 8388608
  138.7 16.9 %copy-start.3 = (bf16[8,50,768]{2,0,1:T(8,128)(2,1)S(1)}, bf16[8,50,768]{2,0,1:T(8,128)(2,1)}, u32[]{:S(2)}) copy-start(bf16[8,50,768]{2,0,1:T(8,128)(2,1)} %param.15) | copy-start | bytes 1843204
  138.7 16.9 %slice-start.1 = ((s8[4718592]{0:T(1024)(128)(4,1)}), s8[524288]{0:T(1024)(128)(4,1)S(1)}, s32[]{:S(2)}) async-start(s8[4718592]{0:T(1024)(128)(4,1)} %bitcast.27), calls=%async_computation.2 | async-start | bytes 1048576
  138.7 15.0 %collective-permute-start.19 = (bf16[64,3968]{1,0:T(8,128)(2,1)S(1)}, bf16[64,3968]{1,0:T(8,128)(2,1)S(1)}, u32[]{:S(2)}, u32[]{:S(2)}) collective-permute-start(bf16[64,3968]{1,0:T(8,128)(2,1)S(1)} %pad_maximum_fusion.refs_0_), channel_id=1, source_target_pairs={{0,8},{1,9},{2,10},{3,11},{4,12},{5,13},{6,14},{7,15},{8,0},{9,1},... | collective-permute-start | bytes 1523720 | tf_op jit(solution)/shard_map/ppermute | solution.py:579
  138.8 14.9 %collective-permute-start.18 = (bf16[64,3968]{1,0:T(8,128)(2,1)S(1)}, bf16[64,3968]{1,0:T(8,128)(2,1)S(1)}, u32[]{:S(2)}, u32[]{:S(2)}) collective-permute-start(bf16[64,3968]{1,0:T(8,128)(2,1)S(1)} %pad_maximum_fusion.refs_0_), channel_id=1, source_target_pairs={{0,16},{1,17},{2,18},{3,19},{4,20},{5,21},{6,22},{7,23},{8,24},{9,... | collective-permute-start | bytes 1523720 | tf_op jit(solution)/shard_map/ppermute | solution.py:579
  153.7 1.9 %collective-permute-start.20 = (bf16[64,3968]{1,0:T(8,128)(2,1)S(1)}, bf16[64,3968]{1,0:T(8,128)(2,1)S(1)}, u32[]{:S(2)}, u32[]{:S(2)}) collective-permute-start(bf16[64,3968]{1,0:T(8,128)(2,1)S(1)} %collective-permute-done.18.refs_1_), channel_id=1, source_target_pairs={{0,8},{1,9},{2,10},{3,11},{4,12},{5,13},{6,14},{7,15},{8,0},{9,1},... | collective-permute-start | bytes 1523720 | tf_op jit(solution)/shard_map/ppermute | solution.py:579
Sparse Core Ops, SparseCore 0:
  10.9 88.1 all-gather.2

commit v5 on v4

--- a/solution.py
+++ b/solution.py
@@ -423,6 +423,9 @@
 FF_STEP = 768
 
 
+FEED_IMAGES = 2
+
+
 def feed_kernel(normed_ref, middle_ref, up_ref, down_ref, *refs):
     out_ref, row_buf = refs[-2:]
     img = pl.program_id(0)
@@ -431,24 +434,28 @@
     for step in range(FF // FF_STEP):
         at = slice(step * FF_STEP, (step + 1) * FF_STEP)
         total = total + dot(gelu(dot(rows, up_ref[:, at])).astype(BF16), down_ref[at, :])
-    for at in range(IMGS_ROW):
+    for at in range(IMGS_ROW // FEED_IMAGES):
 
         @pl.when(img == at)
         def _():
-            row_buf[at * IMG : (at + 1) * IMG] = total[:IMG]
-            row_buf[TAIL_AT + at * TAIL : TAIL_AT + (at + 1) * TAIL] = total[IMG:]
-
-    @pl.when(img == IMGS_ROW - 1)
+            for within in range(FEED_IMAGES):
+                here = at * FEED_IMAGES + within
+                start = within * BLOCK
+                row_buf[here * IMG : (here + 1) * IMG] = total[start : start + IMG]
+                row_buf[TAIL_AT + here * TAIL : TAIL_AT + (here + 1) * TAIL] = total[start + IMG : start + BLOCK]
+
+    @pl.when(img == IMGS_ROW // FEED_IMAGES - 1)
     def _():
         out_ref[0] = row_buf[:ROW].astype(BF16)
 
 
 def feed(normed, middle, up_all, down_all, row, rows_n, chain):
-    spec = pl.BlockSpec((BLOCK, D), lambda i: (row * IMGS_ROW + i, 0))
+    steps = IMGS_ROW // FEED_IMAGES
+    spec = pl.BlockSpec((FEED_IMAGES * BLOCK, D), lambda i: (row * steps + i, 0))
     chained = [] if chain is None else [chain]
     return pl.pallas_call(
         feed_kernel,
-        grid=(IMGS_ROW,),
+        grid=(steps,),
         in_specs=[spec, spec]
         + [pl.BlockSpec(memory_space=pltpu.VMEM)] * 2
         + [pl.BlockSpec(memory_space=pltpu.HBM)] * len(chained),
@@ -456,7 +463,7 @@
         out_shape=pltpu.HBM((rows_n, ROW, D), BF16),
         input_output_aliases={} if chain is None else {4: 0},
         scratch_shapes=[pltpu.VMEM((ROW + SPARE, D), F32)],
-        compiler_params=params(18),
+        compiler_params=params(28),
         cost_estimate=cost(10, 20),
         name="feed",
     )(far(normed), far(middle), up_all, down_all, *chained)

time: 170 us -> 169 us (level)
  no operation moved by 1% of the time
where the time goes in v5:
time: 169 us
  Pallas kernels  90 us (53%)
  waiting for transfers between devices  35.4 us (21%)
  starting transfers between devices  20.1 us (12%)
  between operations  14.4 us (9%)
  local copies, waits for them, and re-layouts  7.25 us (4%)
    pallas_call x1, Pallas kernels, attend(): pl.pallas_call(functools.partial(attend_kernel, plan), grid=(rows_n, IMGS...  30.9 us
    ppermute x21, waiting for transfers between devices, exchange(): return lax.ppermute(value, ('dp', 'fsdp'), pairs)  27.7 us
    pallas_call x2, Pallas kernels, feed(): pl.pallas_call(feed_kernel, grid=(steps,), in_specs=[spec, spec] + [pl.Bl...  27.5 us
    ppermute x21, starting transfers between devices, exchange(): return lax.ppermute(value, ('dp', 'fsdp'), pairs)  20.1 us
    pallas_call x1, Pallas kernels, class_path(): pl.pallas_call(functools.partial(class_kernel, plans), in_specs=[near] *...  11.7 us
    pallas_call x1, Pallas kernels, token_grads(): pl.pallas_call(token_grads_kernel, grid=(rows_n,), in_specs=[row_spec, im...  7.86 us
    all_gather x1, waiting for transfers between devices, fetch_rest(): lax.all_gather(jnp.concatenate([up_part, down_part], axis=0), ('fsdp', 'd...  7.69 us
    pallas_call x1, Pallas kernels, sums(): pl.pallas_call(sums_kernel, grid=(1,), in_specs=[pl.BlockSpec(memory_spac...  6.93 us
  transfers between devices with their start and end apart: 22, of which 7 were waited for; matrix products, arithmetic and copies ran while one was open for 2% of the time, Pallas kernels for 42%

profile of v5, /device:TPU:0, one launch (start us, length us, event | category | flops | bytes accessed | tf_op | source)
XLA Modules:
  0.0 168.8 jit_solution(5783525142245034194)
XLA Ops:
  7.2 0.0 all-gather.3.cloned.1.call-start
  7.2 1.2 constant_dynamic-slice_fusion
  8.4 0.8 pad_maximum_fusion.2
  9.2 0.0 all-gather.3.cloned.1.call-update
  9.2 1.0 constant_dynamic-update-slice_fusion.1
  10.3 0.9 constant_dynamic-update-slice_fusion.refs_0_
  11.2 0.0 copy-start.5
  11.2 0.0 copy-start.10
  11.3 0.0 copy-start.11
  11.3 0.0 copy-start.12
  11.3 5.1 %collective-permute-start.2 = (bf16[48,1536]{1,0:T(8,128)(2,1)S(1)}, bf16[48,1536]{1,0:T(8,128)(2,1)S(1)}, u32[]{:S(2)}, u32[]{:S(2)}) collective-permute-start(bf16[48,1536]{1,0:T(8,128)(2,1)S(1)} %dynamic_slice.12), channel_id=1, source_target_pairs={{0,6},{1,7},{2,4},{3,5},{4,2},{5,3},{6,0},{7,1},{8,14},{9,15},{10,... | collective-permute-start | bytes 442376 | tf_op jit(solution)/shard_map/ppermute | solution.py:586
  16.4 0.6 collective-permute-start
  17.1 1.7 %collective-permute-start.3 = (bf16[96,1536]{1,0:T(8,128)(2,1)S(1)}, bf16[96,1536]{1,0:T(8,128)(2,1)S(1)}, u32[]{:S(2)}, u32[]{:S(2)}) collective-permute-start(bf16[96,1536]{1,0:T(8,128)(2,1)S(1)} %constant_dynamic-slice_fusion.2), channel_id=1, source_target_pairs={{0,1},{1,0},{2,3},{3,2},{4,5},{5,4},{6,7},{7,6},{8,9},{9,8},{10,11... | collective-permute-start | bytes 884744 | tf_op jit(solution)/shard_map/ppermute | solution.py:586
  18.8 0.0 copy-start.2
  18.8 1.1 copy-done.2
  19.9 4.7 %assemble.1 = (bf16[2,1024,768]{2,1,0:T(8,128)(2,1)}, bf16[2,1024,768]{2,1,0:T(8,128)(2,1)}) custom-call(s32[2,4]{1,0:T(2,128)S(1)} %bitcast.26, bf16[2,1024,768]{2,1,0:T(8,128)(2,1)S(1)} %bitcast.22, bf16[400,768]{1,0:T(8,128)(2,1)S(1)} %bitcast.24, f32[1,768]{1,0:T(1,128)S(1)} %reshape.56.gain_ref), custom_call_target="tpu_custom_call" | custom-call | flops 100000000 | bytes 10000000 | tf_op jit(solution)/shard_map/assemble/pallas_call | solution.py:137
  24.5 0.0 collective-permute-done.2
  24.5 8.8 %collective-permute-done.1 = bf16[48,1536]{1,0:T(8,128)(2,1)S(1)} collective-permute-done((bf16[48,1536]{1,0:T(8,128)(2,1)S(1)}, bf16[48,1536]{1,0:T(8,128)(2,1)S(1)}, u32[]{:S(2)}, u32[]{:S(2)}) %collective-permute-start.1) | collective-permute-done | bytes 147488 | tf_op jit(solution)/shard_map/ppermute | solution.py:586
  33.4 0.0 collective-permute-done
  33.4 0.0 copy-start.6
  33.4 1.9 %collective-permute-start.4 = (bf16[144,1536]{1,0:T(8,128)(2,1)S(1)}, bf16[144,1536]{1,0:T(8,128)(2,1)S(1)}, u32[]{:S(2)}, u32[]{:S(2)}) collective-permute-start(bf16[144,1536]{1,0:T(8,128)(2,1)S(1)} %pad_maximum_fusion.1.refs_2_), channel_id=1, source_target_pairs={{0,1},{1,0},{2,3},{3,2},{4,5},{5,4},{6,7},{7,6},{8,9},{9,8},{10,11... | collective-permute-start | bytes 1327112 | tf_op jit(solution)/shard_map/ppermute | solution.py:586
  35.4 1.7 %collective-permute-start.5 = (bf16[144,1536]{1,0:T(8,128)(2,1)S(1)}, bf16[144,1536]{1,0:T(8,128)(2,1)S(1)}, u32[]{:S(2)}, u32[]{:S(2)}) collective-permute-start(bf16[144,1536]{1,0:T(8,128)(2,1)S(1)} %pad_maximum_fusion.1.refs_2_), channel_id=1, source_target_pairs={{0,16},{1,17},{2,18},{3,19},{4,20},{5,21},{6,22},{7,23},{8,24},{9,... | collective-permute-start | bytes 1327112 | tf_op jit(solution)/shard_map/ppermute | solution.py:586
  37.1 0.0 collective-permute-done.3.refs_1_
  37.1 0.0 collective-permute-start.8
  37.1 6.8 %collective-permute-done.4.refs_3_ = bf16[144,1536]{1,0:T(8,128)(2,1)S(1)} collective-permute-done((bf16[144,1536]{1,0:T(8,128)(2,1)S(1)}, bf16[144,1536]{1,0:T(8,128)(2,1)S(1)}, u32[]{:S(2)}, u32[]{:S(2)}) %collective-permute-start.4) | collective-permute-done | bytes 442400 | tf_op jit(solution)/shard_map/ppermute | solution.py:586
  44.0 1.7 collective-permute-start.6
  45.7 4.5 %collective-permute-done.5.refs_4_ = bf16[144,1536]{1,0:T(8,128)(2,1)S(1)} collective-permute-done((bf16[144,1536]{1,0:T(8,128)(2,1)S(1)}, bf16[144,1536]{1,0:T(8,128)(2,1)S(1)}, u32[]{:S(2)}, u32[]{:S(2)}) %collective-permute-start.5) | collective-permute-done | bytes 442400 | tf_op jit(solution)/shard_map/ppermute | solution.py:586
  50.1 0.5 collective-permute-start.10
  50.7 0.0 collective-permute-done.8.refs_7_
  50.7 0.1 collective-permute-start.7
  50.8 3.1 %collective-permute-done.6.refs_5_ = bf16[80,1536]{1,0:T(8,128)(2,1)S(1)} collective-permute-done((bf16[80,1536]{1,0:T(8,128)(2,1)S(1)}, bf16[80,1536]{1,0:T(8,128)(2,1)S(1)}, u32[]{:S(2)}, u32[]{:S(2)}) %collective-permute-start.6) | collective-permute-done | bytes 245792 | tf_op jit(solution)/shard_map/ppermute | solution.py:586
  53.9 0.5 broadcast.7
  54.4 0.7 reduce.5
  55.1 2.6 %collective-permute-done.7.refs_6_ = bf16[64,1536]{1,0:T(8,128)(2,1)} collective-permute-done((bf16[64,1536]{1,0:T(8,128)(2,1)S(1)}, bf16[64,1536]{1,0:T(8,128)(2,1)}, u32[]{:S(2)}, u32[]{:S(2)}) %collective-permute-start.7) | collective-permute-done | bytes 196640 | tf_op jit(solution)/shard_map/ppermute | solution.py:586
  57.7 0.0 collective-permute-start.13
  57.7 0.1 convert_element_type.8
  57.8 0.1 reshape_reshape.4.ids_ref
  57.9 0.1 broadcast_in_dim.2
  57.9 0.1 pad_maximum_fusion.4.grads_ref
  58.0 1.3 copy-done.1
  59.3 0.4 loss_grads.1.d_final_ref
  59.7 0.0 collective-permute-done.9.refs_8_
  59.7 0.0 collective-permute-done.13.refs_12_
  59.7 0.0 collective-permute-done.11.refs_10_
  59.7 0.0 collective-permute-done.12.refs_11_
  59.8 0.7 copy-done.13
  60.5 0.2 copy-done.14
  60.6 30.9 %attend.1 = (bf16[8,16,768]{2,1,0:T(8,128)(2,1)S(1)}, f32[8,16,256]{2,1,0:T(8,128)S(1)}, f32[8,8,768]{2,1,0:T(8,128)S(1)}, bf16[8,256,1536]{2,1,0:T(8,128)(2,1)}...) custom-call(bf16[2,1024,768]{2,1,0:T(8,128)(2,1)} %get-tuple-element.33.normed_ref, ...), custom_call_target="tpu_custom_call" | custom-call | flops 16000000000 | bytes 30000000 | tf_op jit(solution)/shard_map/attend/pallas_call | solution.py:242
  91.5 7.7 %all-gather.3.cloned.1.call-done = bf16[6144,768]{1,0:T(8,128)(2,1)} async-done(((bf16[192,768]{1,0:T(8,128)(2,1)}), bf16[6144,768]{1,0:T(8,128)(2,1)}) %all-gather.3.cloned.1.call-update) | async-done | bytes 9437200 | tf_op jit(solution)/shard_map/all_gather | solution.py:662
  99.2 11.7 %class_path.1 = (bf16[8,3968]{1,0:T(8,128)(2,1)S(1)}, bf16[8,32,256]{2,1,0:T(8,128)(2,1)S(1)}, bf16[8,32,768]{2,1,0:T(8,128)(2,1)S(1)}, f32[16,768]{1,0:T(8,128)...) custom-call(f32[8,768]{1,0:T(8,128)S(1)} %loss_grads.1.d_final_ref, ...), custom_call_target="tpu_custom_call" | custom-call | flops 8000000000 | bytes 30000000 | tf_op jit(solution)/shard_map/class_path/pallas_call | solution.py:403
  110.9 2.0 %collective-permute-start.16 = (bf16[8,3968]{1,0:T(8,128)(2,1)S(1)}, bf16[8,3968]{1,0:T(8,128)(2,1)S(1)}, u32[]{:S(2)}, u32[]{:S(2)}) collective-permute-start(bf16[8,3968]{1,0:T(8,128)(2,1)S(1)} %get-tuple-element.41), channel_id=1, source_target_pairs={{0,6},{1,7},{2,4},{3,5},{4,2},{5,3},{6,0},{7,1},{8,14},{9,15},{10,... | collective-permute-start | bytes 190472 | tf_op jit(solution)/shard_map/ppermute | solution.py:586
  112.9 0.9 collective-permute-start.15
  113.9 1.5 collective-permute-start.14
  115.4 7.9 %token_grads.1 = f32[2,1024,768]{2,1,0:T(8,128)} custom-call(bf16[2,1024,768]{2,1,0:T(8,128)(2,1)} %get-tuple-element.34.resid_ref, bf16[8,32,256]{2,1,0:T(8,128)(2,1)S(1)} %get-tuple-element.42.weights_ref, bf16[8,32,768]{2,1,0:T(8,128)(2,1)S(1)} %get-tuple-element.43.routes_ref, f32[16,768]{1,0:T(8,128)S(1)} %get-tuple-element.44.d_class_ref, ...), custom_call_target="tpu_custom_call" | custom-call | flops 500000000 | bytes 20000000 | tf_op jit(solution)/shard_map/token_grads/pallas_call | solution.py:495
  123.3 1.5 collective-permute-start.17
  124.8 13.6 %feed.2.refs_0_ = bf16[2,1024,768]{2,1,0:T(8,128)(2,1)} custom-call(bf16[2048,768]{1,0:T(8,128)(2,1)} %get-tuple-element.48.normed_ref, f32[2048,768]{1,0:T(8,128)} %get-tuple-element.49.middle_ref, bf16[768,3072]{1,0:T(8,128)(2,1)S(1)} %get-tuple-element.50.up_ref, bf16[3072,768]{1,0:T(8,128)(2,1)S(1)} %get-tuple-element.51.down_ref), custom_call_target="tpu_custom_call" | custom-call | flops 10000000000 | bytes 20000000 | tf_op jit(solution)/shard_map/feed/pallas_call | solution.py:456
  138.4 0.0 copy-start.3
  138.4 0.0 slice-start.1
  138.4 0.1 collective-permute-start.19
  138.5 0.7 collective-permute-start.18
  139.2 14.0 %feed.3 = bf16[2,1024,768]{2,1,0:T(8,128)(2,1)} custom-call(bf16[2048,768]{1,0:T(8,128)(2,1)} %get-tuple-element.48.normed_ref, f32[2048,768]{1,0:T(8,128)} %get-tuple-element.49.middle_ref, bf16[768,3072]{1,0:T(8,128)(2,1)S(1)} %get-tuple-element.50.up_ref, bf16[3072,768]{1,0:T(8,128)(2,1)S(1)} %get-tuple-element.51.down_ref, ...), custom_call_target="tpu_custom_call", output_to_operand_aliasing={{}: (4, {})} | custom-call | flops 10000000000 | bytes 20000000 | tf_op jit(solution)/shard_map/feed/pallas_call | solution.py:456
  153.1 0.0 collective-permute-done.18.refs_1_
  153.1 1.9 %collective-permute-done.20.refs_3_ = bf16[64,3968]{1,0:T(8,128)(2,1)S(1)} collective-permute-done((bf16[64,3968]{1,0:T(8,128)(2,1)S(1)}, bf16[64,3968]{1,0:T(8,128)(2,1)S(1)}, u32[]{:S(2)}, u32[]{:S(2)}) %collective-permute-start.20) | collective-permute-done | bytes 507936 | tf_op jit(solution)/shard_map/ppermute | solution.py:586
  155.0 6.9 %sums.1 = (f32[400,768]{1,0:T(8,128)}, f32[800,768]{1,0:T(8,128)}) custom-call(bf16[768,3072]{1,0:T(8,128)(2,1)S(1)} %bitcast.28, bf16[400,768]{1,0:T(8,128)(2,1)S(1)} %bitcast.25, f32[1,768]{1,0:T(1,128)S(1)} %reshape.56.gain_ref, bf16[64,3968]{1,0:T(8,128)(2,1)S(1)} %pad_maximum_fusion.refs_0_, bf16[64,3968]{1,0:T(8,128)(2,1)S(1)} %collective-permute-done.18.refs_1_, ...), custom_call_target="tpu_custom_call" | custom-call | flops 5000000000 | bytes 15000000 | tf_op jit(solution)/shard_map/sums/pallas_call | solution.py:547
  (51 shorter events, 0.3 us)
Async XLA Ops:
  7.2 11.6 %copy-start.9 = (f32[768]{0:T(1024)S(1)}, f32[768]{0:T(1024)}, u32[]{:S(2)}) copy-start(f32[768]{0:T(1024)} %param.21) | copy-start | bytes 9220
  7.2 11.6 %copy-start.4 = (s32[2,1,4]{2,1,0:T(1,128)S(1)}, s32[2,1,4]{2,1,0:T(1,128)}, u32[]{:S(2)}) copy-start(s32[2,1,4]{2,1,0:T(1,128)} %param.13) | copy-start | bytes 100
  7.2 11.6 %copy-start = (bf16[2,1,1024,768]{3,2,1,0:T(8,128)(2,1)S(1)}, bf16[2,1,1024,768]{3,2,1,0:T(8,128)(2,1)}, u32[]{:S(2)}) copy-start(bf16[2,1,1024,768]{3,2,1,0:T(8,128)(2,1)} %param.12) | copy-start | bytes 9437188
  7.2 92.0 %all-gather.3.cloned.1.call-start = ((), (), s32[]{:S(2)}) async-start(), calls=%async_computation | async-start | bytes 9732096 | tf_op jit(solution)/shard_map/all_gather | solution.py:662
  11.2 7.6 %copy-start.5 = (bf16[96,3072]{1,0:T(8,128)(2,1)}, bf16[96,3072]{1,0:T(8,128)(2,1)S(1)}, u32[]{:S(2)}) copy-start(bf16[96,3072]{1,0:T(8,128)(2,1)S(1)} %constant_dynamic-update-slice_fusion.refs_0_) | copy-start | bytes 1769476
  11.2 46.5 %copy-start.10 = (f32[768]{0:T(1024)S(1)}, f32[768]{0:T(1024)}, u32[]{:S(2)}) copy-start(f32[768]{0:T(1024)} %param.22) | copy-start | bytes 9220
  11.3 46.6 %copy-start.11 = (f32[768]{0:T(1024)S(1)}, f32[768]{0:T(1024)}, u32[]{:S(2)}) copy-start(f32[768]{0:T(1024)} %param.23) | copy-start | bytes 9220
  11.3 46.7 %copy-start.12 = (bf16[2,1,4,100]{3,2,1,0:T(4,128)(2,1)S(1)}, bf16[2,1,4,100]{3,2,1,0:T(4,128)(2,1)}, u32[]{:S(2)}) copy-start(bf16[2,1,4,100]{3,2,1,0:T(4,128)(2,1)} %param.14) | copy-start | bytes 4804
  11.3 13.3 %collective-permute-start.2 = (bf16[48,1536]{1,0:T(8,128)(2,1)S(1)}, bf16[48,1536]{1,0:T(8,128)(2,1)S(1)}, u32[]{:S(2)}, u32[]{:S(2)}) collective-permute-start(bf16[48,1536]{1,0:T(8,128)(2,1)S(1)} %dynamic_slice.12), channel_id=1, source_target_pairs={{0,6},{1,7},{2,4},{3,5},{4,2},{5,3},{6,0},{7,1},{8,14},{9,15},{10,... | collective-permute-start | bytes 442376 | tf_op jit(solution)/shard_map/ppermute | solution.py:586
  16.4 17.0 %collective-permute-start.1 = (bf16[48,1536]{1,0:T(8,128)(2,1)S(1)}, bf16[48,1536]{1,0:T(8,128)(2,1)S(1)}, u32[]{:S(2)}, u32[]{:S(2)}) collective-permute-start(bf16[48,1536]{1,0:T(8,128)(2,1)S(1)} %dynamic_slice.12), channel_id=1, source_target_pairs={{0,4},{1,5},{2,6},{3,7},{4,0},{5,1},{6,2},{7,3},{8,12},{9,13},{10,... | collective-permute-start | bytes 442376 | tf_op jit(solution)/shard_map/ppermute | solution.py:586
  16.4 17.0 %collective-permute-start = (bf16[48,1536]{1,0:T(8,128)(2,1)S(1)}, bf16[48,1536]{1,0:T(8,128)(2,1)S(1)}, u32[]{:S(2)}, u32[]{:S(2)}) collective-permute-start(bf16[48,1536]{1,0:T(8,128)(2,1)S(1)} %dynamic_slice.12), channel_id=1, source_target_pairs={{0,2},{1,3},{2,0},{3,1},{4,6},{5,7},{6,4},{7,5},{8,10},{9,11},{10,... | collective-permute-start | bytes 442376 | tf_op jit(solution)/shard_map/ppermute | solution.py:586
  17.1 20.0 %collective-permute-start.3 = (bf16[96,1536]{1,0:T(8,128)(2,1)S(1)}, bf16[96,1536]{1,0:T(8,128)(2,1)S(1)}, u32[]{:S(2)}, u32[]{:S(2)}) collective-permute-start(bf16[96,1536]{1,0:T(8,128)(2,1)S(1)} %constant_dynamic-slice_fusion.2), channel_id=1, source_target_pairs={{0,1},{1,0},{2,3},{3,2},{4,5},{5,4},{6,7},{7,6},{8,9},{9,8},{10,11... | collective-permute-start | bytes 884744 | tf_op jit(solution)/shard_map/ppermute | solution.py:586
  18.8 1.1 copy-start.2
  33.4 26.4 %copy-start.6 = (bf16[144,1536]{1,0:T(8,128)(2,1)}, bf16[144,1536]{1,0:T(8,128)(2,1)S(1)}, u32[]{:S(2)}) copy-start(bf16[144,1536]{1,0:T(8,128)(2,1)S(1)} %pad_maximum_fusion.1.refs_2_) | copy-start | bytes 1327108
  33.4 10.5 %collective-permute-start.4 = (bf16[144,1536]{1,0:T(8,128)(2,1)S(1)}, bf16[144,1536]{1,0:T(8,128)(2,1)S(1)}, u32[]{:S(2)}, u32[]{:S(2)}) collective-permute-start(bf16[144,1536]{1,0:T(8,128)(2,1)S(1)} %pad_maximum_fusion.1.refs_2_), channel_id=1, source_target_pairs={{0,1},{1,0},{2,3},{3,2},{4,5},{5,4},{6,7},{7,6},{8,9},{9,8},{10,11... | collective-permute-start | bytes 1327112 | tf_op jit(solution)/shard_map/ppermute | solution.py:586
  35.4 14.8 %collective-permute-start.5 = (bf16[144,1536]{1,0:T(8,128)(2,1)S(1)}, bf16[144,1536]{1,0:T(8,128)(2,1)S(1)}, u32[]{:S(2)}, u32[]{:S(2)}) collective-permute-start(bf16[144,1536]{1,0:T(8,128)(2,1)S(1)} %pad_maximum_fusion.1.refs_2_), channel_id=1, source_target_pairs={{0,16},{1,17},{2,18},{3,19},{4,20},{5,21},{6,22},{7,23},{8,24},{9,... | collective-permute-start | bytes 1327112 | tf_op jit(solution)/shard_map/ppermute | solution.py:586
  37.1 22.7 %copy-start.15 = (bf16[96,1536]{1,0:T(8,128)(2,1)}, bf16[96,1536]{1,0:T(8,128)(2,1)S(1)}, u32[]{:S(2)}) copy-start(bf16[96,1536]{1,0:T(8,128)(2,1)S(1)} %collective-permute-done.3.refs_1_) | copy-start | bytes 884740
  37.1 13.6 %collective-permute-start.8 = (bf16[96,1536]{1,0:T(8,128)(2,1)S(1)}, bf16[96,1536]{1,0:T(8,128)(2,1)S(1)}, u32[]{:S(2)}, u32[]{:S(2)}) collective-permute-start(bf16[96,1536]{1,0:T(8,128)(2,1)S(1)} %collective-permute-done.3.refs_1_), channel_id=1, source_target_pairs={{0,8},{1,9},{2,10},{3,11},{4,12},{5,13},{6,14},{7,15},{8,0},{9,1},... | collective-permute-start | bytes 884744 | tf_op jit(solution)/shard_map/ppermute | solution.py:586
  44.0 15.8 %copy-start.7 = (bf16[144,1536]{1,0:T(8,128)(2,1)}, bf16[144,1536]{1,0:T(8,128)(2,1)S(1)}, u32[]{:S(2)}) copy-start(bf16[144,1536]{1,0:T(8,128)(2,1)S(1)} %collective-permute-done.4.refs_3_) | copy-start | bytes 1327108
  44.0 9.9 %collective-permute-start.6 = (bf16[80,1536]{1,0:T(8,128)(2,1)S(1)}, bf16[80,1536]{1,0:T(8,128)(2,1)S(1)}, u32[]{:S(2)}, u32[]{:S(2)}) collective-permute-start(bf16[80,1536]{1,0:T(8,128)(2,1)S(1)} %slice.8), channel_id=1, source_target_pairs={{0,16},{1,17},{2,18},{3,19},{4,20},{5,21},{6,22},{7,23},{8,24},{9,... | collective-permute-start | bytes 737288 | tf_op jit(solution)/shard_map/ppermute | solution.py:586
  45.7 14.0 %collective-permute-start.9 = (bf16[144,1536]{1,0:T(8,128)(2,1)S(1)}, bf16[144,1536]{1,0:T(8,128)(2,1)S(1)}, u32[]{:S(2)}, u32[]{:S(2)}) collective-permute-start(bf16[144,1536]{1,0:T(8,128)(2,1)S(1)} %pad_maximum_fusion.1.refs_2_), channel_id=1, source_target_pairs={{0,8},{1,9},{2,10},{3,11},{4,12},{5,13},{6,14},{7,15},{8,0},{9,1},... | collective-permute-start | bytes 1327112 | tf_op jit(solution)/shard_map/ppermute | solution.py:586
  50.1 9.7 %copy-start.8 = (bf16[144,1536]{1,0:T(8,128)(2,1)}, bf16[144,1536]{1,0:T(8,128)(2,1)S(1)}, u32[]{:S(2)}) copy-start(bf16[144,1536]{1,0:T(8,128)(2,1)S(1)} %collective-permute-done.5.refs_4_) | copy-start | bytes 1327108
  50.1 9.6 %collective-permute-start.11 = (bf16[144,1536]{1,0:T(8,128)(2,1)S(1)}, bf16[144,1536]{1,0:T(8,128)(2,1)S(1)}, u32[]{:S(2)}, u32[]{:S(2)}) collective-permute-start(bf16[144,1536]{1,0:T(8,128)(2,1)S(1)} %collective-permute-done.5.refs_4_), channel_id=1, source_target_pairs={{0,8},{1,9},{2,10},{3,11},{4,12},{5,13},{6,14},{7,15},{8,0},{9,1},... | collective-permute-start | bytes 1327112 | tf_op jit(solution)/shard_map/ppermute | solution.py:586
  50.1 9.6 %collective-permute-start.10 = (bf16[144,1536]{1,0:T(8,128)(2,1)S(1)}, bf16[144,1536]{1,0:T(8,128)(2,1)}, u32[]{:S(2)}, u32[]{:S(2)}) collective-permute-start(bf16[144,1536]{1,0:T(8,128)(2,1)S(1)} %collective-permute-done.4.refs_3_), channel_id=1, source_target_pairs={{0,8},{1,9},{2,10},{3,11},{4,12},{5,13},{6,14},{7,15},{8,0},{9,1},... | collective-permute-start | bytes 1327112 | tf_op jit(solution)/shard_map/ppermute | solution.py:586
  50.7 9.1 %copy-start.16 = (bf16[96,1536]{1,0:T(8,128)(2,1)}, bf16[96,1536]{1,0:T(8,128)(2,1)S(1)}, u32[]{:S(2)}) copy-start(bf16[96,1536]{1,0:T(8,128)(2,1)S(1)} %collective-permute-done.8.refs_7_) | copy-start | bytes 884740
  50.7 7.0 %collective-permute-start.7 = (bf16[64,1536]{1,0:T(8,128)(2,1)S(1)}, bf16[64,1536]{1,0:T(8,128)(2,1)}, u32[]{:S(2)}, u32[]{:S(2)}) collective-permute-start(bf16[64,1536]{1,0:T(8,128)(2,1)S(1)} %slice.9), channel_id=1, source_target_pairs={{0,1},{1,0},{2,3},{3,2},{4,5},{5,4},{6,7},{7,6},{8,9},{9,8},{10,11... | collective-permute-start | bytes 589832 | tf_op jit(solution)/shard_map/ppermute | solution.py:586
  53.9 5.9 %copy-start.17 = (bf16[80,1536]{1,0:T(8,128)(2,1)}, bf16[80,1536]{1,0:T(8,128)(2,1)S(1)}, u32[]{:S(2)}) copy-start(bf16[80,1536]{1,0:T(8,128)(2,1)S(1)} %collective-permute-done.6.refs_5_) | copy-start | bytes 737284
  53.9 5.8 %collective-permute-start.12 = (bf16[80,1536]{1,0:T(8,128)(2,1)S(1)}, bf16[80,1536]{1,0:T(8,128)(2,1)}, u32[]{:S(2)}, u32[]{:S(2)}) collective-permute-start(bf16[80,1536]{1,0:T(8,128)(2,1)S(1)} %collective-permute-done.6.refs_5_), channel_id=1, source_target_pairs={{0,8},{1,9},{2,10},{3,11},{4,12},{5,13},{6,14},{7,15},{8,0},{9,1},... | collective-permute-start | bytes 737288 | tf_op jit(solution)/shard_map/ppermute | solution.py:586
  57.7 2.0 %collective-permute-start.13 = (bf16[64,1536]{1,0:T(8,128)(2,1)}, bf16[64,1536]{1,0:T(8,128)(2,1)}, u32[]{:S(2)}, u32[]{:S(2)}) collective-permute-start(bf16[64,1536]{1,0:T(8,128)(2,1)} %collective-permute-done.7.refs_6_), channel_id=1, source_target_pairs={{0,8},{1,9},{2,10},{3,11},{4,12},{5,13},{6,14},{7,15},{8,0},{9,1},... | collective-permute-start | bytes 589832 | tf_op jit(solution)/shard_map/ppermute | solution.py:586
  58.0 1.3 copy-start.1
  59.7 0.8 copy-start.13
  59.7 0.9 copy-start.14
  110.9 12.3 %collective-permute-start.16 = (bf16[8,3968]{1,0:T(8,128)(2,1)S(1)}, bf16[8,3968]{1,0:T(8,128)(2,1)S(1)}, u32[]{:S(2)}, u32[]{:S(2)}) collective-permute-start(bf16[8,3968]{1,0:T(8,128)(2,1)S(1)} %get-tuple-element.41), channel_id=1, source_target_pairs={{0,6},{1,7},{2,4},{3,5},{4,2},{5,3},{6,0},{7,1},{8,14},{9,15},{10,... | collective-permute-start | bytes 190472 | tf_op jit(solution)/shard_map/ppermute | solution.py:586
  112.9 10.3 %collective-permute-start.15 = (bf16[8,3968]{1,0:T(8,128)(2,1)S(1)}, bf16[8,3968]{1,0:T(8,128)(2,1)S(1)}, u32[]{:S(2)}, u32[]{:S(2)}) collective-permute-start(bf16[8,3968]{1,0:T(8,128)(2,1)S(1)} %get-tuple-element.41), channel_id=1, source_target_pairs={{0,4},{1,5},{2,6},{3,7},{4,0},{5,1},{6,2},{7,3},{8,12},{9,13},{10,... | collective-permute-start | bytes 190472 | tf_op jit(solution)/shard_map/ppermute | solution.py:586
  113.9 9.4 %collective-permute-start.14 = (bf16[8,3968]{1,0:T(8,128)(2,1)S(1)}, bf16[8,3968]{1,0:T(8,128)(2,1)S(1)}, u32[]{:S(2)}, u32[]{:S(2)}) collective-permute-start(bf16[8,3968]{1,0:T(8,128)(2,1)S(1)} %get-tuple-element.41), channel_id=1, source_target_pairs={{0,2},{1,3},{2,0},{3,1},{4,6},{5,7},{6,4},{7,5},{8,10},{9,11},{10,... | collective-permute-start | bytes 190472 | tf_op jit(solution)/shard_map/ppermute | solution.py:586
  123.3 15.0 %collective-permute-start.17 = (bf16[32,3968]{1,0:T(8,128)(2,1)S(1)}, bf16[32,3968]{1,0:T(8,128)(2,1)S(1)}, u32[]{:S(2)}, u32[]{:S(2)}) collective-permute-start(bf16[32,3968]{1,0:T(8,128)(2,1)S(1)} %pad_maximum_fusion.3), channel_id=1, source_target_pairs={{0,1},{1,0},{2,3},{3,2},{4,5},{5,4},{6,7},{7,6},{8,9},{9,8},{10,11... | collective-permute-start | bytes 761864 | tf_op jit(solution)/shard_map/ppermute | solution.py:586
  138.3 16.7 %slice-start = ((s8[4718592]{0:T(1024)(128)(4,1)}), s8[4194304]{0:T(1024)(128)(4,1)S(1)}, s32[]{:S(2)}) async-start(s8[4718592]{0:T(1024)(128)(4,1)} %bitcast.27), calls=%async_computation.1 | async-start | bytes 8388608
  138.4 16.6 %copy-start.3 = (bf16[8,50,768]{2,0,1:T(8,128)(2,1)S(1)}, bf16[8,50,768]{2,0,1:T(8,128)(2,1)}, u32[]{:S(2)}) copy-start(bf16[8,50,768]{2,0,1:T(8,128)(2,1)} %param.15) | copy-start | bytes 1843204
  138.4 16.6 %slice-start.1 = ((s8[4718592]{0:T(1024)(128)(4,1)}), s8[524288]{0:T(1024)(128)(4,1)S(1)}, s32[]{:S(2)}) async-start(s8[4718592]{0:T(1024)(128)(4,1)} %bitcast.27), calls=%async_computation.2 | async-start | bytes 1048576
  138.4 14.7 %collective-permute-start.19 = (bf16[64,3968]{1,0:T(8,128)(2,1)S(1)}, bf16[64,3968]{1,0:T(8,128)(2,1)S(1)}, u32[]{:S(2)}, u32[]{:S(2)}) collective-permute-start(bf16[64,3968]{1,0:T(8,128)(2,1)S(1)} %pad_maximum_fusion.refs_0_), channel_id=1, source_target_pairs={{0,8},{1,9},{2,10},{3,11},{4,12},{5,13},{6,14},{7,15},{8,0},{9,1},... | collective-permute-start | bytes 1523720 | tf_op jit(solution)/shard_map/ppermute | solution.py:586
  138.5 14.6 %collective-permute-start.18 = (bf16[64,3968]{1,0:T(8,128)(2,1)S(1)}, bf16[64,3968]{1,0:T(8,128)(2,1)S(1)}, u32[]{:S(2)}, u32[]{:S(2)}) collective-permute-start(bf16[64,3968]{1,0:T(8,128)(2,1)S(1)} %pad_maximum_fusion.refs_0_), channel_id=1, source_target_pairs={{0,16},{1,17},{2,18},{3,19},{4,20},{5,21},{6,22},{7,23},{8,24},{9,... | collective-permute-start | bytes 1523720 | tf_op jit(solution)/shard_map/ppermute | solution.py:586
  153.1 1.9 %collective-permute-start.20 = (bf16[64,3968]{1,0:T(8,128)(2,1)S(1)}, bf16[64,3968]{1,0:T(8,128)(2,1)S(1)}, u32[]{:S(2)}, u32[]{:S(2)}) collective-permute-start(bf16[64,3968]{1,0:T(8,128)(2,1)S(1)} %collective-permute-done.18.refs_1_), channel_id=1, source_target_pairs={{0,8},{1,9},{2,10},{3,11},{4,12},{5,13},{6,14},{7,15},{8,0},{9,1},... | collective-permute-start | bytes 1523720 | tf_op jit(solution)/shard_map/ppermute | solution.py:586
Sparse Core Ops, SparseCore 0:
  10.9 88.1 all-gather.2
